TPU v7x, 32 devices: a whole 2x2x4 slice. The times are simulated.
32 devices in a mesh: row: 4 (over x, core), col: 8 (over z, y).
Axes of the slice: x: 2, y: 2, z: 4, core: 2. Of those that a mesh axis runs over, the one named last changes fastest.
Arguments:
- vectors: bfloat16 [1, 16, 4096], P(None, None, ('col', 'row')), may hold values from -110 to 110
- h_tiles: bfloat16 [1, 4, 256, 128, 128], P(None, 'row', 'col'), may hold values from -0.15625 to 0.15625
- h_list: int32 [1, 4, 256], P(None, 'row', 'col'), may hold values from -1 to 31, as said below
- j_tiles: bfloat16 [1, 4, 96, 128, 128], P(None, 'row', 'col'), may hold values from -0.25 to 0.25
- j_list: int32 [1, 4, 96], P(None, 'row', 'col'), may hold values from -1 to 63, as said below
Outputs:
- basis: float32 [1, 16, 4096], P(None, None, ('row', 'col'))
- transitions: float32 [1, 2, 16, 16], replicated
Inputs may be any that keep to these rules, and one draw needn't show every extreme that they name: `h_list`: each block's 32 entries list distinct tile positions first and then -1; at most 32 positions a block, and some block lists all 32. `j_list`: each block's 12 entries list distinct codes first and then -1; at most 12 codes a block, and some block lists all 12.
All inputs are finite; a program needn't handle non-finite values.
Results may differ from a plain program's by a relative error of at most 0.0003.
Values may be sent and summed in bfloat16 or wider, within the bound.
No kernel may reach another device: no remote copies, remote signals or barrier semaphores. Data moves between devices by JAX's collectives and lax.ppermute only.
A program may use at most 64 MiB of HBM per device.

v0:
```python
import math

import jax
import jax.numpy as jnp
from jax import lax
from jax.sharding import PartitionSpec as P

NSIT = 6


exact_precision = lax.Precision.HIGHEST


def local_product(tile_data, code_data, vector_block, operator_count, row_tiles):
    sector_count = tile_data.shape[0]
    tile_size = tile_data.shape[2]
    vector_count = vector_block.shape[1]
    column_tiles = vector_block.shape[2] // tile_size
    position_count = row_tiles * column_tiles
    column_vectors = vector_block.reshape(sector_count, vector_count, column_tiles, tile_size)
    places = code_data % position_count
    operator = code_data // position_count
    column_hot = (
        places[:, :, None] % column_tiles == jnp.arange(column_tiles)[None, None, :]
    ).astype(jnp.bfloat16)
    picked = jnp.einsum(
        "sqc,skcb->sqkb", column_hot, column_vectors, preferred_element_type=jnp.float32
    ).astype(jnp.bfloat16)
    product = jnp.einsum("sqab,sqkb->sqka", tile_data, picked, preferred_element_type=jnp.float32)
    row_hot = (
        (operator[:, :, None, None] == jnp.arange(operator_count)[None, None, :, None])
        & (places[:, :, None, None] // column_tiles == jnp.arange(row_tiles)[None, None, None, :])
        & (code_data[:, :, None, None] >= 0)
    ).astype(jnp.float32)
    result = jnp.einsum("sqor,sqka->sokra", row_hot, product, precision=exact_precision)
    return result.reshape(sector_count, operator_count * vector_count, row_tiles * tile_size)


def inverse_root_of(gram, vector_count):
    scale = jnp.sqrt(jnp.sum(gram * gram, axis=(1, 2), keepdims=True) + 1e-06)
    iterate = gram / scale
    identity = jnp.eye(vector_count, dtype=jnp.float32)[None]
    inverse_root = identity
    for iteration in range(NSIT):
        middle = 1.5 * identity - 0.5 * jnp.einsum(
            "skm,sml->skl", inverse_root, iterate, precision=exact_precision
        )
        iterate = jnp.einsum("skm,sml->skl", iterate, middle, precision=exact_precision)
        inverse_root = jnp.einsum("skm,sml->skl", middle, inverse_root, precision=exact_precision)
    return (inverse_root, scale)


def per_device(vectors, h_tiles, h_list, j_tiles, j_list):
    sector_count = vectors.shape[0]
    vector_count = vectors.shape[1]
    tile_size = h_tiles.shape[-1]
    block_rows = vectors.shape[2] * lax.axis_size("col")
    total_rows = block_rows * lax.axis_size("row")
    row_tiles = block_rows // tile_size
    vector_block = lax.all_gather(vectors, "row", axis=2, tiled=True)
    h_part = local_product(
        h_tiles.reshape(sector_count, -1, tile_size, tile_size),
        h_list.reshape(sector_count, -1),
        vector_block,
        1,
        row_tiles,
    )
    j_part = local_product(
        j_tiles.reshape(sector_count, -1, tile_size, tile_size),
        j_list.reshape(sector_count, -1),
        vector_block,
        2,
        row_tiles,
    )
    projected, applied = (
        lax.psum_scatter(h_part, "col", scatter_dimension=2, tiled=True),
        lax.psum_scatter(j_part, "col", scatter_dimension=2, tiled=True),
    )
    gram_part = jnp.einsum("skp,slp->skl", projected, projected, precision=exact_precision)
    gram = lax.psum(gram_part, ("row", "col"))
    inverse_root, scale = inverse_root_of(gram, vector_count)
    basis = jnp.sqrt(total_rows / scale) * jnp.einsum(
        "smk,smp->skp", inverse_root, projected, precision=exact_precision
    )
    element_part = jnp.einsum("skp,smp->skm", basis, applied, precision=exact_precision)
    elements = lax.psum(element_part, ("row", "col")) / math.sqrt(total_rows)
    elements = elements.reshape(sector_count, vector_count, 2, vector_count).transpose(0, 2, 1, 3)
    return (basis, elements)


def solution(mesh):
    return jax.shard_map(
        per_device,
        mesh=mesh,
        in_specs=(
            P(None, None, ("col", "row")),
            P(None, "row", "col", None, None),
            P(None, "row", "col"),
            P(None, "row", "col", None, None),
            P(None, "row", "col"),
        ),
        out_specs=(P(None, None, ("row", "col")), P()),
        check_vma=False,
    )
```

profile of v0, /device:TPU:0, one launch (start us, length us, event | category | flops | bytes accessed | tf_op | source)
XLA Modules:
  0.0 189.2 jit_solution(17668249501114527060)
XLA Ops:
  7.2 0.7 fusion.38
  8.0 6.4 %all_gather.3 = bf16[1,16,512]{2,1,0:T(8,128)(2,1)S(1)} all-gather(bf16[1,16,128]{2,1,0:T(8,128)(2,1)} %param.5), channel_id=1, replica_groups=mesh['row'=4,'col'=8] {'row'}, dimensions={2}, use_global_device_ids=true | all-gather | bytes 20480 | tf_op jit(solution)/shard_map/all_gather | solution.py:60
  14.4 0.2 convolution_convert_fusion
  14.7 0.6 fusion.6
  15.3 0.3 convolution_bitcast_fusion.2
  15.6 0.6 reshape.796
  16.3 0.7 bitcast_compare_fusion
  17.0 0.7 and_select_fusion.1
  17.7 0.2 convolution_convert_fusion.1
  17.9 1.3 convolution_bitcast_fusion.1
  19.2 0.3 convolution_bitcast_fusion
  19.5 13.7 %copy.19 = f32[1,32,1024]{0,1,2:T(8,128)} copy(f32[1,32,1024]{2,0,1:T(1,128)S(1)} %bitcast.122) | data formatting | bytes 262144
  33.2 9.0 %bitcast_reduce_fusion = f32[1024,32]{1,0:T(8,128)} fusion(f32[1,32,1024]{0,1,2:T(8,128)} %copy.19), kind=kLoop, calls=%fused_computation | loop fusion | bytes 262144
  42.2 30.7 %reduce-scatter.5.cloned.1.call-done = f32[1,16,128]{2,1,0:T(8,128)} async-done(((f32[1,16,1024]{2,1,0:T(8,128)}), f32[1,16,128]{2,1,0:T(8,128)}) %reduce-scatter.5.cloned.1.call-update) | async-done | bytes 8208 | tf_op jit(solution)/shard_map/reduce_scatter | solution.py:76
  72.9 0.9 convolution_bitcast_fusion.4
  73.8 40.3 %psum.14 = f32[1,16,16]{2,1,0:T(8,128)S(1)} all-reduce(f32[1,16,16]{2,1,0:T(8,128)S(1)} %convolution_bitcast_fusion.4), channel_id=1, replica_groups=mesh['row'=4,'col'=8] {'row','col'}, use_global_device_ids=true, to_apply=%region_1.2 | all-reduce | flops 256 | bytes 2048 | tf_op jit(solution)/shard_map/psum | solution.py:80
  114.2 0.6 multiply_reduce_fusion
  115.6 0.1 fusion.13
  117.9 0.9 convolution_multiply_fusion
  118.8 19.9 %reduce-scatter.7.cloned.1.call-done = f32[128,32]{1,0:T(8,128)} async-done(((f32[1024,32]{1,0:T(8,128)}), f32[128,32]{1,0:T(8,128)}) %reduce-scatter.7.cloned.1.call-update) | async-done | bytes 16400
  138.7 1.4 reshape_bitcast_fusion
  140.2 1.3 copy.20
  141.6 40.0 %psum.15 = f32[1,16,32]{2,1,0:T(8,128)S(1)} all-reduce(f32[1,16,32]{2,1,0:T(8,128)S(1)} %convolution_bitcast_fusion.3), channel_id=1, replica_groups=mesh['row'=4,'col'=8] {'row','col'}, use_global_device_ids=true, to_apply=%region_4.5 | all-reduce | flops 512 | bytes 4096 | tf_op jit(solution)/shard_map/psum | solution.py:86
  181.7 0.6 copy.30
  (35 shorter events, 2.6 us)
Async XLA Ops:
  7.2 7.5 %copy-start = (bf16[1,1,32,128,128]{4,3,2,1,0:T(8,128)(2,1)S(1)}, bf16[1,1,32,128,128]{4,3,2,1,0:T(8,128)(2,1)}, u32[]{:S(2)}) copy-start(bf16[1,1,32,128,128]{4,3,2,1,0:T(8,128)(2,1)} %param.6) | copy-start | bytes 3145732
  7.2 65.8 %reduce-scatter.5.cloned.1.call-start = ((), (), s32[]{:S(2)}) async-start(), calls=%async_computation.2 | async-start | bytes 73728 | tf_op jit(solution)/shard_map/reduce_scatter | solution.py:76
  16.3 122.5 %reduce-scatter.7.cloned.1.call-start = ((), (), s32[]{:S(2)}) async-start(), calls=%async_computation.3 | async-start | bytes 589824
  118.8 63.5 %copy-start.1 = (f32[16,128]{1,0:T(8,128)}, f32[16,128]{1,0:T(8,128)S(1)}, u32[]{:S(2)}) copy-start(f32[16,128]{1,0:T(8,128)S(1)} %convolution_multiply_fusion) | copy-start | bytes 24580
Sparse Core Ops, SparseCore 0:
  16.4 56.5 reduce-scatter.4
  76.3 62.3 reduce-scatter.6
where the time goes:
time: 190 us; the launch traced here: 189 us
  blocking collectives  86.8 us (46%)
  waiting for transfers between devices  50.7 us (27%)
  local copies, waits for them, and re-layouts  26.9 us (14%)
  between operations  14.9 us (8%)
  matrix products  7.18 us (4%)
  other arithmetic  2.72 us (1%)
    psum x1, blocking collectives, per_device(): gram = lax.psum(gram_part, ('row', 'col'))  40.3 us
    psum x1, blocking collectives, per_device(): elements = lax.psum(element_part, ('row', 'col')) / math.sqrt(total_rows)  40 us
    reduce_scatter x1, waiting for transfers between devices, per_device(): lax.psum_scatter(h_part, 'col', scatter_dimension=2, tiled=True)  30.7 us
    unnamed x8, local copies, waits for them, and re-layouts  25.5 us
    unnamed x3, waiting for transfers between devices  20 us
    all_gather x1, blocking collectives, per_device(): vector_block = lax.all_gather(vectors, 'row', axis=2, tiled=True)  6.39 us
  transfers between devices with their start and end apart: 2, of which 2 were waited for; matrix products, arithmetic and copies ran while one was open for 16% of the time, Pallas kernels for 0%

commit v1 on v0

v1 whole, which is shorter than its diff:
```python
import functools
import math

import jax
import jax.numpy as jnp
from jax import lax
from jax.experimental import pallas as pl
from jax.experimental.pallas import tpu as pltpu
from jax.sharding import PartitionSpec as P

NSIT = 6
J_OPERATORS = 2

exact_precision = lax.Precision.HIGHEST


def digits_of(size):
    digits, stride = [], 1
    while stride < size:
        rest = size // stride
        factor = next(f for f in range(2, rest + 1) if rest % f == 0)
        digits.append((stride, factor))
        stride *= factor
    return digits


def moved(index, digit, shift):
    stride, factor = digit
    value = index // stride % factor
    return index + ((value + shift) % factor - value) * stride


def sent(x, axis, digit, shift):
    size = lax.axis_size(axis)
    return lax.ppermute(x, axis, [(i, moved(i, digit, shift)) for i in range(size)])


def summed(x, axis, digit):
    parts = [sent(x, axis, digit, shift) for shift in range(1, digit[1])]
    return functools.reduce(jnp.add, parts, x)


def scatter_digit(size, piece, tile):
    for stride, factor in digits_of(size):
        if factor == 2 and piece * stride % tile == 0:
            return (stride, factor)
    return None


def product_kernel(layout, place_ref, h_list_ref, j_list_ref, vector_ref, h_ref, j_ref, *refs):
    column_tiles, row_tiles, group, halves = layout
    outs, total = refs[:halves], refs[halves]
    kept_tiles = row_tiles // halves
    vectors, tile = vector_ref.shape[1], h_ref.shape[-1]
    total[...] = jnp.zeros_like(total)
    place = place_ref[0]
    for s in range(vector_ref.shape[0]):
        for tiles, codes in ((h_ref, h_list_ref), (j_ref, j_list_ref)):
            slots = tiles.shape[1]
            for q in range(slots):
                code = codes[s * slots + q]
                spot = jnp.maximum(code, 0)
                strip = spot // column_tiles
                column = spot - strip * column_tiles
                operator = strip // row_tiles
                row = strip - operator * row_tiles
                if tiles is j_ref:
                    operator = operator + 1
                half = row // group % halves
                local = row // (group * halves) * group + row % group
                half = jnp.where(half == place, 0, 1) if halves > 1 else 0
                at = (half * kept_tiles + local) * (J_OPERATORS + 1) + operator
                at = jnp.where(code >= 0, at, row_tiles * (J_OPERATORS + 1))
                picked = vector_ref[s, :, pl.ds(pl.multiple_of(column * tile, tile), tile)]
                product = lax.dot_general(
                    picked, tiles[s, q], (((1,), (1,)), ((), ())), preferred_element_type=jnp.float32
                )
                total[s, at] += product
    count = kept_tiles * (J_OPERATORS + 1)
    for half, out in enumerate(outs):
        out[...] = total[:, half * count : (half + 1) * count]


def tile_products(place, h_list, j_list, vector_block, h_tiles, j_tiles, layout):
    column_tiles, row_tiles, group, halves = layout
    sectors, vectors = vector_block.shape[:2]
    tile = h_tiles.shape[-1]
    count = row_tiles // halves * (J_OPERATORS + 1)
    smem = pl.BlockSpec(memory_space=pltpu.SMEM)
    vmem = pl.BlockSpec(memory_space=pltpu.VMEM)
    shape = jax.ShapeDtypeStruct((sectors, count, vectors, tile), jnp.float32)
    return pl.pallas_call(
        functools.partial(product_kernel, layout),
        out_shape=[shape] * halves,
        in_specs=[smem, smem, smem, vmem, vmem, vmem],
        out_specs=[vmem] * halves,
        scratch_shapes=[
            pltpu.VMEM((sectors, row_tiles * (J_OPERATORS + 1) + 1, vectors, tile), jnp.float32)
        ],
        compiler_params=pltpu.CompilerParams(vmem_limit_bytes=8 << 20),
        name="tile_products",
    )(place, h_list, j_list, vector_block, h_tiles, j_tiles)


def gram_kernel(x_ref, out_ref):
    sectors, count = x_ref.shape[:2]
    operators = J_OPERATORS + 1
    for s in range(sectors):
        for o in range(operators):
            part = None
            for t in range(count // operators):
                term = lax.dot_general(
                    x_ref[s, t * operators],
                    x_ref[s, t * operators + o],
                    (((1,), (1,)), ((), ())),
                    precision=exact_precision,
                    preferred_element_type=jnp.float32,
                )
                part = term if part is None else part + term
            out_ref[s, o] = part


def gram_parts(x):
    sectors, _, vectors, _ = x.shape
    vmem = pl.BlockSpec(memory_space=pltpu.VMEM)
    return pl.pallas_call(
        gram_kernel,
        out_shape=jax.ShapeDtypeStruct((sectors, J_OPERATORS + 1, vectors, vectors), jnp.float32),
        in_specs=[vmem],
        out_specs=vmem,
        compiler_params=pltpu.CompilerParams(vmem_limit_bytes=4 << 20),
        name="gram_parts",
    )(x)


def root_kernel(layout, own_ref, gram_ref, x_ref, basis_ref, elements_ref):
    total_rows, own_tiles = layout
    vectors, tile = x_ref.shape[2:]
    operators = J_OPERATORS + 1

    def dot(a, b):
        return jnp.dot(a, b, precision=exact_precision, preferred_element_type=jnp.float32)

    rows = lax.broadcasted_iota(jnp.int32, (vectors, vectors), 0)
    columns = lax.broadcasted_iota(jnp.int32, (vectors, vectors), 1)
    identity = jnp.where(rows == columns, 1.0, 0.0).astype(jnp.float32)
    for s in range(x_ref.shape[0]):
        gram = gram_ref[s, 0]
        squares = jnp.sum(jnp.sum(gram * gram, axis=1, keepdims=True), axis=0, keepdims=True)
        scale = jnp.sqrt(squares + 1e-06)
        iterate = gram / scale
        root = None
        for iteration in range(NSIT):
            product = iterate if root is None else dot(root, iterate)
            middle = 1.5 * identity - 0.5 * product
            root = middle if root is None else dot(middle, root)
            if iteration < NSIT - 1:
                iterate = dot(iterate, middle)
        factor = jnp.sqrt(total_rows / scale)
        turned = root.T * factor
        for t in range(own_tiles):
            at = (own_ref[0] + t) * operators
            basis_ref[s, :, t * tile : (t + 1) * tile] = dot(turned, x_ref[s, at])
        for a in range(J_OPERATORS):
            elements_ref[s, a] = dot(turned, gram_ref[s, a + 1]) / math.sqrt(total_rows)


def orthonormal(own, gram, x, total_rows, own_tiles):
    sectors, _, vectors, tile = x.shape
    smem = pl.BlockSpec(memory_space=pltpu.SMEM)
    vmem = pl.BlockSpec(memory_space=pltpu.VMEM)
    return pl.pallas_call(
        functools.partial(root_kernel, (total_rows, own_tiles)),
        out_shape=[
            jax.ShapeDtypeStruct((sectors, vectors, own_tiles * tile), jnp.float32),
            jax.ShapeDtypeStruct((sectors, J_OPERATORS, vectors, vectors), jnp.float32),
        ],
        in_specs=[smem, vmem, vmem],
        out_specs=[vmem, vmem],
        compiler_params=pltpu.CompilerParams(vmem_limit_bytes=4 << 20),
        name="orthonormal",
    )(own, gram, x)


def per_device(vectors, h_tiles, h_list, j_tiles, j_list):
    sectors, _, piece = vectors.shape
    tile = h_tiles.shape[-1]
    n_row, n_col = lax.axis_size("row"), lax.axis_size("col")
    column = lax.axis_index("col")
    block_rows = piece * n_col
    row_tiles = block_rows // tile
    column_tiles = piece * n_row // tile
    total_rows = block_rows * n_row
    digit = scatter_digit(n_col, piece, tile)
    halves = 1 if digit is None else 2
    group = 1 if digit is None else piece * digit[0] // tile
    layout = (column_tiles, row_tiles, group, halves)
    place = jnp.zeros((1,), jnp.int32)
    if digit is not None:
        place = place + column // digit[0] % 2

    vector_block = lax.all_gather(vectors, "row", axis=2, tiled=True)
    outs = tile_products(
        place,
        h_list.reshape(-1),
        j_list.reshape(-1),
        vector_block,
        h_tiles.reshape(sectors, -1, tile, tile),
        j_tiles.reshape(sectors, -1, tile, tile),
        layout,
    )
    x = outs[0]
    if digit is not None:
        x = x + sent(outs[1], "col", digit, 1)
    for other in digits_of(n_col):
        if other != digit:
            x = summed(x, "col", other)

    gram = gram_parts(x)
    for other in digits_of(n_row):
        gram = summed(gram, "row", other)
    if digit is not None:
        gram = summed(gram, "col", digit)

    own_tiles = max(1, piece // tile)
    first = column * piece // tile
    own = first if digit is None else first // (group * 2) * group + first % group
    basis, elements = orthonormal(own.reshape(1).astype(jnp.int32), gram, x, total_rows, own_tiles)
    if piece < tile:
        basis = lax.dynamic_slice_in_dim(basis, column * piece % tile, piece, 2)
    return (basis, elements)


def solution(mesh):
    return jax.shard_map(
        per_device,
        mesh=mesh,
        in_specs=(
            P(None, None, ("col", "row")),
            P(None, "row", "col", None, None),
            P(None, "row", "col"),
            P(None, "row", "col", None, None),
            P(None, "row", "col"),
        ),
        out_specs=(P(None, None, ("row", "col")), P()),
        check_vma=False,
    )
```

time: 190 us -> 39.5 us (0.21)
  blocking collectives: 86.8 us -> 6.13 us
  waiting for transfers between devices: 50.7 us -> 14.2 us
  local copies, waits for them, and re-layouts: 26.9 us -> 3.57 us
  between operations: 14.9 us -> 0.68 us
  starting transfers between devices: 0.08 us -> 10.3 us
  matrix products: 7.18 us -> 0 us
  Pallas kernels: 0 us -> 4.35 us
  other arithmetic: 2.72 us -> 0.05 us
    psum x2 -> x0, blocking collectives: 80.4 us -> none  [the longest x1 40.3 us: per_device(): gram = lax.psum(gram_part, ('row', 'col'))]
    reduce_scatter x1 -> x0, waiting for transfers between devices: 30.7 us -> none  [per_device(): lax.psum_scatter(h_part, 'col', scatter_dimension=2, tiled=True)]
    unnamed x8 -> x10, local copies, waits for them, and re-layouts: 25.5 us -> 3.57 us
    unnamed x3 -> x0, waiting for transfers between devices: 20 us -> none
    ppermute x0 -> x6, waiting for transfers between devices: none -> 14.2 us  [sent(): lax.ppermute(x, axis, [(i, moved(i, digit, shift)) for i in range(size)])]
    ppermute x0 -> x6, starting transfers between devices: none -> 10.3 us  [sent(): lax.ppermute(x, axis, [(i, moved(i, digit, shift)) for i in range(size)])]
    dot_general x26 -> x0, matrix products: 7.18 us -> none  [the longest x2 1.93 us: local_product(): jnp.einsum('sqab,sqkb->sqka', tile_data, picked, preferred_element_type=j...]
    pallas_call x0 -> x3, Pallas kernels: none -> 4.35 us  [the longest x1 2.52 us: orthonormal(): pl.pallas_call(functools.partial(root_kernel, (total_rows, own_tiles)), o...]
  transfers between devices with their start and end apart: 2 -> 6, of which waited for: 2 -> 6; matrix products, arithmetic and copies ran while one was open for 16% -> 0% of each run, Pallas kernels for 0% -> 0%
where the time goes in v1:
time: 39.5 us; the launch traced here: 39.3 us
  waiting for transfers between devices  14.2 us (36%)
  starting transfers between devices  10.3 us (26%)
  blocking collectives  6.13 us (16%)
  Pallas kernels  4.35 us (11%)
  local copies, waits for them, and re-layouts  3.57 us (9%)
  between operations  0.68 us (2%)
    ppermute x6, waiting for transfers between devices, sent(): lax.ppermute(x, axis, [(i, moved(i, digit, shift)) for i in range(size)])  14.2 us
    ppermute x6, starting transfers between devices, sent(): lax.ppermute(x, axis, [(i, moved(i, digit, shift)) for i in range(size)])  10.3 us
    all_gather x1, blocking collectives, per_device(): vector_block = lax.all_gather(vectors, 'row', axis=2, tiled=True)  6.13 us
    unnamed x10, local copies, waits for them, and re-layouts  3.57 us
    pallas_call x1, Pallas kernels, orthonormal(): pl.pallas_call(functools.partial(root_kernel, (total_rows, own_tiles)), o...  2.52 us
    pallas_call x1, Pallas kernels, tile_products(): pl.pallas_call(functools.partial(product_kernel, layout), out_shape=[shap...  1.52 us
  transfers between devices with their start and end apart: 6, of which 6 were waited for; matrix products, arithmetic and copies ran while one was open for 0% of the time, Pallas kernels for 0%

profile of v1, /device:TPU:0, one launch (start us, length us, event | category | flops | bytes accessed | tf_op | source)
XLA Modules:
  0.0 39.3 jit_solution(1879469538205418049)
XLA Ops:
  0.6 0.0 copy-start.4
  0.6 0.7 %copy-done.4 = bf16[1,16,128]{2,1,0:T(8,128)(2,1)S(1)} copy-done((bf16[1,16,128]{2,1,0:T(8,128)(2,1)S(1)}, bf16[1,16,128]{2,1,0:T(8,128)(2,1)}, u32[]{:S(2)}) %copy-start.4) | copy-done | bytes 4120
  1.3 6.1 %all_gather.3.vector_ref = bf16[1,16,512]{2,1,0:T(8,128)(2,1)S(1)} all-gather(bf16[1,16,128]{2,1,0:T(8,128)(2,1)S(1)} %copy-done.4), channel_id=1, replica_groups=mesh['row'=4,'col'=8] {'row'}, dimensions={2}, use_global_device_ids=true | all-gather | bytes 20480 | tf_op jit(solution)/shard_map/all_gather | solution.py:202
  7.5 0.0 copy-start.2
  7.5 0.0 copy-start.3
  7.5 0.7 %copy-done.2 = s32[1,1,32]{2,1,0:T(1,128)S(1)} copy-done((s32[1,1,32]{2,1,0:T(1,128)S(1)}, s32[1,1,32]{2,1,0:T(1,128)}, u32[]{:S(2)}) %copy-start.2) | copy-done | bytes 152
  8.1 0.0 copy-done.3
  8.1 1.2 %copy-done = bf16[1,1,32,128,128]{4,3,2,1,0:T(8,128)(2,1)S(1)} copy-done((bf16[1,1,32,128,128]{4,3,2,1,0:T(8,128)(2,1)S(1)}, bf16[1,1,32,128,128]{4,3,2,1,0:T(8,128)(2,1)}, u32[]{:S(2)}) %copy-start) | copy-done | bytes 1048600
  9.4 1.0 %copy-done.1 = bf16[1,1,12,128,128]{4,3,2,1,0:T(8,128)(2,1)S(1)} copy-done((bf16[1,1,12,128,128]{4,3,2,1,0:T(8,128)(2,1)S(1)}, bf16[1,1,12,128,128]{4,3,2,1,0:T(8,128)(2,1)}, u32[]{:S(2)}) %copy-start.1) | copy-done | bytes 393240
  10.3 1.5 %tile_products.1 = (f32[1,12,16,128]{3,2,1,0:T(8,128)S(1)}, f32[1,12,16,128]{3,2,1,0:T(8,128)S(1)}) custom-call(s32[1]{0:T(128)} %bitcast.1.place_ref, s32[32]{0:T(128)S(1)} %bitcast.8, s32[12]{0:T(128)S(1)} %bitcast.9, bf16[1,16,512]{2,1,0:T(8,128)(2,1)S(1)} %all_gather.3.vector_ref, bf16[1,32,128,128]{3,2,1,0:T(8,128)(2,1)S(1)} %bitcast.6, ...), custom_call_target="tpu_custom_call" | custom-call | tf_op jit(solution)/shard_map/tile_products/pallas_call | solution.py:92
  11.9 2.1 %collective-permute-start = (f32[1,12,16,128]{3,2,1,0:T(8,128)S(1)}, f32[1,12,16,128]{3,2,1,0:T(8,128)S(1)}, u32[]{:S(2)}, u32[]{:S(2)}) collective-permute-start(f32[1,12,16,128]{3,2,1,0:T(8,128)S(1)} %get-tuple-element.5), channel_id=1, source_target_pairs={{0,1},{1,0},{2,3},{3,2},{4,5},{5,4},{6,7},{7,6},{8,9},{9,8},{10,11... | collective-permute-start | bytes 294920 | tf_op jit(solution)/shard_map/ppermute | solution.py:35
  14.0 3.3 %collective-permute-done = f32[1,12,16,128]{3,2,1,0:T(8,128)S(1)} collective-permute-done((f32[1,12,16,128]{3,2,1,0:T(8,128)S(1)}, f32[1,12,16,128]{3,2,1,0:T(8,128)S(1)}, u32[]{:S(2)}, u32[]{:S(2)}) %collective-permute-start) | collective-permute-done | bytes 98336 | tf_op jit(solution)/shard_map/ppermute | solution.py:35
  17.3 1.9 %collective-permute-start.1 = (f32[1,12,16,128]{3,2,1,0:T(8,128)S(1)}, f32[1,12,16,128]{3,2,1,0:T(8,128)S(1)}, u32[]{:S(2)}, u32[]{:S(2)}) collective-permute-start(f32[1,12,16,128]{3,2,1,0:T(8,128)S(1)} %add.32), channel_id=1, source_target_pairs={{0,2},{1,3},{2,0},{3,1},{4,6},{5,7},{6,4},{7,5},{8,10},{9,11},{10,... | collective-permute-start | bytes 294920 | tf_op jit(solution)/shard_map/ppermute | solution.py:35
  19.2 2.8 %collective-permute-done.1 = f32[1,12,16,128]{3,2,1,0:T(8,128)S(1)} collective-permute-done((f32[1,12,16,128]{3,2,1,0:T(8,128)S(1)}, f32[1,12,16,128]{3,2,1,0:T(8,128)S(1)}, u32[]{:S(2)}, u32[]{:S(2)}) %collective-permute-start.1) | collective-permute-done | bytes 98336 | tf_op jit(solution)/shard_map/ppermute | solution.py:35
  22.0 2.9 %collective-permute-start.2 = (f32[1,12,16,128]{3,2,1,0:T(8,128)S(1)}, f32[1,12,16,128]{3,2,1,0:T(8,128)S(1)}, u32[]{:S(2)}, u32[]{:S(2)}) collective-permute-start(f32[1,12,16,128]{3,2,1,0:T(8,128)S(1)} %add.33), channel_id=1, source_target_pairs={{0,4},{1,5},{2,6},{3,7},{4,0},{5,1},{6,2},{7,3},{8,12},{9,13},{10,... | collective-permute-start | bytes 294920 | tf_op jit(solution)/shard_map/ppermute | solution.py:35
  24.9 2.7 %collective-permute-done.2 = f32[1,12,16,128]{3,2,1,0:T(8,128)S(1)} collective-permute-done((f32[1,12,16,128]{3,2,1,0:T(8,128)S(1)}, f32[1,12,16,128]{3,2,1,0:T(8,128)S(1)}, u32[]{:S(2)}, u32[]{:S(2)}) %collective-permute-start.2) | collective-permute-done | bytes 98336 | tf_op jit(solution)/shard_map/ppermute | solution.py:35
  27.6 0.3 gram_parts.1
  27.9 0.0 collective-permute-start.3
  27.9 1.2 %collective-permute-done.3 = f32[1,3,16,16]{3,2,1,0:T(8,128)S(1)} collective-permute-done((f32[1,3,16,16]{3,2,1,0:T(8,128)S(1)}, f32[1,3,16,16]{3,2,1,0:T(8,128)S(1)}, u32[]{:S(2)}, u32[]{:S(2)}) %collective-permute-start.3) | collective-permute-done | bytes 3104 | tf_op jit(solution)/shard_map/ppermute | solution.py:35
  29.1 1.7 %collective-permute-start.4 = (f32[1,3,16,16]{3,2,1,0:T(8,128)S(1)}, f32[1,3,16,16]{3,2,1,0:T(8,128)S(1)}, u32[]{:S(2)}, u32[]{:S(2)}) collective-permute-start(f32[1,3,16,16]{3,2,1,0:T(8,128)S(1)} %add.35), channel_id=1, source_target_pairs={{0,16},{8,24},{16,0},{24,8},{1,17},{9,25},{17,1},{25,9},{2,18},{10... | collective-permute-start | bytes 9224 | tf_op jit(solution)/shard_map/ppermute | solution.py:35
  30.8 2.1 %collective-permute-done.4 = f32[1,3,16,16]{3,2,1,0:T(8,128)S(1)} collective-permute-done((f32[1,3,16,16]{3,2,1,0:T(8,128)S(1)}, f32[1,3,16,16]{3,2,1,0:T(8,128)S(1)}, u32[]{:S(2)}, u32[]{:S(2)}) %collective-permute-start.4) | collective-permute-done | bytes 3104 | tf_op jit(solution)/shard_map/ppermute | solution.py:35
  32.9 1.8 %collective-permute-start.5 = (f32[1,3,16,16]{3,2,1,0:T(8,128)S(1)}, f32[1,3,16,16]{3,2,1,0:T(8,128)S(1)}, u32[]{:S(2)}, u32[]{:S(2)}) collective-permute-start(f32[1,3,16,16]{3,2,1,0:T(8,128)S(1)} %add.36), channel_id=1, source_target_pairs={{0,1},{1,0},{2,3},{3,2},{4,5},{5,4},{6,7},{7,6},{8,9},{9,8},{10,11... | collective-permute-start | bytes 9224 | tf_op jit(solution)/shard_map/ppermute | solution.py:35
  34.7 2.1 %collective-permute-done.5 = f32[1,3,16,16]{3,2,1,0:T(8,128)S(1)} collective-permute-done((f32[1,3,16,16]{3,2,1,0:T(8,128)S(1)}, f32[1,3,16,16]{3,2,1,0:T(8,128)S(1)}, u32[]{:S(2)}, u32[]{:S(2)}) %collective-permute-start.5) | collective-permute-done | bytes 3104 | tf_op jit(solution)/shard_map/ppermute | solution.py:35
  36.8 2.5 %orthonormal.1 = (f32[1,16,128]{2,1,0:T(8,128)}, f32[1,2,16,16]{3,2,1,0:T(8,128)}) custom-call(s32[1]{0:T(128)} %bitcast.own_ref, f32[1,3,16,16]{3,2,1,0:T(8,128)S(1)} %add.37.gram_ref, f32[1,12,16,128]{3,2,1,0:T(8,128)S(1)} %add.34.x_ref), custom_call_target="tpu_custom_call" | custom-call | tf_op jit(solution)/shard_map/orthonormal/pallas_call | solution.py:172
  (8 shorter events, 0.1 us)
Async XLA Ops:
  0.6 0.7 %copy-start.4 = (bf16[1,16,128]{2,1,0:T(8,128)(2,1)S(1)}, bf16[1,16,128]{2,1,0:T(8,128)(2,1)}, u32[]{:S(2)}) copy-start(bf16[1,16,128]{2,1,0:T(8,128)(2,1)} %param.5) | copy-start | bytes 12292
  7.5 0.7 %copy-start.2 = (s32[1,1,32]{2,1,0:T(1,128)S(1)}, s32[1,1,32]{2,1,0:T(1,128)}, u32[]{:S(2)}) copy-start(s32[1,1,32]{2,1,0:T(1,128)} %param.7) | copy-start | bytes 388
  7.5 0.7 %copy-start.3 = (s32[1,1,12]{2,1,0:T(1,128)S(1)}, s32[1,1,12]{2,1,0:T(1,128)}, u32[]{:S(2)}) copy-start(s32[1,1,12]{2,1,0:T(1,128)} %param.9) | copy-start | bytes 148
  8.1 1.2 %copy-start = (bf16[1,1,32,128,128]{4,3,2,1,0:T(8,128)(2,1)S(1)}, bf16[1,1,32,128,128]{4,3,2,1,0:T(8,128)(2,1)}, u32[]{:S(2)}) copy-start(bf16[1,1,32,128,128]{4,3,2,1,0:T(8,128)(2,1)} %param.6) | copy-start | bytes 3145732
  9.4 1.0 %copy-start.1 = (bf16[1,1,12,128,128]{4,3,2,1,0:T(8,128)(2,1)S(1)}, bf16[1,1,12,128,128]{4,3,2,1,0:T(8,128)(2,1)}, u32[]{:S(2)}) copy-start(bf16[1,1,12,128,128]{4,3,2,1,0:T(8,128)(2,1)} %param.8) | copy-start | bytes 1179652
  11.9 5.4 %collective-permute-start = (f32[1,12,16,128]{3,2,1,0:T(8,128)S(1)}, f32[1,12,16,128]{3,2,1,0:T(8,128)S(1)}, u32[]{:S(2)}, u32[]{:S(2)}) collective-permute-start(f32[1,12,16,128]{3,2,1,0:T(8,128)S(1)} %get-tuple-element.5), channel_id=1, source_target_pairs={{0,1},{1,0},{2,3},{3,2},{4,5},{5,4},{6,7},{7,6},{8,9},{9,8},{10,11... | collective-permute-start | bytes 294920 | tf_op jit(solution)/shard_map/ppermute | solution.py:35
  17.3 4.7 %collective-permute-start.1 = (f32[1,12,16,128]{3,2,1,0:T(8,128)S(1)}, f32[1,12,16,128]{3,2,1,0:T(8,128)S(1)}, u32[]{:S(2)}, u32[]{:S(2)}) collective-permute-start(f32[1,12,16,128]{3,2,1,0:T(8,128)S(1)} %add.32), channel_id=1, source_target_pairs={{0,2},{1,3},{2,0},{3,1},{4,6},{5,7},{6,4},{7,5},{8,10},{9,11},{10,... | collective-permute-start | bytes 294920 | tf_op jit(solution)/shard_map/ppermute | solution.py:35
  22.0 5.6 %collective-permute-start.2 = (f32[1,12,16,128]{3,2,1,0:T(8,128)S(1)}, f32[1,12,16,128]{3,2,1,0:T(8,128)S(1)}, u32[]{:S(2)}, u32[]{:S(2)}) collective-permute-start(f32[1,12,16,128]{3,2,1,0:T(8,128)S(1)} %add.33), channel_id=1, source_target_pairs={{0,4},{1,5},{2,6},{3,7},{4,0},{5,1},{6,2},{7,3},{8,12},{9,13},{10,... | collective-permute-start | bytes 294920 | tf_op jit(solution)/shard_map/ppermute | solution.py:35
  27.9 1.2 %collective-permute-start.3 = (f32[1,3,16,16]{3,2,1,0:T(8,128)S(1)}, f32[1,3,16,16]{3,2,1,0:T(8,128)S(1)}, u32[]{:S(2)}, u32[]{:S(2)}) collective-permute-start(f32[1,3,16,16]{3,2,1,0:T(8,128)S(1)} %gram_parts.1), channel_id=1, source_target_pairs={{0,8},{8,0},{16,24},{24,16},{1,9},{9,1},{17,25},{25,17},{2,10},{10... | collective-permute-start | bytes 9224 | tf_op jit(solution)/shard_map/ppermute | solution.py:35
  29.1 3.8 %collective-permute-start.4 = (f32[1,3,16,16]{3,2,1,0:T(8,128)S(1)}, f32[1,3,16,16]{3,2,1,0:T(8,128)S(1)}, u32[]{:S(2)}, u32[]{:S(2)}) collective-permute-start(f32[1,3,16,16]{3,2,1,0:T(8,128)S(1)} %add.35), channel_id=1, source_target_pairs={{0,16},{8,24},{16,0},{24,8},{1,17},{9,25},{17,1},{25,9},{2,18},{10... | collective-permute-start | bytes 9224 | tf_op jit(solution)/shard_map/ppermute | solution.py:35
  32.9 3.8 %collective-permute-start.5 = (f32[1,3,16,16]{3,2,1,0:T(8,128)S(1)}, f32[1,3,16,16]{3,2,1,0:T(8,128)S(1)}, u32[]{:S(2)}, u32[]{:S(2)}) collective-permute-start(f32[1,3,16,16]{3,2,1,0:T(8,128)S(1)} %add.36), channel_id=1, source_target_pairs={{0,1},{1,0},{2,3},{3,2},{4,5},{5,4},{6,7},{7,6},{8,9},{9,8},{10,11... | collective-permute-start | bytes 9224 | tf_op jit(solution)/shard_map/ppermute | solution.py:35

commit v2 on v1

v2 whole, which is shorter than its diff:
```python
import functools
import math

import jax
import jax.numpy as jnp
from jax import lax
from jax.experimental import pallas as pl
from jax.experimental.pallas import tpu as pltpu
from jax.sharding import PartitionSpec as P

NSIT = 6
J_OPERATORS = 2
LANES = 128

exact_precision = lax.Precision.HIGHEST


def digits_of(size):
    digits, stride = [], 1
    while stride < size:
        rest = size // stride
        factor = next(f for f in range(2, rest + 1) if rest % f == 0)
        digits.append((stride, factor))
        stride *= factor
    return digits


def moved(index, digit, shift):
    stride, factor = digit
    value = index // stride % factor
    return index + ((value + shift) % factor - value) * stride


def sent(x, axis, digit, shift):
    size = lax.axis_size(axis)
    return lax.ppermute(x, axis, [(i, moved(i, digit, shift)) for i in range(size)])


def across(x, row_mask, column_mask):
    n_row, n_col = lax.axis_size("row"), lax.axis_size("col")
    pairs = [(r, c) for r in range(n_row) for c in range(n_col)]
    moves = [(r * n_col + c, (r ^ row_mask) * n_col + (c ^ column_mask)) for r, c in pairs]
    return lax.ppermute(x, ("row", "col"), moves)


def summed(x, axis, digit):
    parts = [sent(x, axis, digit, shift) for shift in range(1, digit[1])]
    return functools.reduce(jnp.add, parts, x)


def scatter_digit(size, piece, tile):
    for stride, factor in digits_of(size):
        if factor == 2 and piece * stride % tile == 0:
            return (stride, factor)
    return None


def stage_kernel(count, *refs):
    sources, targets, arrived = refs[:count], refs[count : 2 * count], refs[2 * count]
    copies = [
        pltpu.make_async_copy(source, target, arrived.at[n])
        for n, (source, target) in enumerate(zip(sources, targets))
    ]
    for copy in copies:
        copy.start()
    for copy in copies:
        copy.wait()


def staged(*arrays):
    return pl.pallas_call(
        functools.partial(stage_kernel, len(arrays)),
        out_shape=[jax.ShapeDtypeStruct(a.shape, a.dtype) for a in arrays],
        in_specs=[pl.BlockSpec(memory_space=pltpu.HBM)] * len(arrays),
        out_specs=[pl.BlockSpec(memory_space=pltpu.VMEM)] * len(arrays),
        scratch_shapes=[pltpu.SemaphoreType.DMA((len(arrays),))],
        compiler_params=pltpu.CompilerParams(vmem_limit_bytes=8 << 20),
        cost_estimate=pl.CostEstimate(
            flops=0, transcendentals=0, bytes_accessed=sum(a.size * a.dtype.itemsize for a in arrays)
        ),
        name="staged",
    )(*arrays)


def product_kernel(layout, h_list_ref, j_list_ref, *refs):
    column_tiles, row_tiles, group, halves, stride, pieces = layout
    vector_refs, (h_ref, j_ref), outs = refs[:pieces], refs[pieces : pieces + 2], refs[pieces + 2 : -2]
    picked, total = refs[-2:]
    kept_tiles = row_tiles // halves
    tile = h_ref.shape[-1]
    each = column_tiles // pieces
    for n, vector_ref in enumerate(vector_refs):
        for t in range(each):
            picked[:, n * each + t] = vector_ref[:, :, t * tile : (t + 1) * tile]
    total[...] = jnp.zeros_like(total)
    place = lax.axis_index("col") // stride % halves
    turn = lax.axis_index("row")
    for s in range(total.shape[0]):
        for tiles, codes in ((h_ref, h_list_ref), (j_ref, j_list_ref)):
            slots = tiles.shape[1]
            for q in range(slots):
                code = codes[s * slots + q]
                spot = jnp.maximum(code, 0)
                strip = spot // column_tiles
                column = spot - strip * column_tiles
                if pieces > 1:
                    column = column ^ turn
                operator = strip // row_tiles
                row = strip - operator * row_tiles
                if tiles is j_ref:
                    operator = operator + 1
                half = row // group % halves
                local = row // (group * halves) * group + row % group
                half = jnp.where(half == place, 0, 1) if halves > 1 else 0
                at = (half * kept_tiles + local) * (J_OPERATORS + 1) + operator
                at = jnp.where(code >= 0, at, row_tiles * (J_OPERATORS + 1))
                product = lax.dot_general(
                    picked[s, column],
                    tiles[s, q],
                    (((1,), (1,)), ((), ())),
                    preferred_element_type=jnp.float32,
                )
                total[s, at] += product
    count = kept_tiles * (J_OPERATORS + 1)
    for half, out in enumerate(outs):
        out[...] = total[:, half * count : (half + 1) * count]


def tile_products(h_list, j_list, vectors, h_tiles, j_tiles, layout):
    column_tiles, row_tiles, group, halves, stride, pieces = layout
    sectors, count_vectors = vectors[0].shape[:2]
    tile = h_tiles.shape[-1]
    count = row_tiles // halves * (J_OPERATORS + 1)
    smem = pl.BlockSpec(memory_space=pltpu.SMEM)
    vmem = pl.BlockSpec(memory_space=pltpu.VMEM)
    shape = jax.ShapeDtypeStruct((sectors, count, count_vectors, tile), jnp.float32)
    extended = (sectors, row_tiles * (J_OPERATORS + 1) + 1, count_vectors, tile)
    return pl.pallas_call(
        functools.partial(product_kernel, layout),
        out_shape=[shape] * halves,
        in_specs=[smem] * 2 + [vmem] * (pieces + 2),
        out_specs=[vmem] * halves,
        scratch_shapes=[
            pltpu.VMEM((sectors, column_tiles, count_vectors, tile), jnp.bfloat16),
            pltpu.VMEM(extended, jnp.float32),
        ],
        compiler_params=pltpu.CompilerParams(vmem_limit_bytes=8 << 20),
        name="tile_products",
    )(h_list, j_list, *vectors, h_tiles, j_tiles)


def gram_kernel(x_ref, out_ref):
    sectors, count, vectors, _ = x_ref.shape
    operators = J_OPERATORS + 1
    out_ref[...] = jnp.zeros_like(out_ref)
    for s in range(sectors):
        part = None
        for t in range(count // operators):
            strip = x_ref[s, t * operators : (t + 1) * operators]
            term = lax.dot_general(
                strip[0],
                strip.reshape(operators * vectors, -1),
                (((1,), (1,)), ((), ())),
                precision=exact_precision,
                preferred_element_type=jnp.float32,
            )
            part = term if part is None else part + term
        out_ref[s, :, : operators * vectors] = part


def gram_parts(x):
    sectors, _, vectors, _ = x.shape
    vmem = pl.BlockSpec(memory_space=pltpu.VMEM)
    return pl.pallas_call(
        gram_kernel,
        out_shape=jax.ShapeDtypeStruct((sectors, vectors, LANES), jnp.float32),
        in_specs=[vmem],
        out_specs=vmem,
        compiler_params=pltpu.CompilerParams(vmem_limit_bytes=4 << 20),
        name="gram_parts",
    )(x)


def columns_of(matrix, first, count, width):
    return [jnp.broadcast_to(matrix[:, k : k + 1], (count, width)) for k in range(first, first + count)]


def product_of(columns, right):
    parts = [column * right[k : k + 1, :] for k, column in enumerate(columns)]
    while len(parts) > 1:
        parts = [functools.reduce(jnp.add, parts[i : i + 2]) for i in range(0, len(parts), 2)]
    return parts[0]


def root_kernel(layout, gram_ref, x_ref, basis_ref, elements_ref):
    total_rows, own_tiles, piece, group, halves = layout
    first = lax.axis_index("col") * piece // x_ref.shape[-1]
    own = first if halves == 1 else first // (group * halves) * group + first % group
    vectors, tile = x_ref.shape[2:]
    operators = J_OPERATORS + 1
    shape = (vectors, LANES)
    rows = lax.broadcasted_iota(jnp.int32, shape, 0)
    lanes = lax.broadcasted_iota(jnp.int32, shape, 1)
    is_gram = lanes < vectors
    root_at = operators * vectors
    step = jnp.where(lanes == rows, 1.5, 0.0).astype(jnp.float32)
    for s in range(x_ref.shape[0]):
        held = gram_ref[s]
        squares = jnp.where(is_gram, held * held, 0.0)
        squares = jnp.sum(jnp.sum(squares, axis=1, keepdims=True), axis=0, keepdims=True)
        scale = jnp.sqrt(squares + 1e-06)
        held = jnp.where(is_gram, held / scale, held)
        held = jnp.where(lanes == rows + root_at, 1.0, held)
        for iteration in range(NSIT):
            middle = columns_of(step - 0.5 * held, 0, vectors, LANES)
            once = product_of(middle, held)
            if iteration < NSIT - 1:
                held = jnp.where(is_gram, product_of(middle, once), once)
            else:
                held = once
        held = held * jnp.sqrt(total_rows / scale)
        root = columns_of(held, root_at, vectors, tile)
        for t in range(own_tiles):
            at = (own + t) * operators
            basis_ref[s, :, t * tile : (t + 1) * tile] = product_of(root, x_ref[s, at])
        for a in range(J_OPERATORS):
            elements = held[:, (a + 1) * vectors : (a + 2) * vectors]
            elements_ref[s, a] = elements / math.sqrt(total_rows)


def orthonormal(gram, x, layout):
    sectors, _, vectors, tile = x.shape
    vmem = pl.BlockSpec(memory_space=pltpu.VMEM)
    return pl.pallas_call(
        functools.partial(root_kernel, layout),
        out_shape=[
            jax.ShapeDtypeStruct((sectors, vectors, layout[1] * tile), jnp.float32),
            jax.ShapeDtypeStruct((sectors, J_OPERATORS, vectors, vectors), jnp.float32),
        ],
        in_specs=[vmem, vmem],
        out_specs=[vmem, vmem],
        compiler_params=pltpu.CompilerParams(vmem_limit_bytes=4 << 20),
        name="orthonormal",
    )(gram, x)


def per_device(vectors, h_tiles, h_list, j_tiles, j_list):
    sectors, _, piece = vectors.shape
    tile = h_tiles.shape[-1]
    n_row, n_col = lax.axis_size("row"), lax.axis_size("col")
    column = lax.axis_index("col")
    block_rows = piece * n_col
    row_tiles = block_rows // tile
    column_tiles = piece * n_row // tile
    total_rows = block_rows * n_row
    digit = scatter_digit(n_col, piece, tile)
    halves = 1 if digit is None else 2
    group = 1 if digit is None else piece * digit[0] // tile
    stride = 1 if digit is None else digit[0]
    direct = piece == tile and n_row in (2, 4)

    own_vectors, h_codes, j_codes, h_held, j_held = staged(
        vectors,
        h_list.reshape(-1),
        j_list.reshape(-1),
        h_tiles.reshape(sectors, -1, tile, tile),
        j_tiles.reshape(sectors, -1, tile, tile),
    )
    if direct:
        parts = [own_vectors]
        for mask in range(1, n_row):
            parts.append(lax.ppermute(vectors, "row", [(i, i ^ mask) for i in range(n_row)]))
    else:
        parts = [lax.all_gather(vectors, "row", axis=2, tiled=True)]
    outs = tile_products(
        h_codes, j_codes, parts, h_held, j_held,
        (column_tiles, row_tiles, group, halves, stride, len(parts)),
    )
    x = outs[0]
    if digit is not None:
        x = x + sent(outs[1], "col", digit, 1)
    for other in digits_of(n_col):
        if other != digit:
            x = summed(x, "col", other)

    gram = gram_parts(x)
    if direct and n_row == 4 and digit is not None:
        gram = summed(gram, "row", (1, 2))
        gram = gram + across(gram, 0, digit[0]) + across(gram, 2, 0) + across(gram, 2, digit[0])
    else:
        for other in digits_of(n_row):
            gram = summed(gram, "row", other)
        if digit is not None:
            gram = summed(gram, "col", digit)

    own_tiles = max(1, piece // tile)
    basis, elements = orthonormal(gram, x, (total_rows, own_tiles, piece, group, halves))
    if piece < tile:
        basis = lax.dynamic_slice_in_dim(basis, column * piece % tile, piece, 2)
    return (basis, elements)


def solution(mesh):
    return jax.shard_map(
        per_device,
        mesh=mesh,
        in_specs=(
            P(None, None, ("col", "row")),
            P(None, "row", "col", None, None),
            P(None, "row", "col"),
            P(None, "row", "col", None, None),
            P(None, "row", "col"),
        ),
        out_specs=(P(None, None, ("row", "col")), P()),
        check_vma=False,
    )
```

time: 39.5 us -> 34.1 us (0.86)
  blocking collectives: 6.13 us -> 0 us
  starting transfers between devices: 10.3 us -> 12.6 us
  local copies, waits for them, and re-layouts: 3.57 us -> 2.89 us
  Pallas kernels: 4.35 us -> 3.75 us
    ppermute x0 -> x6, starting transfers between devices: none -> 6.68 us  [the longest x3 3.49 us: across(): return lax.ppermute(x, ('row', 'col'), moves)]
    all_gather x1 -> x0, blocking collectives: 6.13 us -> none  [per_device(): vector_block = lax.all_gather(vectors, 'row', axis=2, tiled=True)]
    ppermute x6 -> x4, starting transfers between devices: 10.3 us -> 5.88 us  [sent(): lax.ppermute(x, axis, [(i, moved(i, digit, shift)) for i in range(size)])]
    ppermute x6 -> x4, waiting for transfers between devices: 14.2 us -> 10.3 us  [sent(): lax.ppermute(x, axis, [(i, moved(i, digit, shift)) for i in range(size)])]
    ppermute x0 -> x6, waiting for transfers between devices: none -> 3.69 us  [the longest x3 3.14 us: across(): return lax.ppermute(x, ('row', 'col'), moves)]
    unnamed x10, local copies, waits for them, and re-layouts: 3.57 us -> 2.89 us
    pallas_call x2 -> x3, Pallas kernels: 2.83 us -> 2.23 us  [the longest x1 1.67 us: orthonormal(): pl.pallas_call(functools.partial(root_kernel, layout), out_shape=[jax.Sha...]
  transfers between devices with their start and end apart: 6 -> 10, of which waited for: 6 -> 8; matrix products, arithmetic and copies ran while one was open for 0% -> 0% of each run, Pallas kernels for 0% -> 1%
where the time goes in v2:
time: 34.1 us; the launch traced here: 33.9 us
  waiting for transfers between devices  14 us (41%)
  starting transfers between devices  12.6 us (37%)
  Pallas kernels  3.75 us (11%)
  local copies, waits for them, and re-layouts  2.89 us (8%)
  between operations  0.7 us (2%)
    ppermute x4, waiting for transfers between devices, sent(): lax.ppermute(x, axis, [(i, moved(i, digit, shift)) for i in range(size)])  10.3 us
    ppermute x4, starting transfers between devices, sent(): lax.ppermute(x, axis, [(i, moved(i, digit, shift)) for i in range(size)])  5.88 us
    ppermute x3, starting transfers between devices, across(): return lax.ppermute(x, ('row', 'col'), moves)  3.49 us
    ppermute x3, starting transfers between devices, per_device(): lax.ppermute(vectors, 'row', [(i, i ^ mask) for i in range(n_row)])  3.19 us
    ppermute x3, waiting for transfers between devices, across(): return lax.ppermute(x, ('row', 'col'), moves)  3.14 us
    unnamed x10, local copies, waits for them, and re-layouts  2.89 us
    pallas_call x1, Pallas kernels, orthonormal(): pl.pallas_call(functools.partial(root_kernel, layout), out_shape=[jax.Sha...  1.67 us
    pallas_call x1, Pallas kernels, tile_products(): pl.pallas_call(functools.partial(product_kernel, layout), out_shape=[shap...  1.52 us
  transfers between devices with their start and end apart: 10, of which 8 were waited for; matrix products, arithmetic and copies ran while one was open for 0% of the time, Pallas kernels for 1%

profile of v2, /device:TPU:0, one launch (start us, length us, event | category | flops | bytes accessed | tf_op | source)
XLA Modules:
  0.0 33.9 jit_solution(5074669632093358527)
XLA Ops:
  0.6 0.6 %collective-permute-start = (bf16[1,16,128]{2,1,0:T(8,128)(2,1)}, bf16[1,16,128]{2,1,0:T(8,128)(2,1)S(1)}, u32[]{:S(2)}, u32[]{:S(2)}) collective-permute-start(bf16[1,16,128]{2,1,0:T(8,128)(2,1)} %refs_0_.1), channel_id=1, source_target_pairs={{0,8},{8,0},{16,24},{24,16},{1,9},{9,1},{17,25},{25,17},{2,10},{10... | collective-permute-start | bytes 12296 | tf_op jit(solution)/shard_map/ppermute | solution.py:272
  1.2 2.6 %collective-permute-start.2 = (bf16[1,16,128]{2,1,0:T(8,128)(2,1)}, bf16[1,16,128]{2,1,0:T(8,128)(2,1)S(1)}, u32[]{:S(2)}, u32[]{:S(2)}) collective-permute-start(bf16[1,16,128]{2,1,0:T(8,128)(2,1)} %refs_0_.1), channel_id=1, source_target_pairs={{0,24},{8,16},{16,8},{24,0},{1,25},{9,17},{17,9},{25,1},{2,26},{10... | collective-permute-start | bytes 12296 | tf_op jit(solution)/shard_map/ppermute | solution.py:272
  3.8 0.0 collective-permute-start.1
  3.8 0.6 %copy-done.3 = s32[1,1,32]{2,1,0:T(1,128)S(1)} copy-done((s32[1,1,32]{2,1,0:T(1,128)S(1)}, s32[1,1,32]{2,1,0:T(1,128)}, u32[]{:S(2)}) %copy-start.3) | copy-done | bytes 152
  4.5 1.2 %copy-done = bf16[1,1,32,128,128]{4,3,2,1,0:T(8,128)(2,1)S(1)} copy-done((bf16[1,1,32,128,128]{4,3,2,1,0:T(8,128)(2,1)S(1)}, bf16[1,1,32,128,128]{4,3,2,1,0:T(8,128)(2,1)}, u32[]{:S(2)}) %copy-start) | copy-done | bytes 1048600
  5.7 1.0 %copy-done.1 = bf16[1,1,12,128,128]{4,3,2,1,0:T(8,128)(2,1)S(1)} copy-done((bf16[1,1,12,128,128]{4,3,2,1,0:T(8,128)(2,1)S(1)}, bf16[1,1,12,128,128]{4,3,2,1,0:T(8,128)(2,1)}, u32[]{:S(2)}) %copy-start.1) | copy-done | bytes 393240
  6.7 0.3 staged.1
  7.1 0.5 %collective-permute-done.1.refs_2_ = bf16[1,16,128]{2,1,0:T(8,128)(2,1)S(1)} collective-permute-done((bf16[1,16,128]{2,1,0:T(8,128)(2,1)}, bf16[1,16,128]{2,1,0:T(8,128)(2,1)S(1)}, u32[]{:S(2)}, u32[]{:S(2)}) %collective-permute-start.1) | collective-permute-done | bytes 4128 | tf_op jit(solution)/shard_map/ppermute | solution.py:272
  7.6 1.5 %tile_products.1 = (f32[1,12,16,128]{3,2,1,0:T(8,128)S(1)}, f32[1,12,16,128]{3,2,1,0:T(8,128)S(1)}) custom-call(s32[32]{0:T(128)S(1)} %get-tuple-element.9.h_list_ref, s32[12]{0:T(128)S(1)} %get-tuple-element.10.j_list_ref, bf16[1,16,128]{2,1,0:T(8,128)(2,1)S(1)} %get-tuple-element.11.refs_0_, bf16[1,16,128]{2,1,0:T(8,128)(2,1)S(1)} %collective-permute-done.refs_1_, ...), custom_call_target="tpu_custom_call" | custom-call | tf_op jit(solution)/shard_map/tile_products/pallas_call | solution.py:138
  9.1 1.6 %collective-permute-start.3 = (f32[1,12,16,128]{3,2,1,0:T(8,128)S(1)}, f32[1,12,16,128]{3,2,1,0:T(8,128)S(1)}, u32[]{:S(2)}, u32[]{:S(2)}) collective-permute-start(f32[1,12,16,128]{3,2,1,0:T(8,128)S(1)} %get-tuple-element.15), channel_id=1, source_target_pairs={{0,1},{1,0},{2,3},{3,2},{4,5},{5,4},{6,7},{7,6},{8,9},{9,8},{10,11... | collective-permute-start | bytes 294920 | tf_op jit(solution)/shard_map/ppermute | solution.py:36
  10.7 3.1 %collective-permute-done.3 = f32[1,12,16,128]{3,2,1,0:T(8,128)S(1)} collective-permute-done((f32[1,12,16,128]{3,2,1,0:T(8,128)S(1)}, f32[1,12,16,128]{3,2,1,0:T(8,128)S(1)}, u32[]{:S(2)}, u32[]{:S(2)}) %collective-permute-start.3) | collective-permute-done | bytes 98336 | tf_op jit(solution)/shard_map/ppermute | solution.py:36
  13.8 1.6 %collective-permute-start.4 = (f32[1,12,16,128]{3,2,1,0:T(8,128)S(1)}, f32[1,12,16,128]{3,2,1,0:T(8,128)S(1)}, u32[]{:S(2)}, u32[]{:S(2)}) collective-permute-start(f32[1,12,16,128]{3,2,1,0:T(8,128)S(1)} %add.21), channel_id=1, source_target_pairs={{0,2},{1,3},{2,0},{3,1},{4,6},{5,7},{6,4},{7,5},{8,10},{9,11},{10,... | collective-permute-start | bytes 294920 | tf_op jit(solution)/shard_map/ppermute | solution.py:36
  15.5 3.0 %collective-permute-done.4 = f32[1,12,16,128]{3,2,1,0:T(8,128)S(1)} collective-permute-done((f32[1,12,16,128]{3,2,1,0:T(8,128)S(1)}, f32[1,12,16,128]{3,2,1,0:T(8,128)S(1)}, u32[]{:S(2)}, u32[]{:S(2)}) %collective-permute-start.4) | collective-permute-done | bytes 98336 | tf_op jit(solution)/shard_map/ppermute | solution.py:36
  18.5 2.7 %collective-permute-start.5 = (f32[1,12,16,128]{3,2,1,0:T(8,128)S(1)}, f32[1,12,16,128]{3,2,1,0:T(8,128)S(1)}, u32[]{:S(2)}, u32[]{:S(2)}) collective-permute-start(f32[1,12,16,128]{3,2,1,0:T(8,128)S(1)} %add.22), channel_id=1, source_target_pairs={{0,4},{1,5},{2,6},{3,7},{4,0},{5,1},{6,2},{7,3},{8,12},{9,13},{10,... | collective-permute-start | bytes 294920 | tf_op jit(solution)/shard_map/ppermute | solution.py:36
  21.2 2.9 %collective-permute-done.5 = f32[1,12,16,128]{3,2,1,0:T(8,128)S(1)} collective-permute-done((f32[1,12,16,128]{3,2,1,0:T(8,128)S(1)}, f32[1,12,16,128]{3,2,1,0:T(8,128)S(1)}, u32[]{:S(2)}, u32[]{:S(2)}) %collective-permute-start.5) | collective-permute-done | bytes 98336 | tf_op jit(solution)/shard_map/ppermute | solution.py:36
  24.1 0.3 gram_parts.1
  24.4 1.2 %collective-permute-done.6 = f32[1,16,128]{2,1,0:T(8,128)S(1)} collective-permute-done((f32[1,16,128]{2,1,0:T(8,128)S(1)}, f32[1,16,128]{2,1,0:T(8,128)S(1)}, u32[]{:S(2)}, u32[]{:S(2)}) %collective-permute-start.6) | collective-permute-done | bytes 8224 | tf_op jit(solution)/shard_map/ppermute | solution.py:36
  25.6 2.4 %collective-permute-start.9 = (f32[1,16,128]{2,1,0:T(8,128)S(1)}, f32[1,16,128]{2,1,0:T(8,128)S(1)}, u32[]{:S(2)}, u32[]{:S(2)}) collective-permute-start(f32[1,16,128]{2,1,0:T(8,128)S(1)} %add.24), channel_id=1, source_target_pairs={{0,17},{1,16},{2,19},{3,18},{4,21},{5,20},{6,23},{7,22},{8,25},{9,... | collective-permute-start | bytes 24584 | tf_op jit(solution)/shard_map/ppermute | solution.py:43
  28.0 0.6 %collective-permute-start.8 = (f32[1,16,128]{2,1,0:T(8,128)S(1)}, f32[1,16,128]{2,1,0:T(8,128)S(1)}, u32[]{:S(2)}, u32[]{:S(2)}) collective-permute-start(f32[1,16,128]{2,1,0:T(8,128)S(1)} %add.24), channel_id=1, source_target_pairs={{0,16},{1,17},{2,18},{3,19},{4,20},{5,21},{6,22},{7,23},{8,24},{9,... | collective-permute-start | bytes 24584 | tf_op jit(solution)/shard_map/ppermute | solution.py:43
  28.6 0.5 %collective-permute-start.7 = (f32[1,16,128]{2,1,0:T(8,128)S(1)}, f32[1,16,128]{2,1,0:T(8,128)S(1)}, u32[]{:S(2)}, u32[]{:S(2)}) collective-permute-start(f32[1,16,128]{2,1,0:T(8,128)S(1)} %add.24), channel_id=1, source_target_pairs={{0,1},{1,0},{2,3},{3,2},{4,5},{5,4},{6,7},{7,6},{8,9},{9,8},{10,11... | collective-permute-start | bytes 24584 | tf_op jit(solution)/shard_map/ppermute | solution.py:43
  29.1 1.1 %collective-permute-done.9 = f32[1,16,128]{2,1,0:T(8,128)S(1)} collective-permute-done((f32[1,16,128]{2,1,0:T(8,128)S(1)}, f32[1,16,128]{2,1,0:T(8,128)S(1)}, u32[]{:S(2)}, u32[]{:S(2)}) %collective-permute-start.9) | collective-permute-done | bytes 8224 | tf_op jit(solution)/shard_map/ppermute | solution.py:43
  30.1 1.5 %collective-permute-done.8 = f32[1,16,128]{2,1,0:T(8,128)S(1)} collective-permute-done((f32[1,16,128]{2,1,0:T(8,128)S(1)}, f32[1,16,128]{2,1,0:T(8,128)S(1)}, u32[]{:S(2)}, u32[]{:S(2)}) %collective-permute-start.8) | collective-permute-done | bytes 8224 | tf_op jit(solution)/shard_map/ppermute | solution.py:43
  31.6 0.6 %collective-permute-done.7 = f32[1,16,128]{2,1,0:T(8,128)S(1)} collective-permute-done((f32[1,16,128]{2,1,0:T(8,128)S(1)}, f32[1,16,128]{2,1,0:T(8,128)S(1)}, u32[]{:S(2)}, u32[]{:S(2)}) %collective-permute-start.7) | collective-permute-done | bytes 8224 | tf_op jit(solution)/shard_map/ppermute | solution.py:43
  32.2 1.7 %orthonormal.1 = (f32[1,16,128]{2,1,0:T(8,128)}, f32[1,2,16,16]{3,2,1,0:T(8,128)}) custom-call(f32[1,16,128]{2,1,0:T(8,128)S(1)} %add_add_fusion.gram_ref, f32[1,12,16,128]{3,2,1,0:T(8,128)S(1)} %add.23.x_ref), custom_call_target="tpu_custom_call" | custom-call | tf_op jit(solution)/shard_map/orthonormal/pallas_call | solution.py:234
  (15 shorter events, 0.1 us)
Async XLA Ops:
  0.6 3.2 %copy-start.2 = (bf16[1,16,128]{2,1,0:T(8,128)(2,1)S(1)}, bf16[1,16,128]{2,1,0:T(8,128)(2,1)}, u32[]{:S(2)}) copy-start(bf16[1,16,128]{2,1,0:T(8,128)(2,1)} %refs_0_.1) | copy-start | bytes 12292
  0.6 6.4 %collective-permute-start = (bf16[1,16,128]{2,1,0:T(8,128)(2,1)}, bf16[1,16,128]{2,1,0:T(8,128)(2,1)S(1)}, u32[]{:S(2)}, u32[]{:S(2)}) collective-permute-start(bf16[1,16,128]{2,1,0:T(8,128)(2,1)} %refs_0_.1), channel_id=1, source_target_pairs={{0,8},{8,0},{16,24},{24,16},{1,9},{9,1},{17,25},{25,17},{2,10},{10... | collective-permute-start | bytes 12296 | tf_op jit(solution)/shard_map/ppermute | solution.py:272
  1.2 5.9 %collective-permute-start.2 = (bf16[1,16,128]{2,1,0:T(8,128)(2,1)}, bf16[1,16,128]{2,1,0:T(8,128)(2,1)S(1)}, u32[]{:S(2)}, u32[]{:S(2)}) collective-permute-start(bf16[1,16,128]{2,1,0:T(8,128)(2,1)} %refs_0_.1), channel_id=1, source_target_pairs={{0,24},{8,16},{16,8},{24,0},{1,25},{9,17},{17,9},{25,1},{2,26},{10... | collective-permute-start | bytes 12296 | tf_op jit(solution)/shard_map/ppermute | solution.py:272
  3.8 3.8 %collective-permute-start.1 = (bf16[1,16,128]{2,1,0:T(8,128)(2,1)}, bf16[1,16,128]{2,1,0:T(8,128)(2,1)S(1)}, u32[]{:S(2)}, u32[]{:S(2)}) collective-permute-start(bf16[1,16,128]{2,1,0:T(8,128)(2,1)} %refs_0_.1), channel_id=1, source_target_pairs={{0,16},{8,24},{16,0},{24,8},{1,17},{9,25},{17,1},{25,9},{2,18},{10... | collective-permute-start | bytes 12296 | tf_op jit(solution)/shard_map/ppermute | solution.py:272
  3.8 0.7 %copy-start.3 = (s32[1,1,32]{2,1,0:T(1,128)S(1)}, s32[1,1,32]{2,1,0:T(1,128)}, u32[]{:S(2)}) copy-start(s32[1,1,32]{2,1,0:T(1,128)} %param.7) | copy-start | bytes 388
  3.8 0.7 %copy-start.4 = (s32[1,1,12]{2,1,0:T(1,128)S(1)}, s32[1,1,12]{2,1,0:T(1,128)}, u32[]{:S(2)}) copy-start(s32[1,1,12]{2,1,0:T(1,128)} %param.9) | copy-start | bytes 148
  4.5 1.2 %copy-start = (bf16[1,1,32,128,128]{4,3,2,1,0:T(8,128)(2,1)S(1)}, bf16[1,1,32,128,128]{4,3,2,1,0:T(8,128)(2,1)}, u32[]{:S(2)}) copy-start(bf16[1,1,32,128,128]{4,3,2,1,0:T(8,128)(2,1)} %param.6) | copy-start | bytes 3145732
  5.7 1.0 %copy-start.1 = (bf16[1,1,12,128,128]{4,3,2,1,0:T(8,128)(2,1)S(1)}, bf16[1,1,12,128,128]{4,3,2,1,0:T(8,128)(2,1)}, u32[]{:S(2)}) copy-start(bf16[1,1,12,128,128]{4,3,2,1,0:T(8,128)(2,1)} %param.8) | copy-start | bytes 1179652
  9.1 4.7 %collective-permute-start.3 = (f32[1,12,16,128]{3,2,1,0:T(8,128)S(1)}, f32[1,12,16,128]{3,2,1,0:T(8,128)S(1)}, u32[]{:S(2)}, u32[]{:S(2)}) collective-permute-start(f32[1,12,16,128]{3,2,1,0:T(8,128)S(1)} %get-tuple-element.15), channel_id=1, source_target_pairs={{0,1},{1,0},{2,3},{3,2},{4,5},{5,4},{6,7},{7,6},{8,9},{9,8},{10,11... | collective-permute-start | bytes 294920 | tf_op jit(solution)/shard_map/ppermute | solution.py:36
  13.8 4.7 %collective-permute-start.4 = (f32[1,12,16,128]{3,2,1,0:T(8,128)S(1)}, f32[1,12,16,128]{3,2,1,0:T(8,128)S(1)}, u32[]{:S(2)}, u32[]{:S(2)}) collective-permute-start(f32[1,12,16,128]{3,2,1,0:T(8,128)S(1)} %add.21), channel_id=1, source_target_pairs={{0,2},{1,3},{2,0},{3,1},{4,6},{5,7},{6,4},{7,5},{8,10},{9,11},{10,... | collective-permute-start | bytes 294920 | tf_op jit(solution)/shard_map/ppermute | solution.py:36
  18.5 5.6 %collective-permute-start.5 = (f32[1,12,16,128]{3,2,1,0:T(8,128)S(1)}, f32[1,12,16,128]{3,2,1,0:T(8,128)S(1)}, u32[]{:S(2)}, u32[]{:S(2)}) collective-permute-start(f32[1,12,16,128]{3,2,1,0:T(8,128)S(1)} %add.22), channel_id=1, source_target_pairs={{0,4},{1,5},{2,6},{3,7},{4,0},{5,1},{6,2},{7,3},{8,12},{9,13},{10,... | collective-permute-start | bytes 294920 | tf_op jit(solution)/shard_map/ppermute | solution.py:36
  24.4 1.2 %collective-permute-start.6 = (f32[1,16,128]{2,1,0:T(8,128)S(1)}, f32[1,16,128]{2,1,0:T(8,128)S(1)}, u32[]{:S(2)}, u32[]{:S(2)}) collective-permute-start(f32[1,16,128]{2,1,0:T(8,128)S(1)} %gram_parts.1), channel_id=1, source_target_pairs={{0,8},{8,0},{16,24},{24,16},{1,9},{9,1},{17,25},{25,17},{2,10},{10... | collective-permute-start | bytes 24584 | tf_op jit(solution)/shard_map/ppermute | solution.py:36
  25.6 4.5 %collective-permute-start.9 = (f32[1,16,128]{2,1,0:T(8,128)S(1)}, f32[1,16,128]{2,1,0:T(8,128)S(1)}, u32[]{:S(2)}, u32[]{:S(2)}) collective-permute-start(f32[1,16,128]{2,1,0:T(8,128)S(1)} %add.24), channel_id=1, source_target_pairs={{0,17},{1,16},{2,19},{3,18},{4,21},{5,20},{6,23},{7,22},{8,25},{9,... | collective-permute-start | bytes 24584 | tf_op jit(solution)/shard_map/ppermute | solution.py:43
  28.0 3.7 %collective-permute-start.8 = (f32[1,16,128]{2,1,0:T(8,128)S(1)}, f32[1,16,128]{2,1,0:T(8,128)S(1)}, u32[]{:S(2)}, u32[]{:S(2)}) collective-permute-start(f32[1,16,128]{2,1,0:T(8,128)S(1)} %add.24), channel_id=1, source_target_pairs={{0,16},{1,17},{2,18},{3,19},{4,20},{5,21},{6,22},{7,23},{8,24},{9,... | collective-permute-start | bytes 24584 | tf_op jit(solution)/shard_map/ppermute | solution.py:43
  28.6 3.7 %collective-permute-start.7 = (f32[1,16,128]{2,1,0:T(8,128)S(1)}, f32[1,16,128]{2,1,0:T(8,128)S(1)}, u32[]{:S(2)}, u32[]{:S(2)}) collective-permute-start(f32[1,16,128]{2,1,0:T(8,128)S(1)} %add.24), channel_id=1, source_target_pairs={{0,1},{1,0},{2,3},{3,2},{4,5},{5,4},{6,7},{7,6},{8,9},{9,8},{10,11... | collective-permute-start | bytes 24584 | tf_op jit(solution)/shard_map/ppermute | solution.py:43

commit v3 on v2

--- a/solution.py
+++ b/solution.py
@@ -11,6 +11,7 @@
 NSIT = 6
 J_OPERATORS = 2
 LANES = 128
+COVER_FLOPS = 4 << 30
 
 exact_precision = lax.Precision.HIGHEST
 
@@ -55,98 +56,118 @@
     return None
 
 
-def stage_kernel(count, *refs):
-    sources, targets, arrived = refs[:count], refs[count : 2 * count], refs[2 * count]
-    copies = [
-        pltpu.make_async_copy(source, target, arrived.at[n])
-        for n, (source, target) in enumerate(zip(sources, targets))
-    ]
-    for copy in copies:
-        copy.start()
-    for copy in copies:
-        copy.wait()
-
-
-def staged(*arrays):
+def quotient(x, divisor, limit):
+    if divisor & (divisor - 1) == 0:
+        return lax.shift_right_logical(x, divisor.bit_length() - 1)
+    marks = range(divisor, limit, divisor)
+    return sum((jnp.where(x >= mark, 1, 0) for mark in marks), jnp.zeros_like(x))
+
+
+def spot_kernel(layout, h_list_ref, j_list_ref, spot_ref):
+    column_tiles, row_tiles, group, halves, stride, pieces, bits = layout
+    operators = J_OPERATORS + 1
+    positions = row_tiles * column_tiles
+    place = lax.axis_index("col") // stride % halves
+    turn = lax.axis_index("row")
+    start = 0
+    for list_ref, first in ((h_list_ref, 0), (j_list_ref, 1)):
+        code = list_ref[...]
+        spot = jnp.maximum(code, 0)
+        strip = quotient(spot, column_tiles, J_OPERATORS * positions)
+        column = spot - strip * column_tiles
+        if pieces > 1:
+            column = column ^ turn
+        operator = quotient(strip, row_tiles, J_OPERATORS * row_tiles)
+        row = strip - operator * row_tiles
+        chunk = quotient(row, group, row_tiles)
+        outer = quotient(chunk, halves, row_tiles)
+        local = outer * group + row - chunk * group
+        side = jnp.where(chunk - outer * halves == place, 0, row_tiles // halves * operators)
+        at = side + local * operators + operator + first
+        at = jnp.where(code >= 0, at, row_tiles * operators)
+        slots = code.shape[1]
+        spot_ref[:, start : start + slots] = lax.shift_left(at, bits) + column
+        start += slots
+
+
+def spots(h_list, j_list, layout):
+    vmem = pl.BlockSpec(memory_space=pltpu.VMEM)
     return pl.pallas_call(
-        functools.partial(stage_kernel, len(arrays)),
-        out_shape=[jax.ShapeDtypeStruct(a.shape, a.dtype) for a in arrays],
-        in_specs=[pl.BlockSpec(memory_space=pltpu.HBM)] * len(arrays),
-        out_specs=[pl.BlockSpec(memory_space=pltpu.VMEM)] * len(arrays),
-        scratch_shapes=[pltpu.SemaphoreType.DMA((len(arrays),))],
-        compiler_params=pltpu.CompilerParams(vmem_limit_bytes=8 << 20),
-        cost_estimate=pl.CostEstimate(
-            flops=0, transcendentals=0, bytes_accessed=sum(a.size * a.dtype.itemsize for a in arrays)
-        ),
-        name="staged",
-    )(*arrays)
-
-
-def product_kernel(layout, h_list_ref, j_list_ref, *refs):
-    column_tiles, row_tiles, group, halves, stride, pieces = layout
-    vector_refs, (h_ref, j_ref), outs = refs[:pieces], refs[pieces : pieces + 2], refs[pieces + 2 : -2]
-    picked, total = refs[-2:]
-    kept_tiles = row_tiles // halves
-    tile = h_ref.shape[-1]
+        functools.partial(spot_kernel, layout),
+        out_shape=jax.ShapeDtypeStruct((h_list.shape[0], LANES), jnp.int32),
+        in_specs=[vmem, vmem],
+        out_specs=vmem,
+        compiler_params=pltpu.CompilerParams(vmem_limit_bytes=1 << 20),
+        cost_estimate=pl.CostEstimate(flops=COVER_FLOPS, transcendentals=0, bytes_accessed=1 << 12),
+        name="spots",
+    )(h_list, j_list)
+
+
+def product_kernel(layout, spot_ref, *refs):
+    column_tiles, row_tiles, group, halves, stride, pieces, bits = layout
+    vector_refs, (h_ref, j_ref), outs = refs[:pieces], refs[pieces : pieces + 2], refs[pieces + 2 : -5]
+    held, products, total, spot, arrived = refs[-5:]
+    fetch = pltpu.make_async_copy(spot_ref, spot, arrived)
+    fetch.start()
+    sectors, vectors, tile = held.shape[0], vector_refs[0].shape[1], h_ref.shape[-1]
     each = column_tiles // pieces
+    wide = column_tiles * vectors
+    held[...] = jnp.zeros_like(held)
     for n, vector_ref in enumerate(vector_refs):
         for t in range(each):
-            picked[:, n * each + t] = vector_ref[:, :, t * tile : (t + 1) * tile]
+            at = (n * each + t) * vectors
+            for side in range(2):
+                held[:, side * wide + at : side * wide + at + vectors, side * tile : (side + 1) * tile] = (
+                    vector_ref[:, :, t * tile : (t + 1) * tile]
+                )
     total[...] = jnp.zeros_like(total)
-    place = lax.axis_index("col") // stride % halves
-    turn = lax.axis_index("row")
-    for s in range(total.shape[0]):
-        for tiles, codes in ((h_ref, h_list_ref), (j_ref, j_list_ref)):
-            slots = tiles.shape[1]
-            for q in range(slots):
-                code = codes[s * slots + q]
-                spot = jnp.maximum(code, 0)
-                strip = spot // column_tiles
-                column = spot - strip * column_tiles
-                if pieces > 1:
-                    column = column ^ turn
-                operator = strip // row_tiles
-                row = strip - operator * row_tiles
-                if tiles is j_ref:
-                    operator = operator + 1
-                half = row // group % halves
-                local = row // (group * halves) * group + row % group
-                half = jnp.where(half == place, 0, 1) if halves > 1 else 0
-                at = (half * kept_tiles + local) * (J_OPERATORS + 1) + operator
-                at = jnp.where(code >= 0, at, row_tiles * (J_OPERATORS + 1))
-                product = lax.dot_general(
-                    picked[s, column],
-                    tiles[s, q],
-                    (((1,), (1,)), ((), ())),
-                    preferred_element_type=jnp.float32,
-                )
-                total[s, at] += product
-    count = kept_tiles * (J_OPERATORS + 1)
+    slots = [(tiles, q) for tiles in (h_ref, j_ref) for q in range(tiles.shape[1])]
+    for s in range(sectors):
+        for n in range(0, len(slots), 4):
+            some = [tiles[s, q] for tiles, q in slots[n : n + 4]]
+            pairs = [jnp.concatenate([some[i], some[(i + 1) % len(some)]], 1) for i in range(0, len(some), 2)]
+            product = lax.dot_general(
+                held[s], jnp.concatenate(pairs, 0), (((1,), (1,)), ((), ())), preferred_element_type=jnp.float32
+            )
+            for i in range(len(some)):
+                side, column = i % 2, i // 2
+                part = product[side * wide : (side + 1) * wide, column * tile : (column + 1) * tile]
+                products[s, n + i] = part.reshape(column_tiles, vectors, tile)
+    fetch.wait()
+    for s in range(sectors):
+        for n in range(len(slots)):
+            word = spot[s, n]
+            at = lax.shift_right_logical(word, bits)
+            total[s, at] += products[s, n, word & ((1 << bits) - 1)]
+    count = row_tiles // halves * (J_OPERATORS + 1)
     for half, out in enumerate(outs):
         out[...] = total[:, half * count : (half + 1) * count]
 
 
-def tile_products(h_list, j_list, vectors, h_tiles, j_tiles, layout):
-    column_tiles, row_tiles, group, halves, stride, pieces = layout
+def tile_products(where, vectors, h_tiles, j_tiles, layout):
+    column_tiles, row_tiles, group, halves, stride, pieces, bits = layout
     sectors, count_vectors = vectors[0].shape[:2]
     tile = h_tiles.shape[-1]
+    slots = h_tiles.shape[1] + j_tiles.shape[1]
     count = row_tiles // halves * (J_OPERATORS + 1)
-    smem = pl.BlockSpec(memory_space=pltpu.SMEM)
     vmem = pl.BlockSpec(memory_space=pltpu.VMEM)
     shape = jax.ShapeDtypeStruct((sectors, count, count_vectors, tile), jnp.float32)
     extended = (sectors, row_tiles * (J_OPERATORS + 1) + 1, count_vectors, tile)
     return pl.pallas_call(
         functools.partial(product_kernel, layout),
         out_shape=[shape] * halves,
-        in_specs=[smem] * 2 + [vmem] * (pieces + 2),
+        in_specs=[pl.BlockSpec(memory_space=pl.ANY)] + [vmem] * (pieces + 2),
         out_specs=[vmem] * halves,
         scratch_shapes=[
-            pltpu.VMEM((sectors, column_tiles, count_vectors, tile), jnp.bfloat16),
+            pltpu.VMEM((sectors, 2 * column_tiles * count_vectors, 2 * tile), jnp.bfloat16),
+            pltpu.VMEM((sectors, slots, column_tiles, count_vectors, tile), jnp.float32),
             pltpu.VMEM(extended, jnp.float32),
+            pltpu.SMEM(where.shape, jnp.int32),
+            pltpu.SemaphoreType.DMA,
         ],
         compiler_params=pltpu.CompilerParams(vmem_limit_bytes=8 << 20),
         name="tile_products",
-    )(h_list, j_list, *vectors, h_tiles, j_tiles)
+    )(where, *vectors, h_tiles, j_tiles)
 
 
 def gram_kernel(x_ref, out_ref):
@@ -259,22 +280,21 @@
     stride = 1 if digit is None else digit[0]
     direct = piece == tile and n_row in (2, 4)
 
-    own_vectors, h_codes, j_codes, h_held, j_held = staged(
-        vectors,
-        h_list.reshape(-1),
-        j_list.reshape(-1),
-        h_tiles.reshape(sectors, -1, tile, tile),
-        j_tiles.reshape(sectors, -1, tile, tile),
-    )
     if direct:
-        parts = [own_vectors]
+        parts = [vectors]
         for mask in range(1, n_row):
             parts.append(lax.ppermute(vectors, "row", [(i, i ^ mask) for i in range(n_row)]))
     else:
         parts = [lax.all_gather(vectors, "row", axis=2, tiled=True)]
+    bits = (column_tiles - 1).bit_length()
+    layout = (column_tiles, row_tiles, group, halves, stride, len(parts), bits)
+    where = spots(h_list.reshape(sectors, -1), j_list.reshape(sectors, -1), layout)
     outs = tile_products(
-        h_codes, j_codes, parts, h_held, j_held,
-        (column_tiles, row_tiles, group, halves, stride, len(parts)),
+        where,
+        parts,
+        h_tiles.reshape(sectors, -1, tile, tile),
+        j_tiles.reshape(sectors, -1, tile, tile),
+        layout,
     )
     x = outs[0]
     if digit is not None:
@@ -285,8 +305,8 @@
 
     gram = gram_parts(x)
     if direct and n_row == 4 and digit is not None:
-        gram = summed(gram, "row", (1, 2))
-        gram = gram + across(gram, 0, digit[0]) + across(gram, 2, 0) + across(gram, 2, digit[0])
+        gram = gram + across(gram, 1, 0) + across(gram, 2, 0) + across(gram, 3, 0)
+        gram = gram + across(gram, 0, digit[0])
     else:
         for other in digits_of(n_row):
             gram = summed(gram, "row", other)

time: 34.1 us -> 33.1 us (0.971)
  local copies, waits for them, and re-layouts: 2.89 us -> 0.68 us
  waiting for transfers between devices: 14 us -> 15.9 us
  Pallas kernels: 3.75 us -> 3.14 us
    unnamed x10, local copies, waits for them, and re-layouts: 2.89 us -> 0.68 us
    ppermute x3, waiting for transfers between devices: 0.55 us -> 2.29 us  [per_device(): lax.ppermute(vectors, 'row', [(i, i ^ mask) for i in range(n_row)])]
    ppermute x3 -> x4, waiting for transfers between devices: 3.14 us -> 3.93 us  [across(): return lax.ppermute(x, ('row', 'col'), moves)]
    ppermute x4 -> x3, waiting for transfers between devices: 10.3 us -> 9.69 us  [sent(): lax.ppermute(x, axis, [(i, moved(i, digit, shift)) for i in range(size)])]
    pallas_call x1, Pallas kernels: 1.52 us -> 1.13 us  [tile_products(): pl.pallas_call(functools.partial(product_kernel, layout), out_shape=[shap...]
    ppermute x4 -> x3, starting transfers between devices: 5.88 us -> 5.84 us  [sent(): lax.ppermute(x, axis, [(i, moved(i, digit, shift)) for i in range(size)])]
    ppermute x3 -> x4, starting transfers between devices: 3.49 us -> 3.48 us  [across(): return lax.ppermute(x, ('row', 'col'), moves)]
  transfers between devices with their start and end apart: 10 -> 10, of which waited for: 8 -> 8; matrix products, arithmetic and copies ran while one was open for 0% -> 0% of each run, Pallas kernels for 1% -> 0%
where the time goes in v3:
time: 33.1 us; the launch traced here: 33 us
  waiting for transfers between devices  15.9 us (48%)
  starting transfers between devices  12.6 us (38%)
  Pallas kernels  3.14 us (9%)
  local copies, waits for them, and re-layouts  0.68 us (2%)
  between operations  0.67 us (2%)
    ppermute x3, waiting for transfers between devices, sent(): lax.ppermute(x, axis, [(i, moved(i, digit, shift)) for i in range(size)])  9.69 us
    ppermute x3, starting transfers between devices, sent(): lax.ppermute(x, axis, [(i, moved(i, digit, shift)) for i in range(size)])  5.84 us
    ppermute x4, waiting for transfers between devices, across(): return lax.ppermute(x, ('row', 'col'), moves)  3.93 us
    ppermute x4, starting transfers between devices, across(): return lax.ppermute(x, ('row', 'col'), moves)  3.48 us
    ppermute x3, starting transfers between devices, per_device(): lax.ppermute(vectors, 'row', [(i, i ^ mask) for i in range(n_row)])  3.22 us
    ppermute x3, waiting for transfers between devices, per_device(): lax.ppermute(vectors, 'row', [(i, i ^ mask) for i in range(n_row)])  2.29 us
    pallas_call x1, Pallas kernels, orthonormal(): pl.pallas_call(functools.partial(root_kernel, layout), out_shape=[jax.Sha...  1.67 us
    pallas_call x1, Pallas kernels, tile_products(): pl.pallas_call(functools.partial(product_kernel, layout), out_shape=[shap...  1.13 us
  transfers between devices with their start and end apart: 10, of which 8 were waited for; matrix products, arithmetic and copies ran while one was open for 0% of the time, Pallas kernels for 0%

profile of v3, /device:TPU:0, one launch (start us, length us, event | category | flops | bytes accessed | tf_op | source)
XLA Modules:
  0.0 33.0 jit_solution(12980514708206304134)
XLA Ops:
  0.6 3.0 %collective-permute-start.1 = (bf16[1,16,128]{2,1,0:T(8,128)(2,1)}, bf16[1,16,128]{2,1,0:T(8,128)(2,1)S(1)}, u32[]{:S(2)}, u32[]{:S(2)}) collective-permute-start(bf16[1,16,128]{2,1,0:T(8,128)(2,1)} %refs_0_.1), channel_id=1, source_target_pairs={{0,16},{8,24},{16,0},{24,8},{1,17},{9,25},{17,1},{25,9},{2,18},{10... | collective-permute-start | bytes 12296 | tf_op jit(solution)/shard_map/ppermute | solution.py:286
  3.7 0.0 collective-permute-start
  3.7 0.2 collective-permute-start.2
  3.9 0.7 %copy-done.3 = s32[1,1,32]{2,1,0:T(1,128)S(1)} copy-done((s32[1,1,32]{2,1,0:T(1,128)S(1)}, s32[1,1,32]{2,1,0:T(1,128)}, u32[]{:S(2)}) %copy-start.3) | copy-done | bytes 152
  4.5 0.0 copy-done.4
  4.5 0.1 spots.1.spot_ref
  4.6 0.8 %collective-permute-done.1.refs_2_ = bf16[1,16,128]{2,1,0:T(8,128)(2,1)S(1)} collective-permute-done((bf16[1,16,128]{2,1,0:T(8,128)(2,1)}, bf16[1,16,128]{2,1,0:T(8,128)(2,1)S(1)}, u32[]{:S(2)}, u32[]{:S(2)}) %collective-permute-start.1) | collective-permute-done | bytes 4128 | tf_op jit(solution)/shard_map/ppermute | solution.py:286
  5.5 0.0 collective-permute-done.refs_1_
  5.5 1.4 %collective-permute-done.2.refs_3_ = bf16[1,16,128]{2,1,0:T(8,128)(2,1)S(1)} collective-permute-done((bf16[1,16,128]{2,1,0:T(8,128)(2,1)}, bf16[1,16,128]{2,1,0:T(8,128)(2,1)S(1)}, u32[]{:S(2)}, u32[]{:S(2)}) %collective-permute-start.2) | collective-permute-done | bytes 4128 | tf_op jit(solution)/shard_map/ppermute | solution.py:286
  6.9 1.1 %tile_products.1 = (f32[1,12,16,128]{3,2,1,0:T(8,128)S(1)}, f32[1,12,16,128]{3,2,1,0:T(8,128)S(1)}) custom-call(s32[1,128]{1,0:T(1,128)S(1)} %spots.1.spot_ref, bf16[1,16,128]{2,1,0:T(8,128)(2,1)S(1)} %copy-done.2, bf16[1,16,128]{2,1,0:T(8,128)(2,1)S(1)} %collective-permute-done.refs_1_, bf16[1,16,128]{2,1,0:T(8,128)(2,1)S(1)} %collective-permute-done.1.refs_2_, ...), custom_call_target="tpu_custom_call" | custom-call | tf_op jit(solution)/shard_map/tile_products/pallas_call | solution.py:156
  8.1 1.6 %collective-permute-start.3 = (f32[1,12,16,128]{3,2,1,0:T(8,128)S(1)}, f32[1,12,16,128]{3,2,1,0:T(8,128)S(1)}, u32[]{:S(2)}, u32[]{:S(2)}) collective-permute-start(f32[1,12,16,128]{3,2,1,0:T(8,128)S(1)} %get-tuple-element.5), channel_id=1, source_target_pairs={{0,1},{1,0},{2,3},{3,2},{4,5},{5,4},{6,7},{7,6},{8,9},{9,8},{10,11... | collective-permute-start | bytes 294920 | tf_op jit(solution)/shard_map/ppermute | solution.py:37
  9.6 3.7 %collective-permute-done.3 = f32[1,12,16,128]{3,2,1,0:T(8,128)S(1)} collective-permute-done((f32[1,12,16,128]{3,2,1,0:T(8,128)S(1)}, f32[1,12,16,128]{3,2,1,0:T(8,128)S(1)}, u32[]{:S(2)}, u32[]{:S(2)}) %collective-permute-start.3) | collective-permute-done | bytes 98336 | tf_op jit(solution)/shard_map/ppermute | solution.py:37
  13.3 1.6 %collective-permute-start.4 = (f32[1,12,16,128]{3,2,1,0:T(8,128)S(1)}, f32[1,12,16,128]{3,2,1,0:T(8,128)S(1)}, u32[]{:S(2)}, u32[]{:S(2)}) collective-permute-start(f32[1,12,16,128]{3,2,1,0:T(8,128)S(1)} %add.21), channel_id=1, source_target_pairs={{0,2},{1,3},{2,0},{3,1},{4,6},{5,7},{6,4},{7,5},{8,10},{9,11},{10,... | collective-permute-start | bytes 294920 | tf_op jit(solution)/shard_map/ppermute | solution.py:37
  15.0 3.0 %collective-permute-done.4 = f32[1,12,16,128]{3,2,1,0:T(8,128)S(1)} collective-permute-done((f32[1,12,16,128]{3,2,1,0:T(8,128)S(1)}, f32[1,12,16,128]{3,2,1,0:T(8,128)S(1)}, u32[]{:S(2)}, u32[]{:S(2)}) %collective-permute-start.4) | collective-permute-done | bytes 98336 | tf_op jit(solution)/shard_map/ppermute | solution.py:37
  18.0 2.6 %collective-permute-start.5 = (f32[1,12,16,128]{3,2,1,0:T(8,128)S(1)}, f32[1,12,16,128]{3,2,1,0:T(8,128)S(1)}, u32[]{:S(2)}, u32[]{:S(2)}) collective-permute-start(f32[1,12,16,128]{3,2,1,0:T(8,128)S(1)} %add.22), channel_id=1, source_target_pairs={{0,4},{1,5},{2,6},{3,7},{4,0},{5,1},{6,2},{7,3},{8,12},{9,13},{10,... | collective-permute-start | bytes 294920 | tf_op jit(solution)/shard_map/ppermute | solution.py:37
  20.7 3.0 %collective-permute-done.5 = f32[1,12,16,128]{3,2,1,0:T(8,128)S(1)} collective-permute-done((f32[1,12,16,128]{3,2,1,0:T(8,128)S(1)}, f32[1,12,16,128]{3,2,1,0:T(8,128)S(1)}, u32[]{:S(2)}, u32[]{:S(2)}) %collective-permute-start.5) | collective-permute-done | bytes 98336 | tf_op jit(solution)/shard_map/ppermute | solution.py:37
  23.6 0.3 gram_parts.1
  23.9 0.3 %collective-permute-start.7 = (f32[1,16,128]{2,1,0:T(8,128)S(1)}, f32[1,16,128]{2,1,0:T(8,128)S(1)}, u32[]{:S(2)}, u32[]{:S(2)}) collective-permute-start(f32[1,16,128]{2,1,0:T(8,128)S(1)} %gram_parts.1), channel_id=1, source_target_pairs={{0,16},{1,17},{2,18},{3,19},{4,20},{5,21},{6,22},{7,23},{8,24},{9,... | collective-permute-start | bytes 24584 | tf_op jit(solution)/shard_map/ppermute | solution.py:44
  24.2 1.5 %collective-permute-start.6 = (f32[1,16,128]{2,1,0:T(8,128)S(1)}, f32[1,16,128]{2,1,0:T(8,128)S(1)}, u32[]{:S(2)}, u32[]{:S(2)}) collective-permute-start(f32[1,16,128]{2,1,0:T(8,128)S(1)} %gram_parts.1), channel_id=1, source_target_pairs={{0,8},{1,9},{2,10},{3,11},{4,12},{5,13},{6,14},{7,15},{8,0},{9,1},... | collective-permute-start | bytes 24584 | tf_op jit(solution)/shard_map/ppermute | solution.py:44
  25.8 1.2 %collective-permute-done.8 = f32[1,16,128]{2,1,0:T(8,128)S(1)} collective-permute-done((f32[1,16,128]{2,1,0:T(8,128)S(1)}, f32[1,16,128]{2,1,0:T(8,128)S(1)}, u32[]{:S(2)}, u32[]{:S(2)}) %collective-permute-start.8) | collective-permute-done | bytes 8224 | tf_op jit(solution)/shard_map/ppermute | solution.py:44
  27.0 0.6 %collective-permute-done.7 = f32[1,16,128]{2,1,0:T(8,128)S(1)} collective-permute-done((f32[1,16,128]{2,1,0:T(8,128)S(1)}, f32[1,16,128]{2,1,0:T(8,128)S(1)}, u32[]{:S(2)}, u32[]{:S(2)}) %collective-permute-start.7) | collective-permute-done | bytes 8224 | tf_op jit(solution)/shard_map/ppermute | solution.py:44
  27.6 1.6 %collective-permute-start.9 = (f32[1,16,128]{2,1,0:T(8,128)S(1)}, f32[1,16,128]{2,1,0:T(8,128)S(1)}, u32[]{:S(2)}, u32[]{:S(2)}) collective-permute-start(f32[1,16,128]{2,1,0:T(8,128)S(1)} %add_add_fusion), channel_id=1, source_target_pairs={{0,1},{1,0},{2,3},{3,2},{4,5},{5,4},{6,7},{7,6},{8,9},{9,8},{10,11... | collective-permute-start | bytes 24584 | tf_op jit(solution)/shard_map/ppermute | solution.py:44
  29.2 2.1 %collective-permute-done.9 = f32[1,16,128]{2,1,0:T(8,128)S(1)} collective-permute-done((f32[1,16,128]{2,1,0:T(8,128)S(1)}, f32[1,16,128]{2,1,0:T(8,128)S(1)}, u32[]{:S(2)}, u32[]{:S(2)}) %collective-permute-start.9) | collective-permute-done | bytes 8224 | tf_op jit(solution)/shard_map/ppermute | solution.py:44
  31.3 1.7 %orthonormal.1 = (f32[1,16,128]{2,1,0:T(8,128)}, f32[1,2,16,16]{3,2,1,0:T(8,128)}) custom-call(f32[1,16,128]{2,1,0:T(8,128)S(1)} %add.27.gram_ref, f32[1,12,16,128]{3,2,1,0:T(8,128)S(1)} %add.23.x_ref), custom_call_target="tpu_custom_call" | custom-call | tf_op jit(solution)/shard_map/orthonormal/pallas_call | solution.py:255
  (15 shorter events, 0.1 us)
Async XLA Ops:
  0.6 4.8 %collective-permute-start.1 = (bf16[1,16,128]{2,1,0:T(8,128)(2,1)}, bf16[1,16,128]{2,1,0:T(8,128)(2,1)S(1)}, u32[]{:S(2)}, u32[]{:S(2)}) collective-permute-start(bf16[1,16,128]{2,1,0:T(8,128)(2,1)} %refs_0_.1), channel_id=1, source_target_pairs={{0,16},{8,24},{16,0},{24,8},{1,17},{9,25},{17,1},{25,9},{2,18},{10... | collective-permute-start | bytes 12296 | tf_op jit(solution)/shard_map/ppermute | solution.py:286
  3.7 1.8 %collective-permute-start = (bf16[1,16,128]{2,1,0:T(8,128)(2,1)}, bf16[1,16,128]{2,1,0:T(8,128)(2,1)S(1)}, u32[]{:S(2)}, u32[]{:S(2)}) collective-permute-start(bf16[1,16,128]{2,1,0:T(8,128)(2,1)} %refs_0_.1), channel_id=1, source_target_pairs={{0,8},{8,0},{16,24},{24,16},{1,9},{9,1},{17,25},{25,17},{2,10},{10... | collective-permute-start | bytes 12296 | tf_op jit(solution)/shard_map/ppermute | solution.py:286
  3.7 3.2 %collective-permute-start.2 = (bf16[1,16,128]{2,1,0:T(8,128)(2,1)}, bf16[1,16,128]{2,1,0:T(8,128)(2,1)S(1)}, u32[]{:S(2)}, u32[]{:S(2)}) collective-permute-start(bf16[1,16,128]{2,1,0:T(8,128)(2,1)} %refs_0_.1), channel_id=1, source_target_pairs={{0,24},{8,16},{16,8},{24,0},{1,25},{9,17},{17,9},{25,1},{2,26},{10... | collective-permute-start | bytes 12296 | tf_op jit(solution)/shard_map/ppermute | solution.py:286
  3.9 0.7 %copy-start.3 = (s32[1,1,32]{2,1,0:T(1,128)S(1)}, s32[1,1,32]{2,1,0:T(1,128)}, u32[]{:S(2)}) copy-start(s32[1,1,32]{2,1,0:T(1,128)} %param.7) | copy-start | bytes 388
  3.9 0.7 %copy-start.4 = (s32[1,1,12]{2,1,0:T(1,128)S(1)}, s32[1,1,12]{2,1,0:T(1,128)}, u32[]{:S(2)}) copy-start(s32[1,1,12]{2,1,0:T(1,128)} %param.9) | copy-start | bytes 148
  4.5 2.4 %copy-start = (bf16[1,1,32,128,128]{4,3,2,1,0:T(8,128)(2,1)S(1)}, bf16[1,1,32,128,128]{4,3,2,1,0:T(8,128)(2,1)}, u32[]{:S(2)}) copy-start(bf16[1,1,32,128,128]{4,3,2,1,0:T(8,128)(2,1)} %param.6) | copy-start | bytes 3145732
  4.5 2.4 %copy-start.1 = (bf16[1,1,12,128,128]{4,3,2,1,0:T(8,128)(2,1)S(1)}, bf16[1,1,12,128,128]{4,3,2,1,0:T(8,128)(2,1)}, u32[]{:S(2)}) copy-start(bf16[1,1,12,128,128]{4,3,2,1,0:T(8,128)(2,1)} %param.8) | copy-start | bytes 1179652
  4.5 2.4 %copy-start.2 = (bf16[1,16,128]{2,1,0:T(8,128)(2,1)S(1)}, bf16[1,16,128]{2,1,0:T(8,128)(2,1)}, u32[]{:S(2)}) copy-start(bf16[1,16,128]{2,1,0:T(8,128)(2,1)} %refs_0_.1) | copy-start | bytes 12292
  8.1 5.3 %collective-permute-start.3 = (f32[1,12,16,128]{3,2,1,0:T(8,128)S(1)}, f32[1,12,16,128]{3,2,1,0:T(8,128)S(1)}, u32[]{:S(2)}, u32[]{:S(2)}) collective-permute-start(f32[1,12,16,128]{3,2,1,0:T(8,128)S(1)} %get-tuple-element.5), channel_id=1, source_target_pairs={{0,1},{1,0},{2,3},{3,2},{4,5},{5,4},{6,7},{7,6},{8,9},{9,8},{10,11... | collective-permute-start | bytes 294920 | tf_op jit(solution)/shard_map/ppermute | solution.py:37
  13.3 4.7 %collective-permute-start.4 = (f32[1,12,16,128]{3,2,1,0:T(8,128)S(1)}, f32[1,12,16,128]{3,2,1,0:T(8,128)S(1)}, u32[]{:S(2)}, u32[]{:S(2)}) collective-permute-start(f32[1,12,16,128]{3,2,1,0:T(8,128)S(1)} %add.21), channel_id=1, source_target_pairs={{0,2},{1,3},{2,0},{3,1},{4,6},{5,7},{6,4},{7,5},{8,10},{9,11},{10,... | collective-permute-start | bytes 294920 | tf_op jit(solution)/shard_map/ppermute | solution.py:37
  18.0 5.6 %collective-permute-start.5 = (f32[1,12,16,128]{3,2,1,0:T(8,128)S(1)}, f32[1,12,16,128]{3,2,1,0:T(8,128)S(1)}, u32[]{:S(2)}, u32[]{:S(2)}) collective-permute-start(f32[1,12,16,128]{3,2,1,0:T(8,128)S(1)} %add.22), channel_id=1, source_target_pairs={{0,4},{1,5},{2,6},{3,7},{4,0},{5,1},{6,2},{7,3},{8,12},{9,13},{10,... | collective-permute-start | bytes 294920 | tf_op jit(solution)/shard_map/ppermute | solution.py:37
  23.9 3.1 %collective-permute-start.8 = (f32[1,16,128]{2,1,0:T(8,128)S(1)}, f32[1,16,128]{2,1,0:T(8,128)S(1)}, u32[]{:S(2)}, u32[]{:S(2)}) collective-permute-start(f32[1,16,128]{2,1,0:T(8,128)S(1)} %gram_parts.1), channel_id=1, source_target_pairs={{0,24},{1,25},{2,26},{3,27},{4,28},{5,29},{6,30},{7,31},{8,16},{9,... | collective-permute-start | bytes 24584 | tf_op jit(solution)/shard_map/ppermute | solution.py:44
  23.9 3.7 %collective-permute-start.7 = (f32[1,16,128]{2,1,0:T(8,128)S(1)}, f32[1,16,128]{2,1,0:T(8,128)S(1)}, u32[]{:S(2)}, u32[]{:S(2)}) collective-permute-start(f32[1,16,128]{2,1,0:T(8,128)S(1)} %gram_parts.1), channel_id=1, source_target_pairs={{0,16},{1,17},{2,18},{3,19},{4,20},{5,21},{6,22},{7,23},{8,24},{9,... | collective-permute-start | bytes 24584 | tf_op jit(solution)/shard_map/ppermute | solution.py:44
  24.2 3.4 %collective-permute-start.6 = (f32[1,16,128]{2,1,0:T(8,128)S(1)}, f32[1,16,128]{2,1,0:T(8,128)S(1)}, u32[]{:S(2)}, u32[]{:S(2)}) collective-permute-start(f32[1,16,128]{2,1,0:T(8,128)S(1)} %gram_parts.1), channel_id=1, source_target_pairs={{0,8},{1,9},{2,10},{3,11},{4,12},{5,13},{6,14},{7,15},{8,0},{9,1},... | collective-permute-start | bytes 24584 | tf_op jit(solution)/shard_map/ppermute | solution.py:44
  27.6 3.7 %collective-permute-start.9 = (f32[1,16,128]{2,1,0:T(8,128)S(1)}, f32[1,16,128]{2,1,0:T(8,128)S(1)}, u32[]{:S(2)}, u32[]{:S(2)}) collective-permute-start(f32[1,16,128]{2,1,0:T(8,128)S(1)} %add_add_fusion), channel_id=1, source_target_pairs={{0,1},{1,0},{2,3},{3,2},{4,5},{5,4},{6,7},{7,6},{8,9},{9,8},{10,11... | collective-permute-start | bytes 24584 | tf_op jit(solution)/shard_map/ppermute | solution.py:44

commit v4 on v3

--- a/solution.py
+++ b/solution.py
@@ -11,6 +11,7 @@
 NSIT = 6
 J_OPERATORS = 2
 LANES = 128
+H_CHAINS = 3
 COVER_FLOPS = 4 << 30
 
 exact_precision = lax.Precision.HIGHEST
@@ -65,12 +66,11 @@
 
 def spot_kernel(layout, h_list_ref, j_list_ref, spot_ref):
     column_tiles, row_tiles, group, halves, stride, pieces, bits = layout
-    operators = J_OPERATORS + 1
     positions = row_tiles * column_tiles
     place = lax.axis_index("col") // stride % halves
     turn = lax.axis_index("row")
     start = 0
-    for list_ref, first in ((h_list_ref, 0), (j_list_ref, 1)):
+    for list_ref, count in ((h_list_ref, 1), (j_list_ref, J_OPERATORS)):
         code = list_ref[...]
         spot = jnp.maximum(code, 0)
         strip = quotient(spot, column_tiles, J_OPERATORS * positions)
@@ -82,9 +82,8 @@
         chunk = quotient(row, group, row_tiles)
         outer = quotient(chunk, halves, row_tiles)
         local = outer * group + row - chunk * group
-        side = jnp.where(chunk - outer * halves == place, 0, row_tiles // halves * operators)
-        at = side + local * operators + operator + first
-        at = jnp.where(code >= 0, at, row_tiles * operators)
+        strips = jnp.where(chunk - outer * halves == place, 0, row_tiles // halves) + local
+        at = jnp.where(code >= 0, strips * count + operator, row_tiles * count)
         slots = code.shape[1]
         spot_ref[:, start : start + slots] = lax.shift_left(at, bits) + column
         start += slots
@@ -103,10 +102,34 @@
     )(h_list, j_list)
 
 
+def turn_kernel(*refs):
+    count = len(refs) // 2
+    for source, target in zip(refs[:count], refs[count:]):
+        for s in range(source.shape[0]):
+            for q in range(source.shape[1]):
+                target[s, q] = source[s, q].T
+
+
+def turned(*arrays):
+    vmem = pl.BlockSpec(memory_space=pltpu.VMEM)
+    return pl.pallas_call(
+        turn_kernel,
+        out_shape=[jax.ShapeDtypeStruct(a.shape, a.dtype) for a in arrays],
+        in_specs=[vmem] * len(arrays),
+        out_specs=[vmem] * len(arrays),
+        compiler_params=pltpu.CompilerParams(vmem_limit_bytes=4 << 20),
+        cost_estimate=pl.CostEstimate(
+            flops=0, transcendentals=0, bytes_accessed=2 * sum(a.size * a.dtype.itemsize for a in arrays)
+        ),
+        name="turned",
+    )(*arrays)
+
+
 def product_kernel(layout, spot_ref, *refs):
     column_tiles, row_tiles, group, halves, stride, pieces, bits = layout
-    vector_refs, (h_ref, j_ref), outs = refs[:pieces], refs[pieces : pieces + 2], refs[pieces + 2 : -5]
-    held, products, total, spot, arrived = refs[-5:]
+    vector_refs, (h_ref, j_ref), outs = refs[:pieces], refs[pieces : pieces + 2], refs[pieces + 2 : pieces + 2 + halves]
+    held, products, spot, arrived = refs[pieces + 2 + halves : pieces + 6 + halves]
+    totals = refs[pieces + 6 + halves :]
     fetch = pltpu.make_async_copy(spot_ref, spot, arrived)
     fetch.start()
     sectors, vectors, tile = held.shape[0], vector_refs[0].shape[1], h_ref.shape[-1]
@@ -120,28 +143,39 @@
                 held[:, side * wide + at : side * wide + at + vectors, side * tile : (side + 1) * tile] = (
                     vector_ref[:, :, t * tile : (t + 1) * tile]
                 )
-    total[...] = jnp.zeros_like(total)
+    for total in totals:
+        total[...] = jnp.zeros_like(total)
     slots = [(tiles, q) for tiles in (h_ref, j_ref) for q in range(tiles.shape[1])]
     for s in range(sectors):
         for n in range(0, len(slots), 4):
             some = [tiles[s, q] for tiles, q in slots[n : n + 4]]
-            pairs = [jnp.concatenate([some[i], some[(i + 1) % len(some)]], 1) for i in range(0, len(some), 2)]
-            product = lax.dot_general(
-                held[s], jnp.concatenate(pairs, 0), (((1,), (1,)), ((), ())), preferred_element_type=jnp.float32
+            pairs = [jnp.concatenate([some[i], some[(i + 1) % len(some)]], 0) for i in range(0, len(some), 2)]
+            product = jnp.dot(
+                held[s], jnp.concatenate(pairs, 1), preferred_element_type=jnp.float32
             )
             for i in range(len(some)):
                 side, column = i % 2, i // 2
                 part = product[side * wide : (side + 1) * wide, column * tile : (column + 1) * tile]
                 products[s, n + i] = part.reshape(column_tiles, vectors, tile)
     fetch.wait()
+    chains = len(totals) - 1
+    h_slots = h_ref.shape[1]
+    order = [(n // chains, totals[n % chains], n) for n in range(h_slots)]
+    order += [(n - h_slots, totals[-1], n) for n in range(h_slots, len(slots))]
+    order.sort(key=lambda entry: entry[0])
+    kept_tiles = row_tiles // halves
     for s in range(sectors):
-        for n in range(len(slots)):
+        for _, total, n in order:
             word = spot[s, n]
             at = lax.shift_right_logical(word, bits)
             total[s, at] += products[s, n, word & ((1 << bits) - 1)]
-    count = row_tiles // halves * (J_OPERATORS + 1)
-    for half, out in enumerate(outs):
-        out[...] = total[:, half * count : (half + 1) * count]
+        for half, out in enumerate(outs):
+            for t in range(kept_tiles):
+                strip = half * kept_tiles + t
+                first = t * (J_OPERATORS + 1)
+                out[s, first] = functools.reduce(jnp.add, [total[s, strip] for total in totals[:-1]])
+                for a in range(J_OPERATORS):
+                    out[s, first + 1 + a] = totals[-1][s, strip * J_OPERATORS + a]
 
 
 def tile_products(where, vectors, h_tiles, j_tiles, layout):
@@ -152,7 +186,8 @@
     count = row_tiles // halves * (J_OPERATORS + 1)
     vmem = pl.BlockSpec(memory_space=pltpu.VMEM)
     shape = jax.ShapeDtypeStruct((sectors, count, count_vectors, tile), jnp.float32)
-    extended = (sectors, row_tiles * (J_OPERATORS + 1) + 1, count_vectors, tile)
+    h_total = (sectors, row_tiles + 1, count_vectors, tile)
+    j_total = (sectors, row_tiles * J_OPERATORS + 1, count_vectors, tile)
     return pl.pallas_call(
         functools.partial(product_kernel, layout),
         out_shape=[shape] * halves,
@@ -161,10 +196,11 @@
         scratch_shapes=[
             pltpu.VMEM((sectors, 2 * column_tiles * count_vectors, 2 * tile), jnp.bfloat16),
             pltpu.VMEM((sectors, slots, column_tiles, count_vectors, tile), jnp.float32),
-            pltpu.VMEM(extended, jnp.float32),
             pltpu.SMEM(where.shape, jnp.int32),
             pltpu.SemaphoreType.DMA,
-        ],
+        ]
+        + [pltpu.VMEM(h_total, jnp.float32)] * H_CHAINS
+        + [pltpu.VMEM(j_total, jnp.float32)],
         compiler_params=pltpu.CompilerParams(vmem_limit_bytes=8 << 20),
         name="tile_products",
     )(where, *vectors, h_tiles, j_tiles)
@@ -289,13 +325,10 @@
     bits = (column_tiles - 1).bit_length()
     layout = (column_tiles, row_tiles, group, halves, stride, len(parts), bits)
     where = spots(h_list.reshape(sectors, -1), j_list.reshape(sectors, -1), layout)
-    outs = tile_products(
-        where,
-        parts,
-        h_tiles.reshape(sectors, -1, tile, tile),
-        j_tiles.reshape(sectors, -1, tile, tile),
-        layout,
+    h_turned, j_turned = turned(
+        h_tiles.reshape(sectors, -1, tile, tile), j_tiles.reshape(sectors, -1, tile, tile)
     )
+    outs = tile_products(where, parts, h_turned, j_turned, layout)
     x = outs[0]
     if digit is not None:
         x = x + sent(outs[1], "col", digit, 1)

time: 33.1 us -> 32.7 us (0.988)
  waiting for transfers between devices: 15.9 us -> 14.2 us
  local copies, waits for them, and re-layouts: 0.68 us -> 1.9 us
    ppermute x3, waiting for transfers between devices: 2.29 us -> 0.62 us  [per_device(): lax.ppermute(vectors, 'row', [(i, i ^ mask) for i in range(n_row)])]
    unnamed x10, local copies, waits for them, and re-layouts: 0.68 us -> 1.9 us
    pallas_call x1, Pallas kernels: 1.13 us -> 0.66 us  [tile_products(): pl.pallas_call(functools.partial(product_kernel, layout), out_shape=[shap...]
    pallas_call x0 -> x1, Pallas kernels: none -> 0.42 us  [turned(): pl.pallas_call(turn_kernel, out_shape=[jax.ShapeDtypeStruct(a.shape, a.dt...]
  transfers between devices with their start and end apart: 10 -> 10, of which waited for: 8 -> 7; matrix products, arithmetic and copies ran while one was open for 0% -> 0% of each run, Pallas kernels for 0% -> 2%
where the time goes in v4:
time: 32.7 us; the launch traced here: 32.5 us
  waiting for transfers between devices  14.2 us (43%)
  starting transfers between devices  12.6 us (39%)
  Pallas kernels  3.08 us (9%)
  local copies, waits for them, and re-layouts  1.9 us (6%)
  between operations  0.69 us (2%)
    ppermute x3, waiting for transfers between devices, sent(): lax.ppermute(x, axis, [(i, moved(i, digit, shift)) for i in range(size)])  9.6 us
    ppermute x3, starting transfers between devices, sent(): lax.ppermute(x, axis, [(i, moved(i, digit, shift)) for i in range(size)])  5.95 us
    ppermute x4, waiting for transfers between devices, across(): return lax.ppermute(x, ('row', 'col'), moves)  3.95 us
    ppermute x4, starting transfers between devices, across(): return lax.ppermute(x, ('row', 'col'), moves)  3.47 us
    ppermute x3, starting transfers between devices, per_device(): lax.ppermute(vectors, 'row', [(i, i ^ mask) for i in range(n_row)])  3.23 us
    unnamed x10, local copies, waits for them, and re-layouts  1.9 us
    pallas_call x1, Pallas kernels, orthonormal(): pl.pallas_call(functools.partial(root_kernel, layout), out_shape=[jax.Sha...  1.67 us
    pallas_call x1, Pallas kernels, tile_products(): pl.pallas_call(functools.partial(product_kernel, layout), out_shape=[shap...  0.66 us
  transfers between devices with their start and end apart: 10, of which 7 were waited for; matrix products, arithmetic and copies ran while one was open for 0% of the time, Pallas kernels for 2%

profile of v4, /device:TPU:0, one launch (start us, length us, event | category | flops | bytes accessed | tf_op | source)
XLA Modules:
  0.0 32.5 jit_solution(4407799877232186446)
XLA Ops:
  0.6 3.0 %collective-permute-start.1 = (bf16[1,16,128]{2,1,0:T(8,128)(2,1)}, bf16[1,16,128]{2,1,0:T(8,128)(2,1)S(1)}, u32[]{:S(2)}, u32[]{:S(2)}) collective-permute-start(bf16[1,16,128]{2,1,0:T(8,128)(2,1)} %refs_0_.1), channel_id=1, source_target_pairs={{0,16},{8,24},{16,0},{24,8},{1,17},{9,25},{17,1},{25,9},{2,18},{10... | collective-permute-start | bytes 12296 | tf_op jit(solution)/shard_map/ppermute | solution.py:322
  3.7 0.2 collective-permute-start.2
  3.9 0.7 %copy-done.3 = s32[1,1,32]{2,1,0:T(1,128)S(1)} copy-done((s32[1,1,32]{2,1,0:T(1,128)S(1)}, s32[1,1,32]{2,1,0:T(1,128)}, u32[]{:S(2)}) %copy-start.3) | copy-done | bytes 152
  4.5 0.0 copy-done.4
  4.5 0.1 spots.1.spot_ref
  4.6 1.1 %copy-done = bf16[1,1,32,128,128]{4,3,2,1,0:T(8,128)(2,1)S(1)} copy-done((bf16[1,1,32,128,128]{4,3,2,1,0:T(8,128)(2,1)S(1)}, bf16[1,1,32,128,128]{4,3,2,1,0:T(8,128)(2,1)}, u32[]{:S(2)}) %copy-start) | copy-done | bytes 1048600
  5.8 0.1 copy-done.1
  5.8 0.4 %turned.1 = (bf16[1,32,128,128]{3,2,1,0:T(8,128)(2,1)S(1)}, bf16[1,12,128,128]{3,2,1,0:T(8,128)(2,1)S(1)}) custom-call(bf16[1,32,128,128]{3,2,1,0:T(8,128)(2,1)S(1)} %bitcast.4, bf16[1,12,128,128]{3,2,1,0:T(8,128)(2,1)S(1)} %bitcast.5), custom_call_target="tpu_custom_call" | custom-call | bytes 2883584 | tf_op jit(solution)/shard_map/turned/pallas_call | solution.py:115
  6.3 0.6 %collective-permute-done.2.refs_3_ = bf16[1,16,128]{2,1,0:T(8,128)(2,1)S(1)} collective-permute-done((bf16[1,16,128]{2,1,0:T(8,128)(2,1)}, bf16[1,16,128]{2,1,0:T(8,128)(2,1)S(1)}, u32[]{:S(2)}, u32[]{:S(2)}) %collective-permute-start.2) | collective-permute-done | bytes 4128 | tf_op jit(solution)/shard_map/ppermute | solution.py:322
  6.9 0.7 %tile_products.1 = (f32[1,12,16,128]{3,2,1,0:T(8,128)S(1)}, f32[1,12,16,128]{3,2,1,0:T(8,128)S(1)}) custom-call(s32[1,128]{1,0:T(1,128)S(1)} %spots.1.spot_ref, bf16[1,16,128]{2,1,0:T(8,128)(2,1)S(1)} %copy-done.2, bf16[1,16,128]{2,1,0:T(8,128)(2,1)S(1)} %collective-permute-done.refs_1_, bf16[1,16,128]{2,1,0:T(8,128)(2,1)S(1)} %collective-permute-done.1.refs_2_, ...), custom_call_target="tpu_custom_call" | custom-call | tf_op jit(solution)/shard_map/tile_products/pallas_call | solution.py:191
  7.6 1.7 %collective-permute-start.3 = (f32[1,12,16,128]{3,2,1,0:T(8,128)S(1)}, f32[1,12,16,128]{3,2,1,0:T(8,128)S(1)}, u32[]{:S(2)}, u32[]{:S(2)}) collective-permute-start(f32[1,12,16,128]{3,2,1,0:T(8,128)S(1)} %get-tuple-element.9), channel_id=1, source_target_pairs={{0,1},{1,0},{2,3},{3,2},{4,5},{5,4},{6,7},{7,6},{8,9},{9,8},{10,11... | collective-permute-start | bytes 294920 | tf_op jit(solution)/shard_map/ppermute | solution.py:38
  9.2 3.6 %collective-permute-done.3 = f32[1,12,16,128]{3,2,1,0:T(8,128)S(1)} collective-permute-done((f32[1,12,16,128]{3,2,1,0:T(8,128)S(1)}, f32[1,12,16,128]{3,2,1,0:T(8,128)S(1)}, u32[]{:S(2)}, u32[]{:S(2)}) %collective-permute-start.3) | collective-permute-done | bytes 98336 | tf_op jit(solution)/shard_map/ppermute | solution.py:38
  12.9 1.6 %collective-permute-start.4 = (f32[1,12,16,128]{3,2,1,0:T(8,128)S(1)}, f32[1,12,16,128]{3,2,1,0:T(8,128)S(1)}, u32[]{:S(2)}, u32[]{:S(2)}) collective-permute-start(f32[1,12,16,128]{3,2,1,0:T(8,128)S(1)} %add.21), channel_id=1, source_target_pairs={{0,2},{1,3},{2,0},{3,1},{4,6},{5,7},{6,4},{7,5},{8,10},{9,11},{10,... | collective-permute-start | bytes 294920 | tf_op jit(solution)/shard_map/ppermute | solution.py:38
  14.5 3.0 %collective-permute-done.4 = f32[1,12,16,128]{3,2,1,0:T(8,128)S(1)} collective-permute-done((f32[1,12,16,128]{3,2,1,0:T(8,128)S(1)}, f32[1,12,16,128]{3,2,1,0:T(8,128)S(1)}, u32[]{:S(2)}, u32[]{:S(2)}) %collective-permute-start.4) | collective-permute-done | bytes 98336 | tf_op jit(solution)/shard_map/ppermute | solution.py:38
  17.6 2.7 %collective-permute-start.5 = (f32[1,12,16,128]{3,2,1,0:T(8,128)S(1)}, f32[1,12,16,128]{3,2,1,0:T(8,128)S(1)}, u32[]{:S(2)}, u32[]{:S(2)}) collective-permute-start(f32[1,12,16,128]{3,2,1,0:T(8,128)S(1)} %add.22), channel_id=1, source_target_pairs={{0,4},{1,5},{2,6},{3,7},{4,0},{5,1},{6,2},{7,3},{8,12},{9,13},{10,... | collective-permute-start | bytes 294920 | tf_op jit(solution)/shard_map/ppermute | solution.py:38
  20.2 2.9 %collective-permute-done.5 = f32[1,12,16,128]{3,2,1,0:T(8,128)S(1)} collective-permute-done((f32[1,12,16,128]{3,2,1,0:T(8,128)S(1)}, f32[1,12,16,128]{3,2,1,0:T(8,128)S(1)}, u32[]{:S(2)}, u32[]{:S(2)}) %collective-permute-start.5) | collective-permute-done | bytes 98336 | tf_op jit(solution)/shard_map/ppermute | solution.py:38
  23.2 0.3 gram_parts.1
  23.4 1.1 %collective-permute-start.7 = (f32[1,16,128]{2,1,0:T(8,128)S(1)}, f32[1,16,128]{2,1,0:T(8,128)S(1)}, u32[]{:S(2)}, u32[]{:S(2)}) collective-permute-start(f32[1,16,128]{2,1,0:T(8,128)S(1)} %gram_parts.1), channel_id=1, source_target_pairs={{0,16},{1,17},{2,18},{3,19},{4,20},{5,21},{6,22},{7,23},{8,24},{9,... | collective-permute-start | bytes 24584 | tf_op jit(solution)/shard_map/ppermute | solution.py:45
  24.5 0.8 %collective-permute-start.6 = (f32[1,16,128]{2,1,0:T(8,128)S(1)}, f32[1,16,128]{2,1,0:T(8,128)S(1)}, u32[]{:S(2)}, u32[]{:S(2)}) collective-permute-start(f32[1,16,128]{2,1,0:T(8,128)S(1)} %gram_parts.1), channel_id=1, source_target_pairs={{0,8},{1,9},{2,10},{3,11},{4,12},{5,13},{6,14},{7,15},{8,0},{9,1},... | collective-permute-start | bytes 24584 | tf_op jit(solution)/shard_map/ppermute | solution.py:45
  25.3 1.2 %collective-permute-done.8 = f32[1,16,128]{2,1,0:T(8,128)S(1)} collective-permute-done((f32[1,16,128]{2,1,0:T(8,128)S(1)}, f32[1,16,128]{2,1,0:T(8,128)S(1)}, u32[]{:S(2)}, u32[]{:S(2)}) %collective-permute-start.8) | collective-permute-done | bytes 8224 | tf_op jit(solution)/shard_map/ppermute | solution.py:45
  26.5 0.6 %collective-permute-done.7 = f32[1,16,128]{2,1,0:T(8,128)S(1)} collective-permute-done((f32[1,16,128]{2,1,0:T(8,128)S(1)}, f32[1,16,128]{2,1,0:T(8,128)S(1)}, u32[]{:S(2)}, u32[]{:S(2)}) %collective-permute-start.7) | collective-permute-done | bytes 8224 | tf_op jit(solution)/shard_map/ppermute | solution.py:45
  27.1 1.6 %collective-permute-start.9 = (f32[1,16,128]{2,1,0:T(8,128)S(1)}, f32[1,16,128]{2,1,0:T(8,128)S(1)}, u32[]{:S(2)}, u32[]{:S(2)}) collective-permute-start(f32[1,16,128]{2,1,0:T(8,128)S(1)} %add_add_fusion), channel_id=1, source_target_pairs={{0,1},{1,0},{2,3},{3,2},{4,5},{5,4},{6,7},{7,6},{8,9},{9,8},{10,11... | collective-permute-start | bytes 24584 | tf_op jit(solution)/shard_map/ppermute | solution.py:45
  28.7 2.1 %collective-permute-done.9 = f32[1,16,128]{2,1,0:T(8,128)S(1)} collective-permute-done((f32[1,16,128]{2,1,0:T(8,128)S(1)}, f32[1,16,128]{2,1,0:T(8,128)S(1)}, u32[]{:S(2)}, u32[]{:S(2)}) %collective-permute-start.9) | collective-permute-done | bytes 8224 | tf_op jit(solution)/shard_map/ppermute | solution.py:45
  30.9 1.7 %orthonormal.1 = (f32[1,16,128]{2,1,0:T(8,128)}, f32[1,2,16,16]{3,2,1,0:T(8,128)}) custom-call(f32[1,16,128]{2,1,0:T(8,128)S(1)} %add.27.gram_ref, f32[1,12,16,128]{3,2,1,0:T(8,128)S(1)} %add.23.x_ref), custom_call_target="tpu_custom_call" | custom-call | tf_op jit(solution)/shard_map/orthonormal/pallas_call | solution.py:291
  (16 shorter events, 0.1 us)
Async XLA Ops:
  0.6 5.6 %collective-permute-start.1 = (bf16[1,16,128]{2,1,0:T(8,128)(2,1)}, bf16[1,16,128]{2,1,0:T(8,128)(2,1)S(1)}, u32[]{:S(2)}, u32[]{:S(2)}) collective-permute-start(bf16[1,16,128]{2,1,0:T(8,128)(2,1)} %refs_0_.1), channel_id=1, source_target_pairs={{0,16},{8,24},{16,0},{24,8},{1,17},{9,25},{17,1},{25,9},{2,18},{10... | collective-permute-start | bytes 12296 | tf_op jit(solution)/shard_map/ppermute | solution.py:322
  3.7 2.6 %collective-permute-start = (bf16[1,16,128]{2,1,0:T(8,128)(2,1)}, bf16[1,16,128]{2,1,0:T(8,128)(2,1)S(1)}, u32[]{:S(2)}, u32[]{:S(2)}) collective-permute-start(bf16[1,16,128]{2,1,0:T(8,128)(2,1)} %refs_0_.1), channel_id=1, source_target_pairs={{0,8},{8,0},{16,24},{24,16},{1,9},{9,1},{17,25},{25,17},{2,10},{10... | collective-permute-start | bytes 12296 | tf_op jit(solution)/shard_map/ppermute | solution.py:322
  3.7 3.2 %collective-permute-start.2 = (bf16[1,16,128]{2,1,0:T(8,128)(2,1)}, bf16[1,16,128]{2,1,0:T(8,128)(2,1)S(1)}, u32[]{:S(2)}, u32[]{:S(2)}) collective-permute-start(bf16[1,16,128]{2,1,0:T(8,128)(2,1)} %refs_0_.1), channel_id=1, source_target_pairs={{0,24},{8,16},{16,8},{24,0},{1,25},{9,17},{17,9},{25,1},{2,26},{10... | collective-permute-start | bytes 12296 | tf_op jit(solution)/shard_map/ppermute | solution.py:322
  3.9 0.7 %copy-start.3 = (s32[1,1,32]{2,1,0:T(1,128)S(1)}, s32[1,1,32]{2,1,0:T(1,128)}, u32[]{:S(2)}) copy-start(s32[1,1,32]{2,1,0:T(1,128)} %param.7) | copy-start | bytes 388
  3.9 0.7 %copy-start.4 = (s32[1,1,12]{2,1,0:T(1,128)S(1)}, s32[1,1,12]{2,1,0:T(1,128)}, u32[]{:S(2)}) copy-start(s32[1,1,12]{2,1,0:T(1,128)} %param.9) | copy-start | bytes 148
  4.5 1.2 %copy-start = (bf16[1,1,32,128,128]{4,3,2,1,0:T(8,128)(2,1)S(1)}, bf16[1,1,32,128,128]{4,3,2,1,0:T(8,128)(2,1)}, u32[]{:S(2)}) copy-start(bf16[1,1,32,128,128]{4,3,2,1,0:T(8,128)(2,1)} %param.6) | copy-start | bytes 3145732
  4.5 1.3 %copy-start.1 = (bf16[1,1,12,128,128]{4,3,2,1,0:T(8,128)(2,1)S(1)}, bf16[1,1,12,128,128]{4,3,2,1,0:T(8,128)(2,1)}, u32[]{:S(2)}) copy-start(bf16[1,1,12,128,128]{4,3,2,1,0:T(8,128)(2,1)} %param.8) | copy-start | bytes 1179652
  5.8 1.1 %copy-start.2 = (bf16[1,16,128]{2,1,0:T(8,128)(2,1)S(1)}, bf16[1,16,128]{2,1,0:T(8,128)(2,1)}, u32[]{:S(2)}) copy-start(bf16[1,16,128]{2,1,0:T(8,128)(2,1)} %refs_0_.1) | copy-start | bytes 12292
  7.6 5.3 %collective-permute-start.3 = (f32[1,12,16,128]{3,2,1,0:T(8,128)S(1)}, f32[1,12,16,128]{3,2,1,0:T(8,128)S(1)}, u32[]{:S(2)}, u32[]{:S(2)}) collective-permute-start(f32[1,12,16,128]{3,2,1,0:T(8,128)S(1)} %get-tuple-element.9), channel_id=1, source_target_pairs={{0,1},{1,0},{2,3},{3,2},{4,5},{5,4},{6,7},{7,6},{8,9},{9,8},{10,11... | collective-permute-start | bytes 294920 | tf_op jit(solution)/shard_map/ppermute | solution.py:38
  12.9 4.7 %collective-permute-start.4 = (f32[1,12,16,128]{3,2,1,0:T(8,128)S(1)}, f32[1,12,16,128]{3,2,1,0:T(8,128)S(1)}, u32[]{:S(2)}, u32[]{:S(2)}) collective-permute-start(f32[1,12,16,128]{3,2,1,0:T(8,128)S(1)} %add.21), channel_id=1, source_target_pairs={{0,2},{1,3},{2,0},{3,1},{4,6},{5,7},{6,4},{7,5},{8,10},{9,11},{10,... | collective-permute-start | bytes 294920 | tf_op jit(solution)/shard_map/ppermute | solution.py:38
  17.6 5.6 %collective-permute-start.5 = (f32[1,12,16,128]{3,2,1,0:T(8,128)S(1)}, f32[1,12,16,128]{3,2,1,0:T(8,128)S(1)}, u32[]{:S(2)}, u32[]{:S(2)}) collective-permute-start(f32[1,12,16,128]{3,2,1,0:T(8,128)S(1)} %add.22), channel_id=1, source_target_pairs={{0,4},{1,5},{2,6},{3,7},{4,0},{5,1},{6,2},{7,3},{8,12},{9,13},{10,... | collective-permute-start | bytes 294920 | tf_op jit(solution)/shard_map/ppermute | solution.py:38
  23.4 3.1 %collective-permute-start.8 = (f32[1,16,128]{2,1,0:T(8,128)S(1)}, f32[1,16,128]{2,1,0:T(8,128)S(1)}, u32[]{:S(2)}, u32[]{:S(2)}) collective-permute-start(f32[1,16,128]{2,1,0:T(8,128)S(1)} %gram_parts.1), channel_id=1, source_target_pairs={{0,24},{1,25},{2,26},{3,27},{4,28},{5,29},{6,30},{7,31},{8,16},{9,... | collective-permute-start | bytes 24584 | tf_op jit(solution)/shard_map/ppermute | solution.py:45
  23.4 3.7 %collective-permute-start.7 = (f32[1,16,128]{2,1,0:T(8,128)S(1)}, f32[1,16,128]{2,1,0:T(8,128)S(1)}, u32[]{:S(2)}, u32[]{:S(2)}) collective-permute-start(f32[1,16,128]{2,1,0:T(8,128)S(1)} %gram_parts.1), channel_id=1, source_target_pairs={{0,16},{1,17},{2,18},{3,19},{4,20},{5,21},{6,22},{7,23},{8,24},{9,... | collective-permute-start | bytes 24584 | tf_op jit(solution)/shard_map/ppermute | solution.py:45
  24.5 2.6 %collective-permute-start.6 = (f32[1,16,128]{2,1,0:T(8,128)S(1)}, f32[1,16,128]{2,1,0:T(8,128)S(1)}, u32[]{:S(2)}, u32[]{:S(2)}) collective-permute-start(f32[1,16,128]{2,1,0:T(8,128)S(1)} %gram_parts.1), channel_id=1, source_target_pairs={{0,8},{1,9},{2,10},{3,11},{4,12},{5,13},{6,14},{7,15},{8,0},{9,1},... | collective-permute-start | bytes 24584 | tf_op jit(solution)/shard_map/ppermute | solution.py:45
  27.1 3.7 %collective-permute-start.9 = (f32[1,16,128]{2,1,0:T(8,128)S(1)}, f32[1,16,128]{2,1,0:T(8,128)S(1)}, u32[]{:S(2)}, u32[]{:S(2)}) collective-permute-start(f32[1,16,128]{2,1,0:T(8,128)S(1)} %add_add_fusion), channel_id=1, source_target_pairs={{0,1},{1,0},{2,3},{3,2},{4,5},{5,4},{6,7},{7,6},{8,9},{9,8},{10,11... | collective-permute-start | bytes 24584 | tf_op jit(solution)/shard_map/ppermute | solution.py:45

commit v5 on v3

--- a/solution.py
+++ b/solution.py
@@ -63,14 +63,17 @@
     return sum((jnp.where(x >= mark, 1, 0) for mark in marks), jnp.zeros_like(x))
 
 
-def spot_kernel(layout, h_list_ref, j_list_ref, spot_ref):
+def lead_kernel(place_ref):
+    place_ref[...] = jnp.full(place_ref.shape, lax.axis_index("row"), jnp.int32)
+
+
+def spot_kernel(layout, lead_ref, h_list_ref, j_list_ref, spot_ref):
     column_tiles, row_tiles, group, halves, stride, pieces, bits = layout
-    operators = J_OPERATORS + 1
     positions = row_tiles * column_tiles
     place = lax.axis_index("col") // stride % halves
-    turn = lax.axis_index("row")
+    turn = lead_ref[:1, :1]
     start = 0
-    for list_ref, first in ((h_list_ref, 0), (j_list_ref, 1)):
+    for list_ref, count in ((h_list_ref, 1), (j_list_ref, J_OPERATORS)):
         code = list_ref[...]
         spot = jnp.maximum(code, 0)
         strip = quotient(spot, column_tiles, J_OPERATORS * positions)
@@ -82,9 +85,8 @@
         chunk = quotient(row, group, row_tiles)
         outer = quotient(chunk, halves, row_tiles)
         local = outer * group + row - chunk * group
-        side = jnp.where(chunk - outer * halves == place, 0, row_tiles // halves * operators)
-        at = side + local * operators + operator + first
-        at = jnp.where(code >= 0, at, row_tiles * operators)
+        strips = jnp.where(chunk - outer * halves == place, 0, row_tiles // halves) + local
+        at = jnp.where(code >= 0, strips * count + operator, row_tiles * count)
         slots = code.shape[1]
         spot_ref[:, start : start + slots] = lax.shift_left(at, bits) + column
         start += slots
@@ -92,82 +94,95 @@
 
 def spots(h_list, j_list, layout):
     vmem = pl.BlockSpec(memory_space=pltpu.VMEM)
-    return pl.pallas_call(
-        functools.partial(spot_kernel, layout),
-        out_shape=jax.ShapeDtypeStruct((h_list.shape[0], LANES), jnp.int32),
-        in_specs=[vmem, vmem],
+    cover = pl.CostEstimate(flops=COVER_FLOPS, transcendentals=0, bytes_accessed=1 << 12)
+    lead = pl.pallas_call(
+        lead_kernel,
+        out_shape=jax.ShapeDtypeStruct((8, LANES), jnp.int32),
         out_specs=vmem,
         compiler_params=pltpu.CompilerParams(vmem_limit_bytes=1 << 20),
-        cost_estimate=pl.CostEstimate(flops=COVER_FLOPS, transcendentals=0, bytes_accessed=1 << 12),
+        cost_estimate=cover,
+        name="lead",
+    )()
+    return pl.pallas_call(
+        functools.partial(spot_kernel, layout),
+        out_shape=jax.ShapeDtypeStruct((h_list.shape[0], h_list.shape[1] + j_list.shape[1]), jnp.int32),
+        in_specs=[vmem] * 3,
+        out_specs=vmem,
+        compiler_params=pltpu.CompilerParams(vmem_limit_bytes=1 << 20),
+        cost_estimate=cover,
         name="spots",
-    )(h_list, j_list)
-
-
-def product_kernel(layout, spot_ref, *refs):
+    )(lead, h_list, j_list)
+
+
+def turn_kernel(layout, where_ref, h_ref, j_ref, h_block_ref, j_block_ref, spot, arrived):
+    bits = layout[-1]
+    fetch = pltpu.make_async_copy(where_ref, spot, arrived)
+    fetch.start()
+    h_block_ref[...] = jnp.zeros_like(h_block_ref)
+    j_block_ref[...] = jnp.zeros_like(j_block_ref)
+    fetch.wait()
+    sectors, h_slots = h_ref.shape[:2]
+    for s in range(sectors):
+        for tiles, block, first in ((h_ref, h_block_ref, 0), (j_ref, j_block_ref, h_slots)):
+            for q in range(tiles.shape[1]):
+                word = spot[s, first + q]
+                strip = lax.shift_right_logical(word, bits)
+                block[s, word & ((1 << bits) - 1), strip] = tiles[s, q].T
+
+
+def turned(where, h_tiles, j_tiles, layout):
+    column_tiles, row_tiles = layout[:2]
+    sectors, _, tile, _ = h_tiles.shape
+    vmem = pl.BlockSpec(memory_space=pltpu.VMEM)
+    shapes = [(sectors, column_tiles, row_tiles * n + 1, tile, tile) for n in (1, J_OPERATORS)]
+    moved_bytes = 4 * (h_tiles.size + j_tiles.size)
+    return pl.pallas_call(
+        functools.partial(turn_kernel, layout),
+        out_shape=[jax.ShapeDtypeStruct(shape, h_tiles.dtype) for shape in shapes],
+        in_specs=[pl.BlockSpec(memory_space=pl.ANY), vmem, vmem],
+        out_specs=[vmem, vmem],
+        scratch_shapes=[pltpu.SMEM(where.shape, jnp.int32), pltpu.SemaphoreType.DMA],
+        compiler_params=pltpu.CompilerParams(vmem_limit_bytes=4 << 20),
+        cost_estimate=pl.CostEstimate(flops=0, transcendentals=0, bytes_accessed=moved_bytes),
+        name="turned",
+    )(where, h_tiles, j_tiles)
+
+
+def product_kernel(layout, *refs):
     column_tiles, row_tiles, group, halves, stride, pieces, bits = layout
-    vector_refs, (h_ref, j_ref), outs = refs[:pieces], refs[pieces : pieces + 2], refs[pieces + 2 : -5]
-    held, products, total, spot, arrived = refs[-5:]
-    fetch = pltpu.make_async_copy(spot_ref, spot, arrived)
-    fetch.start()
-    sectors, vectors, tile = held.shape[0], vector_refs[0].shape[1], h_ref.shape[-1]
+    vector_refs, (h_block_ref, j_block_ref), outs = refs[:pieces], refs[pieces : pieces + 2], refs[pieces + 2 :]
+    kept_tiles, operators = row_tiles // halves, J_OPERATORS + 1
+    tile = h_block_ref.shape[-1]
     each = column_tiles // pieces
-    wide = column_tiles * vectors
-    held[...] = jnp.zeros_like(held)
-    for n, vector_ref in enumerate(vector_refs):
-        for t in range(each):
-            at = (n * each + t) * vectors
-            for side in range(2):
-                held[:, side * wide + at : side * wide + at + vectors, side * tile : (side + 1) * tile] = (
-                    vector_ref[:, :, t * tile : (t + 1) * tile]
-                )
-    total[...] = jnp.zeros_like(total)
-    slots = [(tiles, q) for tiles in (h_ref, j_ref) for q in range(tiles.shape[1])]
-    for s in range(sectors):
-        for n in range(0, len(slots), 4):
-            some = [tiles[s, q] for tiles, q in slots[n : n + 4]]
-            pairs = [jnp.concatenate([some[i], some[(i + 1) % len(some)]], 1) for i in range(0, len(some), 2)]
-            product = lax.dot_general(
-                held[s], jnp.concatenate(pairs, 0), (((1,), (1,)), ((), ())), preferred_element_type=jnp.float32
-            )
-            for i in range(len(some)):
-                side, column = i % 2, i // 2
-                part = product[side * wide : (side + 1) * wide, column * tile : (column + 1) * tile]
-                products[s, n + i] = part.reshape(column_tiles, vectors, tile)
-    fetch.wait()
-    for s in range(sectors):
-        for n in range(len(slots)):
-            word = spot[s, n]
-            at = lax.shift_right_logical(word, bits)
-            total[s, at] += products[s, n, word & ((1 << bits) - 1)]
-    count = row_tiles // halves * (J_OPERATORS + 1)
-    for half, out in enumerate(outs):
-        out[...] = total[:, half * count : (half + 1) * count]
-
-
-def tile_products(where, vectors, h_tiles, j_tiles, layout):
+    for s in range(outs[0].shape[0]):
+        lined = jnp.concatenate(
+            [vector_ref[s, :, t * tile : (t + 1) * tile] for vector_ref in vector_refs for t in range(each)], 1
+        )
+        for block_ref, first, count in ((j_block_ref, 1, J_OPERATORS), (h_block_ref, 0, 1)):
+            for strip in range(0, row_tiles * count, 2):
+                strips = range(strip, min(strip + 2, row_tiles * count))
+                block = [jnp.concatenate([block_ref[s, c, n] for n in strips], 1) for c in range(column_tiles)]
+                product = jnp.dot(lined, jnp.concatenate(block, 0), preferred_element_type=jnp.float32)
+                for i, n in enumerate(strips):
+                    t = n // count
+                    at = t % kept_tiles * operators + first + n % count
+                    outs[t // kept_tiles][s, at] = product[:, i * tile : (i + 1) * tile]
+
+
+def tile_products(vectors, h_block, j_block, layout):
     column_tiles, row_tiles, group, halves, stride, pieces, bits = layout
     sectors, count_vectors = vectors[0].shape[:2]
-    tile = h_tiles.shape[-1]
-    slots = h_tiles.shape[1] + j_tiles.shape[1]
     count = row_tiles // halves * (J_OPERATORS + 1)
     vmem = pl.BlockSpec(memory_space=pltpu.VMEM)
-    shape = jax.ShapeDtypeStruct((sectors, count, count_vectors, tile), jnp.float32)
-    extended = (sectors, row_tiles * (J_OPERATORS + 1) + 1, count_vectors, tile)
+    shape = jax.ShapeDtypeStruct((sectors, count, count_vectors, h_block.shape[-1]), jnp.float32)
     return pl.pallas_call(
         functools.partial(product_kernel, layout),
         out_shape=[shape] * halves,
-        in_specs=[pl.BlockSpec(memory_space=pl.ANY)] + [vmem] * (pieces + 2),
+        in_specs=[vmem] * (pieces + 2),
         out_specs=[vmem] * halves,
-        scratch_shapes=[
-            pltpu.VMEM((sectors, 2 * column_tiles * count_vectors, 2 * tile), jnp.bfloat16),
-            pltpu.VMEM((sectors, slots, column_tiles, count_vectors, tile), jnp.float32),
-            pltpu.VMEM(extended, jnp.float32),
-            pltpu.SMEM(where.shape, jnp.int32),
-            pltpu.SemaphoreType.DMA,
-        ],
-        compiler_params=pltpu.CompilerParams(vmem_limit_bytes=8 << 20),
+        compiler_params=pltpu.CompilerParams(vmem_limit_bytes=4 << 20),
         name="tile_products",
-    )(where, *vectors, h_tiles, j_tiles)
+    )(*vectors, h_block, j_block)
 
 
 def gram_kernel(x_ref, out_ref):
@@ -220,33 +235,34 @@
     vectors, tile = x_ref.shape[2:]
     operators = J_OPERATORS + 1
     shape = (vectors, LANES)
-    rows = lax.broadcasted_iota(jnp.int32, shape, 0)
     lanes = lax.broadcasted_iota(jnp.int32, shape, 1)
     is_gram = lanes < vectors
-    root_at = operators * vectors
-    step = jnp.where(lanes == rows, 1.5, 0.0).astype(jnp.float32)
+    ranks = lax.broadcasted_iota(jnp.int32, (vectors, 1), 0)
+    steps = [jnp.where(ranks == k, 1.5, 0.0).astype(jnp.float32) for k in range(vectors)]
     for s in range(x_ref.shape[0]):
         held = gram_ref[s]
+        columns = columns_of(held, 0, vectors, LANES)
         squares = jnp.where(is_gram, held * held, 0.0)
-        squares = jnp.sum(jnp.sum(squares, axis=1, keepdims=True), axis=0, keepdims=True)
+        squares = jnp.sum(jnp.sum(squares, axis=0, keepdims=True), axis=1, keepdims=True)
         scale = jnp.sqrt(squares + 1e-06)
         held = jnp.where(is_gram, held / scale, held)
-        held = jnp.where(lanes == rows + root_at, 1.0, held)
+        blocks = [x_ref[s, (own + t) * operators] for t in range(own_tiles)]
+        half = 0.5 / scale
         for iteration in range(NSIT):
-            middle = columns_of(step - 0.5 * held, 0, vectors, LANES)
+            middle = [step - half * column for step, column in zip(steps, columns)]
             once = product_of(middle, held)
+            blocks = [product_of(middle, block) for block in blocks]
             if iteration < NSIT - 1:
                 held = jnp.where(is_gram, product_of(middle, once), once)
+                columns, half = columns_of(held, 0, vectors, LANES), 0.5
             else:
                 held = once
-        held = held * jnp.sqrt(total_rows / scale)
-        root = columns_of(held, root_at, vectors, tile)
-        for t in range(own_tiles):
-            at = (own + t) * operators
-            basis_ref[s, :, t * tile : (t + 1) * tile] = product_of(root, x_ref[s, at])
+        factor = jnp.sqrt(total_rows / scale)
+        for t, block in enumerate(blocks):
+            basis_ref[s, :, t * tile : (t + 1) * tile] = block * factor
+        held = held * (factor / math.sqrt(total_rows))
         for a in range(J_OPERATORS):
-            elements = held[:, (a + 1) * vectors : (a + 2) * vectors]
-            elements_ref[s, a] = elements / math.sqrt(total_rows)
+            elements_ref[s, a] = held[:, (a + 1) * vectors : (a + 2) * vectors]
 
 
 def orthonormal(gram, x, layout):
@@ -289,13 +305,10 @@
     bits = (column_tiles - 1).bit_length()
     layout = (column_tiles, row_tiles, group, halves, stride, len(parts), bits)
     where = spots(h_list.reshape(sectors, -1), j_list.reshape(sectors, -1), layout)
-    outs = tile_products(
-        where,
-        parts,
-        h_tiles.reshape(sectors, -1, tile, tile),
-        j_tiles.reshape(sectors, -1, tile, tile),
-        layout,
+    h_block, j_block = turned(
+        where, h_tiles.reshape(sectors, -1, tile, tile), j_tiles.reshape(sectors, -1, tile, tile), layout
     )
+    outs = tile_products(parts, h_block, j_block, layout)
     x = outs[0]
     if digit is not None:
         x = x + sent(outs[1], "col", digit, 1)

time: 33.1 us -> 32.4 us (0.979)
  waiting for transfers between devices: 15.9 us -> 14.3 us
  local copies, waits for them, and re-layouts: 0.68 us -> 1.16 us
    ppermute x3, waiting for transfers between devices: 2.29 us -> 0.73 us  [per_device(): lax.ppermute(vectors, 'row', [(i, i ^ mask) for i in range(n_row)])]
    pallas_call x0 -> x2, Pallas kernels: none -> 0.98 us  [the longest x1 0.98 us: turned(): pl.pallas_call(functools.partial(turn_kernel, layout), out_shape=[jax.Sha...]
    pallas_call x1, Pallas kernels: 1.13 us -> 0.52 us  [tile_products(): pl.pallas_call(functools.partial(product_kernel, layout), out_shape=[shap...]
    unnamed x10, local copies, waits for them, and re-layouts: 0.68 us -> 1.16 us
  transfers between devices with their start and end apart: 10 -> 10, of which waited for: 8 -> 7; matrix products, arithmetic and copies ran while one was open for 0% -> 0% of each run, Pallas kernels for 0% -> 3%
where the time goes in v5:
time: 32.4 us; the launch traced here: 32.2 us
  waiting for transfers between devices  14.3 us (44%)
  starting transfers between devices  12.5 us (39%)
  Pallas kernels  3.44 us (11%)
  local copies, waits for them, and re-layouts  1.16 us (4%)
  between operations  0.72 us (2%)
    ppermute x3, waiting for transfers between devices, sent(): lax.ppermute(x, axis, [(i, moved(i, digit, shift)) for i in range(size)])  9.66 us
    ppermute x3, starting transfers between devices, sent(): lax.ppermute(x, axis, [(i, moved(i, digit, shift)) for i in range(size)])  5.82 us
    ppermute x4, waiting for transfers between devices, across(): return lax.ppermute(x, ('row', 'col'), moves)  3.95 us
    ppermute x4, starting transfers between devices, across(): return lax.ppermute(x, ('row', 'col'), moves)  3.47 us
    ppermute x3, starting transfers between devices, per_device(): lax.ppermute(vectors, 'row', [(i, i ^ mask) for i in range(n_row)])  3.23 us
    pallas_call x1, Pallas kernels, orthonormal(): pl.pallas_call(functools.partial(root_kernel, layout), out_shape=[jax.Sha...  1.55 us
    unnamed x10, local copies, waits for them, and re-layouts  1.16 us
    pallas_call x1, Pallas kernels, turned(): pl.pallas_call(functools.partial(turn_kernel, layout), out_shape=[jax.Sha...  0.98 us
  transfers between devices with their start and end apart: 10, of which 7 were waited for; matrix products, arithmetic and copies ran while one was open for 0% of the time, Pallas kernels for 3%

profile of v5, /device:TPU:0, one launch (start us, length us, event | category | flops | bytes accessed | tf_op | source)
XLA Modules:
  0.0 32.2 jit_solution(3514876893579139402)
XLA Ops:
  0.6 3.0 %collective-permute-start.1 = (bf16[1,16,128]{2,1,0:T(8,128)(2,1)}, bf16[1,16,128]{2,1,0:T(8,128)(2,1)S(1)}, u32[]{:S(2)}, u32[]{:S(2)}) collective-permute-start(bf16[1,16,128]{2,1,0:T(8,128)(2,1)} %refs_0_.1), channel_id=1, source_target_pairs={{0,16},{8,24},{16,0},{24,8},{1,17},{9,25},{17,1},{25,9},{2,18},{10... | collective-permute-start | bytes 12296 | tf_op jit(solution)/shard_map/ppermute | solution.py:302
  3.7 0.2 collective-permute-start.2
  3.9 0.0 copy-start.1
  3.9 0.0 copy-start.2
  3.9 0.1 spots.1.where_ref
  4.1 1.1 %copy-done = bf16[1,1,32,128,128]{4,3,2,1,0:T(8,128)(2,1)S(1)} copy-done((bf16[1,1,32,128,128]{4,3,2,1,0:T(8,128)(2,1)S(1)}, bf16[1,1,32,128,128]{4,3,2,1,0:T(8,128)(2,1)}, u32[]{:S(2)}) %copy-start) | copy-done | bytes 1048600
  5.1 0.1 copy-done.1
  5.2 1.0 %turned.1 = (bf16[1,4,9,128,128]{4,3,2,1,0:T(8,128)(2,1)S(1)}, bf16[1,4,17,128,128]{4,3,2,1,0:T(8,128)(2,1)S(1)}) custom-call(s32[1,44]{1,0:T(1,128)S(1)} %spots.1.where_ref, bf16[1,32,128,128]{3,2,1,0:T(8,128)(2,1)S(1)} %bitcast.4, bf16[1,12,128,128]{3,2,1,0:T(8,128)(2,1)S(1)} %bitcast.5), custom_call_target="tpu_custom_call" | custom-call | bytes 2883584 | tf_op jit(solution)/shard_map/turned/pallas_call | solution.py:139
  6.2 0.7 %collective-permute-done.2.refs_3_ = bf16[1,16,128]{2,1,0:T(8,128)(2,1)S(1)} collective-permute-done((bf16[1,16,128]{2,1,0:T(8,128)(2,1)}, bf16[1,16,128]{2,1,0:T(8,128)(2,1)S(1)}, u32[]{:S(2)}, u32[]{:S(2)}) %collective-permute-start.2) | collective-permute-done | bytes 4128 | tf_op jit(solution)/shard_map/ppermute | solution.py:302
  6.9 0.5 %tile_products.1 = (f32[1,12,16,128]{3,2,1,0:T(8,128)S(1)}, f32[1,12,16,128]{3,2,1,0:T(8,128)S(1)}) custom-call(bf16[1,16,128]{2,1,0:T(8,128)(2,1)S(1)} %copy-done.2, bf16[1,16,128]{2,1,0:T(8,128)(2,1)S(1)} %collective-permute-done.refs_1_, bf16[1,16,128]{2,1,0:T(8,128)(2,1)S(1)} %collective-permute-done.1.refs_2_, ...), custom_call_target="tpu_custom_call" | custom-call | tf_op jit(solution)/shard_map/tile_products/pallas_call | solution.py:178
  7.5 1.5 %collective-permute-start.3 = (f32[1,12,16,128]{3,2,1,0:T(8,128)S(1)}, f32[1,12,16,128]{3,2,1,0:T(8,128)S(1)}, u32[]{:S(2)}, u32[]{:S(2)}) collective-permute-start(f32[1,12,16,128]{3,2,1,0:T(8,128)S(1)} %get-tuple-element.9), channel_id=1, source_target_pairs={{0,1},{1,0},{2,3},{3,2},{4,5},{5,4},{6,7},{7,6},{8,9},{9,8},{10,11... | collective-permute-start | bytes 294920 | tf_op jit(solution)/shard_map/ppermute | solution.py:37
  9.0 3.7 %collective-permute-done.3 = f32[1,12,16,128]{3,2,1,0:T(8,128)S(1)} collective-permute-done((f32[1,12,16,128]{3,2,1,0:T(8,128)S(1)}, f32[1,12,16,128]{3,2,1,0:T(8,128)S(1)}, u32[]{:S(2)}, u32[]{:S(2)}) %collective-permute-start.3) | collective-permute-done | bytes 98336 | tf_op jit(solution)/shard_map/ppermute | solution.py:37
  12.7 1.6 %collective-permute-start.4 = (f32[1,12,16,128]{3,2,1,0:T(8,128)S(1)}, f32[1,12,16,128]{3,2,1,0:T(8,128)S(1)}, u32[]{:S(2)}, u32[]{:S(2)}) collective-permute-start(f32[1,12,16,128]{3,2,1,0:T(8,128)S(1)} %add.21), channel_id=1, source_target_pairs={{0,2},{1,3},{2,0},{3,1},{4,6},{5,7},{6,4},{7,5},{8,10},{9,11},{10,... | collective-permute-start | bytes 294920 | tf_op jit(solution)/shard_map/ppermute | solution.py:37
  14.3 3.0 %collective-permute-done.4 = f32[1,12,16,128]{3,2,1,0:T(8,128)S(1)} collective-permute-done((f32[1,12,16,128]{3,2,1,0:T(8,128)S(1)}, f32[1,12,16,128]{3,2,1,0:T(8,128)S(1)}, u32[]{:S(2)}, u32[]{:S(2)}) %collective-permute-start.4) | collective-permute-done | bytes 98336 | tf_op jit(solution)/shard_map/ppermute | solution.py:37
  17.4 2.7 %collective-permute-start.5 = (f32[1,12,16,128]{3,2,1,0:T(8,128)S(1)}, f32[1,12,16,128]{3,2,1,0:T(8,128)S(1)}, u32[]{:S(2)}, u32[]{:S(2)}) collective-permute-start(f32[1,12,16,128]{3,2,1,0:T(8,128)S(1)} %add.22), channel_id=1, source_target_pairs={{0,4},{1,5},{2,6},{3,7},{4,0},{5,1},{6,2},{7,3},{8,12},{9,13},{10,... | collective-permute-start | bytes 294920 | tf_op jit(solution)/shard_map/ppermute | solution.py:37
  20.0 2.9 %collective-permute-done.5 = f32[1,12,16,128]{3,2,1,0:T(8,128)S(1)} collective-permute-done((f32[1,12,16,128]{3,2,1,0:T(8,128)S(1)}, f32[1,12,16,128]{3,2,1,0:T(8,128)S(1)}, u32[]{:S(2)}, u32[]{:S(2)}) %collective-permute-start.5) | collective-permute-done | bytes 98336 | tf_op jit(solution)/shard_map/ppermute | solution.py:37
  23.0 0.3 gram_parts.1
  23.2 0.8 %collective-permute-start.7 = (f32[1,16,128]{2,1,0:T(8,128)S(1)}, f32[1,16,128]{2,1,0:T(8,128)S(1)}, u32[]{:S(2)}, u32[]{:S(2)}) collective-permute-start(f32[1,16,128]{2,1,0:T(8,128)S(1)} %gram_parts.1), channel_id=1, source_target_pairs={{0,16},{1,17},{2,18},{3,19},{4,20},{5,21},{6,22},{7,23},{8,24},{9,... | collective-permute-start | bytes 24584 | tf_op jit(solution)/shard_map/ppermute | solution.py:44
  24.0 1.1 %collective-permute-start.6 = (f32[1,16,128]{2,1,0:T(8,128)S(1)}, f32[1,16,128]{2,1,0:T(8,128)S(1)}, u32[]{:S(2)}, u32[]{:S(2)}) collective-permute-start(f32[1,16,128]{2,1,0:T(8,128)S(1)} %gram_parts.1), channel_id=1, source_target_pairs={{0,8},{1,9},{2,10},{3,11},{4,12},{5,13},{6,14},{7,15},{8,0},{9,1},... | collective-permute-start | bytes 24584 | tf_op jit(solution)/shard_map/ppermute | solution.py:44
  25.1 1.2 %collective-permute-done.8 = f32[1,16,128]{2,1,0:T(8,128)S(1)} collective-permute-done((f32[1,16,128]{2,1,0:T(8,128)S(1)}, f32[1,16,128]{2,1,0:T(8,128)S(1)}, u32[]{:S(2)}, u32[]{:S(2)}) %collective-permute-start.8) | collective-permute-done | bytes 8224 | tf_op jit(solution)/shard_map/ppermute | solution.py:44
  26.3 0.6 %collective-permute-done.7 = f32[1,16,128]{2,1,0:T(8,128)S(1)} collective-permute-done((f32[1,16,128]{2,1,0:T(8,128)S(1)}, f32[1,16,128]{2,1,0:T(8,128)S(1)}, u32[]{:S(2)}, u32[]{:S(2)}) %collective-permute-start.7) | collective-permute-done | bytes 8224 | tf_op jit(solution)/shard_map/ppermute | solution.py:44
  26.9 1.6 %collective-permute-start.9 = (f32[1,16,128]{2,1,0:T(8,128)S(1)}, f32[1,16,128]{2,1,0:T(8,128)S(1)}, u32[]{:S(2)}, u32[]{:S(2)}) collective-permute-start(f32[1,16,128]{2,1,0:T(8,128)S(1)} %add_add_fusion), channel_id=1, source_target_pairs={{0,1},{1,0},{2,3},{3,2},{4,5},{5,4},{6,7},{7,6},{8,9},{9,8},{10,11... | collective-permute-start | bytes 24584 | tf_op jit(solution)/shard_map/ppermute | solution.py:44
  28.5 2.1 %collective-permute-done.9 = f32[1,16,128]{2,1,0:T(8,128)S(1)} collective-permute-done((f32[1,16,128]{2,1,0:T(8,128)S(1)}, f32[1,16,128]{2,1,0:T(8,128)S(1)}, u32[]{:S(2)}, u32[]{:S(2)}) %collective-permute-start.9) | collective-permute-done | bytes 8224 | tf_op jit(solution)/shard_map/ppermute | solution.py:44
  30.7 1.6 %orthonormal.1 = (f32[1,16,128]{2,1,0:T(8,128)}, f32[1,2,16,16]{3,2,1,0:T(8,128)}) custom-call(f32[1,16,128]{2,1,0:T(8,128)S(1)} %add.27.gram_ref, f32[1,12,16,128]{3,2,1,0:T(8,128)S(1)} %add.23.x_ref), custom_call_target="tpu_custom_call" | custom-call | tf_op jit(solution)/shard_map/orthonormal/pallas_call | solution.py:271
  (17 shorter events, 0.1 us)
Async XLA Ops:
  0.6 3.3 %copy-start.4 = (s32[1,1,12]{2,1,0:T(1,128)S(1)}, s32[1,1,12]{2,1,0:T(1,128)}, u32[]{:S(2)}) copy-start(s32[1,1,12]{2,1,0:T(1,128)} %param.9) | copy-start | bytes 148
  0.6 3.2 %copy-start.3 = (s32[1,1,32]{2,1,0:T(1,128)S(1)}, s32[1,1,32]{2,1,0:T(1,128)}, u32[]{:S(2)}) copy-start(s32[1,1,32]{2,1,0:T(1,128)} %param.7) | copy-start | bytes 388
  0.6 5.5 %collective-permute-start.1 = (bf16[1,16,128]{2,1,0:T(8,128)(2,1)}, bf16[1,16,128]{2,1,0:T(8,128)(2,1)S(1)}, u32[]{:S(2)}, u32[]{:S(2)}) collective-permute-start(bf16[1,16,128]{2,1,0:T(8,128)(2,1)} %refs_0_.1), channel_id=1, source_target_pairs={{0,16},{8,24},{16,0},{24,8},{1,17},{9,25},{17,1},{25,9},{2,18},{10... | collective-permute-start | bytes 12296 | tf_op jit(solution)/shard_map/ppermute | solution.py:302
  3.7 2.5 %collective-permute-start = (bf16[1,16,128]{2,1,0:T(8,128)(2,1)}, bf16[1,16,128]{2,1,0:T(8,128)(2,1)S(1)}, u32[]{:S(2)}, u32[]{:S(2)}) collective-permute-start(bf16[1,16,128]{2,1,0:T(8,128)(2,1)} %refs_0_.1), channel_id=1, source_target_pairs={{0,8},{8,0},{16,24},{24,16},{1,9},{9,1},{17,25},{25,17},{2,10},{10... | collective-permute-start | bytes 12296 | tf_op jit(solution)/shard_map/ppermute | solution.py:302
  3.7 3.2 %collective-permute-start.2 = (bf16[1,16,128]{2,1,0:T(8,128)(2,1)}, bf16[1,16,128]{2,1,0:T(8,128)(2,1)S(1)}, u32[]{:S(2)}, u32[]{:S(2)}) collective-permute-start(bf16[1,16,128]{2,1,0:T(8,128)(2,1)} %refs_0_.1), channel_id=1, source_target_pairs={{0,24},{8,16},{16,8},{24,0},{1,25},{9,17},{17,9},{25,1},{2,26},{10... | collective-permute-start | bytes 12296 | tf_op jit(solution)/shard_map/ppermute | solution.py:302
  3.9 1.2 %copy-start = (bf16[1,1,32,128,128]{4,3,2,1,0:T(8,128)(2,1)S(1)}, bf16[1,1,32,128,128]{4,3,2,1,0:T(8,128)(2,1)}, u32[]{:S(2)}) copy-start(bf16[1,1,32,128,128]{4,3,2,1,0:T(8,128)(2,1)} %param.6) | copy-start | bytes 3145732
  3.9 1.3 %copy-start.1 = (bf16[1,1,12,128,128]{4,3,2,1,0:T(8,128)(2,1)S(1)}, bf16[1,1,12,128,128]{4,3,2,1,0:T(8,128)(2,1)}, u32[]{:S(2)}) copy-start(bf16[1,1,12,128,128]{4,3,2,1,0:T(8,128)(2,1)} %param.8) | copy-start | bytes 1179652
  3.9 3.0 %copy-start.2 = (bf16[1,16,128]{2,1,0:T(8,128)(2,1)S(1)}, bf16[1,16,128]{2,1,0:T(8,128)(2,1)}, u32[]{:S(2)}) copy-start(bf16[1,16,128]{2,1,0:T(8,128)(2,1)} %refs_0_.1) | copy-start | bytes 12292
  7.5 5.2 %collective-permute-start.3 = (f32[1,12,16,128]{3,2,1,0:T(8,128)S(1)}, f32[1,12,16,128]{3,2,1,0:T(8,128)S(1)}, u32[]{:S(2)}, u32[]{:S(2)}) collective-permute-start(f32[1,12,16,128]{3,2,1,0:T(8,128)S(1)} %get-tuple-element.9), channel_id=1, source_target_pairs={{0,1},{1,0},{2,3},{3,2},{4,5},{5,4},{6,7},{7,6},{8,9},{9,8},{10,11... | collective-permute-start | bytes 294920 | tf_op jit(solution)/shard_map/ppermute | solution.py:37
  12.7 4.7 %collective-permute-start.4 = (f32[1,12,16,128]{3,2,1,0:T(8,128)S(1)}, f32[1,12,16,128]{3,2,1,0:T(8,128)S(1)}, u32[]{:S(2)}, u32[]{:S(2)}) collective-permute-start(f32[1,12,16,128]{3,2,1,0:T(8,128)S(1)} %add.21), channel_id=1, source_target_pairs={{0,2},{1,3},{2,0},{3,1},{4,6},{5,7},{6,4},{7,5},{8,10},{9,11},{10,... | collective-permute-start | bytes 294920 | tf_op jit(solution)/shard_map/ppermute | solution.py:37
  17.4 5.6 %collective-permute-start.5 = (f32[1,12,16,128]{3,2,1,0:T(8,128)S(1)}, f32[1,12,16,128]{3,2,1,0:T(8,128)S(1)}, u32[]{:S(2)}, u32[]{:S(2)}) collective-permute-start(f32[1,12,16,128]{3,2,1,0:T(8,128)S(1)} %add.22), channel_id=1, source_target_pairs={{0,4},{1,5},{2,6},{3,7},{4,0},{5,1},{6,2},{7,3},{8,12},{9,13},{10,... | collective-permute-start | bytes 294920 | tf_op jit(solution)/shard_map/ppermute | solution.py:37
  23.2 3.1 %collective-permute-start.8 = (f32[1,16,128]{2,1,0:T(8,128)S(1)}, f32[1,16,128]{2,1,0:T(8,128)S(1)}, u32[]{:S(2)}, u32[]{:S(2)}) collective-permute-start(f32[1,16,128]{2,1,0:T(8,128)S(1)} %gram_parts.1), channel_id=1, source_target_pairs={{0,24},{1,25},{2,26},{3,27},{4,28},{5,29},{6,30},{7,31},{8,16},{9,... | collective-permute-start | bytes 24584 | tf_op jit(solution)/shard_map/ppermute | solution.py:44
  23.2 3.7 %collective-permute-start.7 = (f32[1,16,128]{2,1,0:T(8,128)S(1)}, f32[1,16,128]{2,1,0:T(8,128)S(1)}, u32[]{:S(2)}, u32[]{:S(2)}) collective-permute-start(f32[1,16,128]{2,1,0:T(8,128)S(1)} %gram_parts.1), channel_id=1, source_target_pairs={{0,16},{1,17},{2,18},{3,19},{4,20},{5,21},{6,22},{7,23},{8,24},{9,... | collective-permute-start | bytes 24584 | tf_op jit(solution)/shard_map/ppermute | solution.py:44
  24.0 2.9 %collective-permute-start.6 = (f32[1,16,128]{2,1,0:T(8,128)S(1)}, f32[1,16,128]{2,1,0:T(8,128)S(1)}, u32[]{:S(2)}, u32[]{:S(2)}) collective-permute-start(f32[1,16,128]{2,1,0:T(8,128)S(1)} %gram_parts.1), channel_id=1, source_target_pairs={{0,8},{1,9},{2,10},{3,11},{4,12},{5,13},{6,14},{7,15},{8,0},{9,1},... | collective-permute-start | bytes 24584 | tf_op jit(solution)/shard_map/ppermute | solution.py:44
  26.9 3.7 %collective-permute-start.9 = (f32[1,16,128]{2,1,0:T(8,128)S(1)}, f32[1,16,128]{2,1,0:T(8,128)S(1)}, u32[]{:S(2)}, u32[]{:S(2)}) collective-permute-start(f32[1,16,128]{2,1,0:T(8,128)S(1)} %add_add_fusion), channel_id=1, source_target_pairs={{0,1},{1,0},{2,3},{3,2},{4,5},{5,4},{6,7},{7,6},{8,9},{9,8},{10,11... | collective-permute-start | bytes 24584 | tf_op jit(solution)/shard_map/ppermute | solution.py:44

commit v6 on v5

--- a/solution.py
+++ b/solution.py
@@ -148,39 +148,44 @@
     )(where, h_tiles, j_tiles)
 
 
-def product_kernel(layout, *refs):
+def product_kernel(layout, half, *refs):
     column_tiles, row_tiles, group, halves, stride, pieces, bits = layout
-    vector_refs, (h_block_ref, j_block_ref), outs = refs[:pieces], refs[pieces : pieces + 2], refs[pieces + 2 :]
+    vector_refs, (h_block_ref, j_block_ref, out_ref) = refs[:pieces], refs[pieces:]
     kept_tiles, operators = row_tiles // halves, J_OPERATORS + 1
     tile = h_block_ref.shape[-1]
     each = column_tiles // pieces
-    for s in range(outs[0].shape[0]):
+    for s in range(out_ref.shape[0]):
         lined = jnp.concatenate(
             [vector_ref[s, :, t * tile : (t + 1) * tile] for vector_ref in vector_refs for t in range(each)], 1
         )
         for block_ref, first, count in ((j_block_ref, 1, J_OPERATORS), (h_block_ref, 0, 1)):
-            for strip in range(0, row_tiles * count, 2):
-                strips = range(strip, min(strip + 2, row_tiles * count))
+            start, stop = half * kept_tiles * count, (half + 1) * kept_tiles * count
+            for strip in range(start, stop, 2):
+                strips = range(strip, min(strip + 2, stop))
                 block = [jnp.concatenate([block_ref[s, c, n] for n in strips], 1) for c in range(column_tiles)]
                 product = jnp.dot(lined, jnp.concatenate(block, 0), preferred_element_type=jnp.float32)
                 for i, n in enumerate(strips):
-                    t = n // count
-                    at = t % kept_tiles * operators + first + n % count
-                    outs[t // kept_tiles][s, at] = product[:, i * tile : (i + 1) * tile]
-
-
-def tile_products(vectors, h_block, j_block, layout):
+                    at = n // count % kept_tiles * operators + first + n % count
+                    out_ref[s, at] = product[:, i * tile : (i + 1) * tile]
+
+
+def tile_products(vectors, h_block, j_block, layout, half):
     column_tiles, row_tiles, group, halves, stride, pieces, bits = layout
     sectors, count_vectors = vectors[0].shape[:2]
+    tile = h_block.shape[-1]
     count = row_tiles // halves * (J_OPERATORS + 1)
     vmem = pl.BlockSpec(memory_space=pltpu.VMEM)
-    shape = jax.ShapeDtypeStruct((sectors, count, count_vectors, h_block.shape[-1]), jnp.float32)
-    return pl.pallas_call(
-        functools.partial(product_kernel, layout),
-        out_shape=[shape] * halves,
+    return pl.pallas_call(
+        functools.partial(product_kernel, layout, half),
+        out_shape=jax.ShapeDtypeStruct((sectors, count, count_vectors, tile), jnp.float32),
         in_specs=[vmem] * (pieces + 2),
-        out_specs=[vmem] * halves,
+        out_specs=vmem,
         compiler_params=pltpu.CompilerParams(vmem_limit_bytes=4 << 20),
+        cost_estimate=pl.CostEstimate(
+            flops=2 * sectors * count * count_vectors * tile * tile * column_tiles,
+            transcendentals=0,
+            bytes_accessed=2 * sectors * count * tile * tile * column_tiles,
+        ),
         name="tile_products",
     )(*vectors, h_block, j_block)
 
@@ -308,10 +313,12 @@
     h_block, j_block = turned(
         where, h_tiles.reshape(sectors, -1, tile, tile), j_tiles.reshape(sectors, -1, tile, tile), layout
     )
-    outs = tile_products(parts, h_block, j_block, layout)
-    x = outs[0]
+    arriving = None
     if digit is not None:
-        x = x + sent(outs[1], "col", digit, 1)
+        arriving = sent(tile_products(parts, h_block, j_block, layout, 1), "col", digit, 1)
+    x = tile_products(parts, h_block, j_block, layout, 0)
+    if digit is not None:
+        x = x + arriving
     for other in digits_of(n_col):
         if other != digit:
             x = summed(x, "col", other)

time: 32.4 us -> 31.6 us (0.975)
  waiting for transfers between devices: 14.3 us -> 13.5 us
    ppermute x3, waiting for transfers between devices: 9.66 us -> 8.7 us  [sent(): lax.ppermute(x, axis, [(i, moved(i, digit, shift)) for i in range(size)])]
  transfers between devices with their start and end apart: 10 -> 10, of which waited for: 7 -> 7; matrix products, arithmetic and copies ran while one was open for 0% -> 0% of each run, Pallas kernels for 3% -> 5%
where the time goes in v6:
time: 31.6 us; the launch traced here: 31.4 us
  waiting for transfers between devices  13.5 us (43%)
  starting transfers between devices  12.5 us (40%)
  Pallas kernels  3.55 us (11%)
  local copies, waits for them, and re-layouts  1.16 us (4%)
  between operations  0.71 us (2%)
    ppermute x3, waiting for transfers between devices, sent(): lax.ppermute(x, axis, [(i, moved(i, digit, shift)) for i in range(size)])  8.7 us
    ppermute x3, starting transfers between devices, sent(): lax.ppermute(x, axis, [(i, moved(i, digit, shift)) for i in range(size)])  5.88 us
    ppermute x4, waiting for transfers between devices, across(): return lax.ppermute(x, ('row', 'col'), moves)  3.95 us
    ppermute x4, starting transfers between devices, across(): return lax.ppermute(x, ('row', 'col'), moves)  3.47 us
    ppermute x3, starting transfers between devices, per_device(): lax.ppermute(vectors, 'row', [(i, i ^ mask) for i in range(n_row)])  3.15 us
    pallas_call x1, Pallas kernels, orthonormal(): pl.pallas_call(functools.partial(root_kernel, layout), out_shape=[jax.Sha...  1.55 us
    unnamed x10, local copies, waits for them, and re-layouts  1.16 us
    pallas_call x1, Pallas kernels, turned(): pl.pallas_call(functools.partial(turn_kernel, layout), out_shape=[jax.Sha...  0.98 us
  transfers between devices with their start and end apart: 10, of which 7 were waited for; matrix products, arithmetic and copies ran while one was open for 0% of the time, Pallas kernels for 5%

profile of v6, /device:TPU:0, one launch (start us, length us, event | category | flops | bytes accessed | tf_op | source)
XLA Modules:
  0.0 31.4 jit_solution(4263584959938021352)
XLA Ops:
  0.6 2.5 %collective-permute-start.2 = (bf16[1,16,128]{2,1,0:T(8,128)(2,1)}, bf16[1,16,128]{2,1,0:T(8,128)(2,1)S(1)}, u32[]{:S(2)}, u32[]{:S(2)}) collective-permute-start(bf16[1,16,128]{2,1,0:T(8,128)(2,1)} %refs_0_.3), channel_id=1, source_target_pairs={{0,24},{8,16},{16,8},{24,0},{1,25},{9,17},{17,9},{25,1},{2,26},{10... | collective-permute-start | bytes 12296 | tf_op jit(solution)/shard_map/ppermute | solution.py:307
  3.1 0.6 %collective-permute-start.1 = (bf16[1,16,128]{2,1,0:T(8,128)(2,1)}, bf16[1,16,128]{2,1,0:T(8,128)(2,1)S(1)}, u32[]{:S(2)}, u32[]{:S(2)}) collective-permute-start(bf16[1,16,128]{2,1,0:T(8,128)(2,1)} %refs_0_.3), channel_id=1, source_target_pairs={{0,16},{8,24},{16,0},{24,8},{1,17},{9,25},{17,1},{25,9},{2,18},{10... | collective-permute-start | bytes 12296 | tf_op jit(solution)/shard_map/ppermute | solution.py:307
  3.8 0.0 collective-permute-start
  3.8 0.1 spots.1.where_ref
  4.0 1.1 %copy-done = bf16[1,1,32,128,128]{4,3,2,1,0:T(8,128)(2,1)S(1)} copy-done((bf16[1,1,32,128,128]{4,3,2,1,0:T(8,128)(2,1)S(1)}, bf16[1,1,32,128,128]{4,3,2,1,0:T(8,128)(2,1)}, u32[]{:S(2)}) %copy-start) | copy-done | bytes 1048600
  5.0 0.1 copy-done.1
  5.1 1.0 %turned.1 = (bf16[1,4,9,128,128]{4,3,2,1,0:T(8,128)(2,1)S(1)}, bf16[1,4,17,128,128]{4,3,2,1,0:T(8,128)(2,1)S(1)}) custom-call(s32[1,44]{1,0:T(1,128)S(1)} %spots.1.where_ref, bf16[1,32,128,128]{3,2,1,0:T(8,128)(2,1)S(1)} %bitcast.4, bf16[1,12,128,128]{3,2,1,0:T(8,128)(2,1)S(1)} %bitcast.5), custom_call_target="tpu_custom_call" | custom-call | bytes 2883584 | tf_op jit(solution)/shard_map/turned/pallas_call | solution.py:139
  6.1 0.8 %collective-permute-done.1.refs_2_ = bf16[1,16,128]{2,1,0:T(8,128)(2,1)S(1)} collective-permute-done((bf16[1,16,128]{2,1,0:T(8,128)(2,1)}, bf16[1,16,128]{2,1,0:T(8,128)(2,1)S(1)}, u32[]{:S(2)}, u32[]{:S(2)}) %collective-permute-start.1) | collective-permute-done | bytes 4128 | tf_op jit(solution)/shard_map/ppermute | solution.py:307
  6.9 0.3 %tile_products.3 = f32[1,12,16,128]{3,2,1,0:T(8,128)S(1)} custom-call(bf16[1,16,128]{2,1,0:T(8,128)(2,1)S(1)} %copy-done.2, bf16[1,16,128]{2,1,0:T(8,128)(2,1)S(1)} %collective-permute-done.refs_1_, bf16[1,16,128]{2,1,0:T(8,128)(2,1)S(1)} %collective-permute-done.1.refs_2_, bf16[1,16,128]{2,1,0:T(8,128)(2,1)S(1)} %collective-permute-done.2.refs_3_, ...), custom_call_target="tpu_custom_call" | custom-call | flops 25165824 | bytes 1572864 | tf_op jit(solution)/shard_map/tile_products/pallas_call | solution.py:178
  7.3 1.5 %collective-permute-start.3 = (f32[1,12,16,128]{3,2,1,0:T(8,128)S(1)}, f32[1,12,16,128]{3,2,1,0:T(8,128)S(1)}, u32[]{:S(2)}, u32[]{:S(2)}) collective-permute-start(f32[1,12,16,128]{3,2,1,0:T(8,128)S(1)} %tile_products.3), channel_id=1, source_target_pairs={{0,1},{1,0},{2,3},{3,2},{4,5},{5,4},{6,7},{7,6},{8,9},{9,8},{10,11... | collective-permute-start | bytes 294920 | tf_op jit(solution)/shard_map/ppermute | solution.py:37
  8.8 0.3 tile_products.2
  9.1 2.8 %collective-permute-done.3 = f32[1,12,16,128]{3,2,1,0:T(8,128)S(1)} collective-permute-done((f32[1,12,16,128]{3,2,1,0:T(8,128)S(1)}, f32[1,12,16,128]{3,2,1,0:T(8,128)S(1)}, u32[]{:S(2)}, u32[]{:S(2)}) %collective-permute-start.3) | collective-permute-done | bytes 98336 | tf_op jit(solution)/shard_map/ppermute | solution.py:37
  11.9 1.6 %collective-permute-start.4 = (f32[1,12,16,128]{3,2,1,0:T(8,128)S(1)}, f32[1,12,16,128]{3,2,1,0:T(8,128)S(1)}, u32[]{:S(2)}, u32[]{:S(2)}) collective-permute-start(f32[1,12,16,128]{3,2,1,0:T(8,128)S(1)} %add.21), channel_id=1, source_target_pairs={{0,2},{1,3},{2,0},{3,1},{4,6},{5,7},{6,4},{7,5},{8,10},{9,11},{10,... | collective-permute-start | bytes 294920 | tf_op jit(solution)/shard_map/ppermute | solution.py:37
  13.5 3.0 %collective-permute-done.4 = f32[1,12,16,128]{3,2,1,0:T(8,128)S(1)} collective-permute-done((f32[1,12,16,128]{3,2,1,0:T(8,128)S(1)}, f32[1,12,16,128]{3,2,1,0:T(8,128)S(1)}, u32[]{:S(2)}, u32[]{:S(2)}) %collective-permute-start.4) | collective-permute-done | bytes 98336 | tf_op jit(solution)/shard_map/ppermute | solution.py:37
  16.6 2.7 %collective-permute-start.5 = (f32[1,12,16,128]{3,2,1,0:T(8,128)S(1)}, f32[1,12,16,128]{3,2,1,0:T(8,128)S(1)}, u32[]{:S(2)}, u32[]{:S(2)}) collective-permute-start(f32[1,12,16,128]{3,2,1,0:T(8,128)S(1)} %add.22), channel_id=1, source_target_pairs={{0,4},{1,5},{2,6},{3,7},{4,0},{5,1},{6,2},{7,3},{8,12},{9,13},{10,... | collective-permute-start | bytes 294920 | tf_op jit(solution)/shard_map/ppermute | solution.py:37
  19.3 2.9 %collective-permute-done.5 = f32[1,12,16,128]{3,2,1,0:T(8,128)S(1)} collective-permute-done((f32[1,12,16,128]{3,2,1,0:T(8,128)S(1)}, f32[1,12,16,128]{3,2,1,0:T(8,128)S(1)}, u32[]{:S(2)}, u32[]{:S(2)}) %collective-permute-start.5) | collective-permute-done | bytes 98336 | tf_op jit(solution)/shard_map/ppermute | solution.py:37
  22.2 0.3 gram_parts.1
  22.5 1.2 %collective-permute-start.7 = (f32[1,16,128]{2,1,0:T(8,128)S(1)}, f32[1,16,128]{2,1,0:T(8,128)S(1)}, u32[]{:S(2)}, u32[]{:S(2)}) collective-permute-start(f32[1,16,128]{2,1,0:T(8,128)S(1)} %gram_parts.1), channel_id=1, source_target_pairs={{0,16},{1,17},{2,18},{3,19},{4,20},{5,21},{6,22},{7,23},{8,24},{9,... | collective-permute-start | bytes 24584 | tf_op jit(solution)/shard_map/ppermute | solution.py:44
  23.7 0.7 %collective-permute-start.6 = (f32[1,16,128]{2,1,0:T(8,128)S(1)}, f32[1,16,128]{2,1,0:T(8,128)S(1)}, u32[]{:S(2)}, u32[]{:S(2)}) collective-permute-start(f32[1,16,128]{2,1,0:T(8,128)S(1)} %gram_parts.1), channel_id=1, source_target_pairs={{0,8},{1,9},{2,10},{3,11},{4,12},{5,13},{6,14},{7,15},{8,0},{9,1},... | collective-permute-start | bytes 24584 | tf_op jit(solution)/shard_map/ppermute | solution.py:44
  24.3 1.2 %collective-permute-done.8 = f32[1,16,128]{2,1,0:T(8,128)S(1)} collective-permute-done((f32[1,16,128]{2,1,0:T(8,128)S(1)}, f32[1,16,128]{2,1,0:T(8,128)S(1)}, u32[]{:S(2)}, u32[]{:S(2)}) %collective-permute-start.8) | collective-permute-done | bytes 8224 | tf_op jit(solution)/shard_map/ppermute | solution.py:44
  25.6 0.6 %collective-permute-done.7 = f32[1,16,128]{2,1,0:T(8,128)S(1)} collective-permute-done((f32[1,16,128]{2,1,0:T(8,128)S(1)}, f32[1,16,128]{2,1,0:T(8,128)S(1)}, u32[]{:S(2)}, u32[]{:S(2)}) %collective-permute-start.7) | collective-permute-done | bytes 8224 | tf_op jit(solution)/shard_map/ppermute | solution.py:44
  26.2 1.6 %collective-permute-start.9 = (f32[1,16,128]{2,1,0:T(8,128)S(1)}, f32[1,16,128]{2,1,0:T(8,128)S(1)}, u32[]{:S(2)}, u32[]{:S(2)}) collective-permute-start(f32[1,16,128]{2,1,0:T(8,128)S(1)} %add_add_fusion), channel_id=1, source_target_pairs={{0,1},{1,0},{2,3},{3,2},{4,5},{5,4},{6,7},{7,6},{8,9},{9,8},{10,11... | collective-permute-start | bytes 24584 | tf_op jit(solution)/shard_map/ppermute | solution.py:44
  27.8 2.1 %collective-permute-done.9 = f32[1,16,128]{2,1,0:T(8,128)S(1)} collective-permute-done((f32[1,16,128]{2,1,0:T(8,128)S(1)}, f32[1,16,128]{2,1,0:T(8,128)S(1)}, u32[]{:S(2)}, u32[]{:S(2)}) %collective-permute-start.9) | collective-permute-done | bytes 8224 | tf_op jit(solution)/shard_map/ppermute | solution.py:44
  29.9 1.6 %orthonormal.1 = (f32[1,16,128]{2,1,0:T(8,128)}, f32[1,2,16,16]{3,2,1,0:T(8,128)}) custom-call(f32[1,16,128]{2,1,0:T(8,128)S(1)} %add.27.gram_ref, f32[1,12,16,128]{3,2,1,0:T(8,128)S(1)} %add.23.x_ref), custom_call_target="tpu_custom_call" | custom-call | tf_op jit(solution)/shard_map/orthonormal/pallas_call | solution.py:276
  (18 shorter events, 0.1 us)
Async XLA Ops:
  0.6 3.2 %copy-start.4 = (s32[1,1,12]{2,1,0:T(1,128)S(1)}, s32[1,1,12]{2,1,0:T(1,128)}, u32[]{:S(2)}) copy-start(s32[1,1,12]{2,1,0:T(1,128)} %param.9) | copy-start | bytes 148
  0.6 3.2 %copy-start.3 = (s32[1,1,32]{2,1,0:T(1,128)S(1)}, s32[1,1,32]{2,1,0:T(1,128)}, u32[]{:S(2)}) copy-start(s32[1,1,32]{2,1,0:T(1,128)} %param.7) | copy-start | bytes 388
  0.6 5.5 %collective-permute-start.2 = (bf16[1,16,128]{2,1,0:T(8,128)(2,1)}, bf16[1,16,128]{2,1,0:T(8,128)(2,1)S(1)}, u32[]{:S(2)}, u32[]{:S(2)}) collective-permute-start(bf16[1,16,128]{2,1,0:T(8,128)(2,1)} %refs_0_.3), channel_id=1, source_target_pairs={{0,24},{8,16},{16,8},{24,0},{1,25},{9,17},{17,9},{25,1},{2,26},{10... | collective-permute-start | bytes 12296 | tf_op jit(solution)/shard_map/ppermute | solution.py:307
  3.1 3.8 %collective-permute-start.1 = (bf16[1,16,128]{2,1,0:T(8,128)(2,1)}, bf16[1,16,128]{2,1,0:T(8,128)(2,1)S(1)}, u32[]{:S(2)}, u32[]{:S(2)}) collective-permute-start(bf16[1,16,128]{2,1,0:T(8,128)(2,1)} %refs_0_.3), channel_id=1, source_target_pairs={{0,16},{8,24},{16,0},{24,8},{1,17},{9,25},{17,1},{25,9},{2,18},{10... | collective-permute-start | bytes 12296 | tf_op jit(solution)/shard_map/ppermute | solution.py:307
  3.8 3.2 %collective-permute-start = (bf16[1,16,128]{2,1,0:T(8,128)(2,1)}, bf16[1,16,128]{2,1,0:T(8,128)(2,1)S(1)}, u32[]{:S(2)}, u32[]{:S(2)}) collective-permute-start(bf16[1,16,128]{2,1,0:T(8,128)(2,1)} %refs_0_.3), channel_id=1, source_target_pairs={{0,8},{8,0},{16,24},{24,16},{1,9},{9,1},{17,25},{25,17},{2,10},{10... | collective-permute-start | bytes 12296 | tf_op jit(solution)/shard_map/ppermute | solution.py:307
  3.8 1.2 %copy-start = (bf16[1,1,32,128,128]{4,3,2,1,0:T(8,128)(2,1)S(1)}, bf16[1,1,32,128,128]{4,3,2,1,0:T(8,128)(2,1)}, u32[]{:S(2)}) copy-start(bf16[1,1,32,128,128]{4,3,2,1,0:T(8,128)(2,1)} %param.6) | copy-start | bytes 3145732
  3.8 1.3 %copy-start.1 = (bf16[1,1,12,128,128]{4,3,2,1,0:T(8,128)(2,1)S(1)}, bf16[1,1,12,128,128]{4,3,2,1,0:T(8,128)(2,1)}, u32[]{:S(2)}) copy-start(bf16[1,1,12,128,128]{4,3,2,1,0:T(8,128)(2,1)} %param.8) | copy-start | bytes 1179652
  3.8 3.1 %copy-start.2 = (bf16[1,16,128]{2,1,0:T(8,128)(2,1)S(1)}, bf16[1,16,128]{2,1,0:T(8,128)(2,1)}, u32[]{:S(2)}) copy-start(bf16[1,16,128]{2,1,0:T(8,128)(2,1)} %refs_0_.3) | copy-start | bytes 12292
  7.3 4.6 %collective-permute-start.3 = (f32[1,12,16,128]{3,2,1,0:T(8,128)S(1)}, f32[1,12,16,128]{3,2,1,0:T(8,128)S(1)}, u32[]{:S(2)}, u32[]{:S(2)}) collective-permute-start(f32[1,12,16,128]{3,2,1,0:T(8,128)S(1)} %tile_products.3), channel_id=1, source_target_pairs={{0,1},{1,0},{2,3},{3,2},{4,5},{5,4},{6,7},{7,6},{8,9},{9,8},{10,11... | collective-permute-start | bytes 294920 | tf_op jit(solution)/shard_map/ppermute | solution.py:37
  11.9 4.7 %collective-permute-start.4 = (f32[1,12,16,128]{3,2,1,0:T(8,128)S(1)}, f32[1,12,16,128]{3,2,1,0:T(8,128)S(1)}, u32[]{:S(2)}, u32[]{:S(2)}) collective-permute-start(f32[1,12,16,128]{3,2,1,0:T(8,128)S(1)} %add.21), channel_id=1, source_target_pairs={{0,2},{1,3},{2,0},{3,1},{4,6},{5,7},{6,4},{7,5},{8,10},{9,11},{10,... | collective-permute-start | bytes 294920 | tf_op jit(solution)/shard_map/ppermute | solution.py:37
  16.6 5.6 %collective-permute-start.5 = (f32[1,12,16,128]{3,2,1,0:T(8,128)S(1)}, f32[1,12,16,128]{3,2,1,0:T(8,128)S(1)}, u32[]{:S(2)}, u32[]{:S(2)}) collective-permute-start(f32[1,12,16,128]{3,2,1,0:T(8,128)S(1)} %add.22), channel_id=1, source_target_pairs={{0,4},{1,5},{2,6},{3,7},{4,0},{5,1},{6,2},{7,3},{8,12},{9,13},{10,... | collective-permute-start | bytes 294920 | tf_op jit(solution)/shard_map/ppermute | solution.py:37
  22.5 3.1 %collective-permute-start.8 = (f32[1,16,128]{2,1,0:T(8,128)S(1)}, f32[1,16,128]{2,1,0:T(8,128)S(1)}, u32[]{:S(2)}, u32[]{:S(2)}) collective-permute-start(f32[1,16,128]{2,1,0:T(8,128)S(1)} %gram_parts.1), channel_id=1, source_target_pairs={{0,24},{1,25},{2,26},{3,27},{4,28},{5,29},{6,30},{7,31},{8,16},{9,... | collective-permute-start | bytes 24584 | tf_op jit(solution)/shard_map/ppermute | solution.py:44
  22.5 3.7 %collective-permute-start.7 = (f32[1,16,128]{2,1,0:T(8,128)S(1)}, f32[1,16,128]{2,1,0:T(8,128)S(1)}, u32[]{:S(2)}, u32[]{:S(2)}) collective-permute-start(f32[1,16,128]{2,1,0:T(8,128)S(1)} %gram_parts.1), channel_id=1, source_target_pairs={{0,16},{1,17},{2,18},{3,19},{4,20},{5,21},{6,22},{7,23},{8,24},{9,... | collective-permute-start | bytes 24584 | tf_op jit(solution)/shard_map/ppermute | solution.py:44
  23.7 2.5 %collective-permute-start.6 = (f32[1,16,128]{2,1,0:T(8,128)S(1)}, f32[1,16,128]{2,1,0:T(8,128)S(1)}, u32[]{:S(2)}, u32[]{:S(2)}) collective-permute-start(f32[1,16,128]{2,1,0:T(8,128)S(1)} %gram_parts.1), channel_id=1, source_target_pairs={{0,8},{1,9},{2,10},{3,11},{4,12},{5,13},{6,14},{7,15},{8,0},{9,1},... | collective-permute-start | bytes 24584 | tf_op jit(solution)/shard_map/ppermute | solution.py:44
  26.2 3.7 %collective-permute-start.9 = (f32[1,16,128]{2,1,0:T(8,128)S(1)}, f32[1,16,128]{2,1,0:T(8,128)S(1)}, u32[]{:S(2)}, u32[]{:S(2)}) collective-permute-start(f32[1,16,128]{2,1,0:T(8,128)S(1)} %add_add_fusion), channel_id=1, source_target_pairs={{0,1},{1,0},{2,3},{3,2},{4,5},{5,4},{6,7},{7,6},{8,9},{9,8},{10,11... | collective-permute-start | bytes 24584 | tf_op jit(solution)/shard_map/ppermute | solution.py:44

commit v7 on v6

--- a/solution.py
+++ b/solution.py
@@ -195,18 +195,15 @@
     operators = J_OPERATORS + 1
     out_ref[...] = jnp.zeros_like(out_ref)
     for s in range(sectors):
-        part = None
-        for t in range(count // operators):
-            strip = x_ref[s, t * operators : (t + 1) * operators]
-            term = lax.dot_general(
-                strip[0],
-                strip.reshape(operators * vectors, -1),
-                (((1,), (1,)), ((), ())),
-                precision=exact_precision,
-                preferred_element_type=jnp.float32,
-            )
-            part = term if part is None else part + term
-        out_ref[s, :, : operators * vectors] = part
+        strips = [x_ref[s, t * operators : (t + 1) * operators] for t in range(count // operators)]
+        right = jnp.concatenate([strip.reshape(operators * vectors, -1) for strip in strips], 1)
+        out_ref[s, :, : operators * vectors] = lax.dot_general(
+            right[:vectors],
+            right,
+            (((1,), (1,)), ((), ())),
+            precision=exact_precision,
+            preferred_element_type=jnp.float32,
+        )
 
 
 def gram_parts(x):

time: 31.6 us -> 31.5 us (level)
  no operation moved by 1% of the time
where the time goes in v7:
time: 31.5 us; the launch traced here: 31.4 us
  waiting for transfers between devices  13.5 us (43%)
  starting transfers between devices  12.5 us (40%)
  Pallas kernels  3.49 us (11%)
  local copies, waits for them, and re-layouts  1.16 us (4%)
  between operations  0.71 us (2%)
    ppermute x3, waiting for transfers between devices, sent(): lax.ppermute(x, axis, [(i, moved(i, digit, shift)) for i in range(size)])  8.7 us
    ppermute x3, starting transfers between devices, sent(): lax.ppermute(x, axis, [(i, moved(i, digit, shift)) for i in range(size)])  5.88 us
    ppermute x4, waiting for transfers between devices, across(): return lax.ppermute(x, ('row', 'col'), moves)  3.95 us
    ppermute x4, starting transfers between devices, across(): return lax.ppermute(x, ('row', 'col'), moves)  3.46 us
    ppermute x3, starting transfers between devices, per_device(): lax.ppermute(vectors, 'row', [(i, i ^ mask) for i in range(n_row)])  3.15 us
    pallas_call x1, Pallas kernels, orthonormal(): pl.pallas_call(functools.partial(root_kernel, layout), out_shape=[jax.Sha...  1.55 us
    unnamed x10, local copies, waits for them, and re-layouts  1.16 us
    pallas_call x1, Pallas kernels, turned(): pl.pallas_call(functools.partial(turn_kernel, layout), out_shape=[jax.Sha...  0.98 us
  transfers between devices with their start and end apart: 10, of which 7 were waited for; matrix products, arithmetic and copies ran while one was open for 0% of the time, Pallas kernels for 5%

profile of v7, /device:TPU:0, one launch (start us, length us, event | category | flops | bytes accessed | tf_op | source)
XLA Modules:
  0.0 31.4 jit_solution(6406986925325843412)
XLA Ops:
  0.6 2.5 %collective-permute-start.2 = (bf16[1,16,128]{2,1,0:T(8,128)(2,1)}, bf16[1,16,128]{2,1,0:T(8,128)(2,1)S(1)}, u32[]{:S(2)}, u32[]{:S(2)}) collective-permute-start(bf16[1,16,128]{2,1,0:T(8,128)(2,1)} %refs_0_.3), channel_id=1, source_target_pairs={{0,24},{8,16},{16,8},{24,0},{1,25},{9,17},{17,9},{25,1},{2,26},{10... | collective-permute-start | bytes 12296 | tf_op jit(solution)/shard_map/ppermute | solution.py:304
  3.1 0.6 %collective-permute-start.1 = (bf16[1,16,128]{2,1,0:T(8,128)(2,1)}, bf16[1,16,128]{2,1,0:T(8,128)(2,1)S(1)}, u32[]{:S(2)}, u32[]{:S(2)}) collective-permute-start(bf16[1,16,128]{2,1,0:T(8,128)(2,1)} %refs_0_.3), channel_id=1, source_target_pairs={{0,16},{8,24},{16,0},{24,8},{1,17},{9,25},{17,1},{25,9},{2,18},{10... | collective-permute-start | bytes 12296 | tf_op jit(solution)/shard_map/ppermute | solution.py:304
  3.8 0.0 collective-permute-start
  3.8 0.1 spots.1.where_ref
  4.0 1.1 %copy-done = bf16[1,1,32,128,128]{4,3,2,1,0:T(8,128)(2,1)S(1)} copy-done((bf16[1,1,32,128,128]{4,3,2,1,0:T(8,128)(2,1)S(1)}, bf16[1,1,32,128,128]{4,3,2,1,0:T(8,128)(2,1)}, u32[]{:S(2)}) %copy-start) | copy-done | bytes 1048600
  5.0 0.1 copy-done.1
  5.1 1.0 %turned.1 = (bf16[1,4,9,128,128]{4,3,2,1,0:T(8,128)(2,1)S(1)}, bf16[1,4,17,128,128]{4,3,2,1,0:T(8,128)(2,1)S(1)}) custom-call(s32[1,44]{1,0:T(1,128)S(1)} %spots.1.where_ref, bf16[1,32,128,128]{3,2,1,0:T(8,128)(2,1)S(1)} %bitcast.4, bf16[1,12,128,128]{3,2,1,0:T(8,128)(2,1)S(1)} %bitcast.5), custom_call_target="tpu_custom_call" | custom-call | bytes 2883584 | tf_op jit(solution)/shard_map/turned/pallas_call | solution.py:139
  6.1 0.8 %collective-permute-done.1.refs_2_ = bf16[1,16,128]{2,1,0:T(8,128)(2,1)S(1)} collective-permute-done((bf16[1,16,128]{2,1,0:T(8,128)(2,1)}, bf16[1,16,128]{2,1,0:T(8,128)(2,1)S(1)}, u32[]{:S(2)}, u32[]{:S(2)}) %collective-permute-start.1) | collective-permute-done | bytes 4128 | tf_op jit(solution)/shard_map/ppermute | solution.py:304
  6.9 0.3 %tile_products.3 = f32[1,12,16,128]{3,2,1,0:T(8,128)S(1)} custom-call(bf16[1,16,128]{2,1,0:T(8,128)(2,1)S(1)} %copy-done.2, bf16[1,16,128]{2,1,0:T(8,128)(2,1)S(1)} %collective-permute-done.refs_1_, bf16[1,16,128]{2,1,0:T(8,128)(2,1)S(1)} %collective-permute-done.1.refs_2_, bf16[1,16,128]{2,1,0:T(8,128)(2,1)S(1)} %collective-permute-done.2.refs_3_, ...), custom_call_target="tpu_custom_call" | custom-call | flops 25165824 | bytes 1572864 | tf_op jit(solution)/shard_map/tile_products/pallas_call | solution.py:178
  7.3 1.5 %collective-permute-start.3 = (f32[1,12,16,128]{3,2,1,0:T(8,128)S(1)}, f32[1,12,16,128]{3,2,1,0:T(8,128)S(1)}, u32[]{:S(2)}, u32[]{:S(2)}) collective-permute-start(f32[1,12,16,128]{3,2,1,0:T(8,128)S(1)} %tile_products.3), channel_id=1, source_target_pairs={{0,1},{1,0},{2,3},{3,2},{4,5},{5,4},{6,7},{7,6},{8,9},{9,8},{10,11... | collective-permute-start | bytes 294920 | tf_op jit(solution)/shard_map/ppermute | solution.py:37
  8.8 0.3 %tile_products.2 = f32[1,12,16,128]{3,2,1,0:T(8,128)S(1)} custom-call(bf16[1,16,128]{2,1,0:T(8,128)(2,1)S(1)} %copy-done.2, bf16[1,16,128]{2,1,0:T(8,128)(2,1)S(1)} %collective-permute-done.refs_1_, bf16[1,16,128]{2,1,0:T(8,128)(2,1)S(1)} %collective-permute-done.1.refs_2_, bf16[1,16,128]{2,1,0:T(8,128)(2,1)S(1)} %collective-permute-done.2.refs_3_, ...), custom_call_target="tpu_custom_call" | custom-call | flops 25165824 | bytes 1572864 | tf_op jit(solution)/shard_map/tile_products/pallas_call | solution.py:178
  9.1 2.8 %collective-permute-done.3 = f32[1,12,16,128]{3,2,1,0:T(8,128)S(1)} collective-permute-done((f32[1,12,16,128]{3,2,1,0:T(8,128)S(1)}, f32[1,12,16,128]{3,2,1,0:T(8,128)S(1)}, u32[]{:S(2)}, u32[]{:S(2)}) %collective-permute-start.3) | collective-permute-done | bytes 98336 | tf_op jit(solution)/shard_map/ppermute | solution.py:37
  11.9 1.6 %collective-permute-start.4 = (f32[1,12,16,128]{3,2,1,0:T(8,128)S(1)}, f32[1,12,16,128]{3,2,1,0:T(8,128)S(1)}, u32[]{:S(2)}, u32[]{:S(2)}) collective-permute-start(f32[1,12,16,128]{3,2,1,0:T(8,128)S(1)} %add.21), channel_id=1, source_target_pairs={{0,2},{1,3},{2,0},{3,1},{4,6},{5,7},{6,4},{7,5},{8,10},{9,11},{10,... | collective-permute-start | bytes 294920 | tf_op jit(solution)/shard_map/ppermute | solution.py:37
  13.5 3.0 %collective-permute-done.4 = f32[1,12,16,128]{3,2,1,0:T(8,128)S(1)} collective-permute-done((f32[1,12,16,128]{3,2,1,0:T(8,128)S(1)}, f32[1,12,16,128]{3,2,1,0:T(8,128)S(1)}, u32[]{:S(2)}, u32[]{:S(2)}) %collective-permute-start.4) | collective-permute-done | bytes 98336 | tf_op jit(solution)/shard_map/ppermute | solution.py:37
  16.6 2.7 %collective-permute-start.5 = (f32[1,12,16,128]{3,2,1,0:T(8,128)S(1)}, f32[1,12,16,128]{3,2,1,0:T(8,128)S(1)}, u32[]{:S(2)}, u32[]{:S(2)}) collective-permute-start(f32[1,12,16,128]{3,2,1,0:T(8,128)S(1)} %add.22), channel_id=1, source_target_pairs={{0,4},{1,5},{2,6},{3,7},{4,0},{5,1},{6,2},{7,3},{8,12},{9,13},{10,... | collective-permute-start | bytes 294920 | tf_op jit(solution)/shard_map/ppermute | solution.py:37
  19.3 2.9 %collective-permute-done.5 = f32[1,12,16,128]{3,2,1,0:T(8,128)S(1)} collective-permute-done((f32[1,12,16,128]{3,2,1,0:T(8,128)S(1)}, f32[1,12,16,128]{3,2,1,0:T(8,128)S(1)}, u32[]{:S(2)}, u32[]{:S(2)}) %collective-permute-start.5) | collective-permute-done | bytes 98336 | tf_op jit(solution)/shard_map/ppermute | solution.py:37
  22.2 0.2 gram_parts.1
  22.4 1.2 %collective-permute-start.7 = (f32[1,16,128]{2,1,0:T(8,128)S(1)}, f32[1,16,128]{2,1,0:T(8,128)S(1)}, u32[]{:S(2)}, u32[]{:S(2)}) collective-permute-start(f32[1,16,128]{2,1,0:T(8,128)S(1)} %gram_parts.1), channel_id=1, source_target_pairs={{0,16},{1,17},{2,18},{3,19},{4,20},{5,21},{6,22},{7,23},{8,24},{9,... | collective-permute-start | bytes 24584 | tf_op jit(solution)/shard_map/ppermute | solution.py:44
  23.6 0.7 %collective-permute-start.6 = (f32[1,16,128]{2,1,0:T(8,128)S(1)}, f32[1,16,128]{2,1,0:T(8,128)S(1)}, u32[]{:S(2)}, u32[]{:S(2)}) collective-permute-start(f32[1,16,128]{2,1,0:T(8,128)S(1)} %gram_parts.1), channel_id=1, source_target_pairs={{0,8},{1,9},{2,10},{3,11},{4,12},{5,13},{6,14},{7,15},{8,0},{9,1},... | collective-permute-start | bytes 24584 | tf_op jit(solution)/shard_map/ppermute | solution.py:44
  24.3 1.2 %collective-permute-done.8 = f32[1,16,128]{2,1,0:T(8,128)S(1)} collective-permute-done((f32[1,16,128]{2,1,0:T(8,128)S(1)}, f32[1,16,128]{2,1,0:T(8,128)S(1)}, u32[]{:S(2)}, u32[]{:S(2)}) %collective-permute-start.8) | collective-permute-done | bytes 8224 | tf_op jit(solution)/shard_map/ppermute | solution.py:44
  25.5 0.6 %collective-permute-done.7 = f32[1,16,128]{2,1,0:T(8,128)S(1)} collective-permute-done((f32[1,16,128]{2,1,0:T(8,128)S(1)}, f32[1,16,128]{2,1,0:T(8,128)S(1)}, u32[]{:S(2)}, u32[]{:S(2)}) %collective-permute-start.7) | collective-permute-done | bytes 8224 | tf_op jit(solution)/shard_map/ppermute | solution.py:44
  26.1 1.6 %collective-permute-start.9 = (f32[1,16,128]{2,1,0:T(8,128)S(1)}, f32[1,16,128]{2,1,0:T(8,128)S(1)}, u32[]{:S(2)}, u32[]{:S(2)}) collective-permute-start(f32[1,16,128]{2,1,0:T(8,128)S(1)} %add_add_fusion), channel_id=1, source_target_pairs={{0,1},{1,0},{2,3},{3,2},{4,5},{5,4},{6,7},{7,6},{8,9},{9,8},{10,11... | collective-permute-start | bytes 24584 | tf_op jit(solution)/shard_map/ppermute | solution.py:44
  27.7 2.1 %collective-permute-done.9 = f32[1,16,128]{2,1,0:T(8,128)S(1)} collective-permute-done((f32[1,16,128]{2,1,0:T(8,128)S(1)}, f32[1,16,128]{2,1,0:T(8,128)S(1)}, u32[]{:S(2)}, u32[]{:S(2)}) %collective-permute-start.9) | collective-permute-done | bytes 8224 | tf_op jit(solution)/shard_map/ppermute | solution.py:44
  29.8 1.6 %orthonormal.1 = (f32[1,16,128]{2,1,0:T(8,128)}, f32[1,2,16,16]{3,2,1,0:T(8,128)}) custom-call(f32[1,16,128]{2,1,0:T(8,128)S(1)} %add.27.gram_ref, f32[1,12,16,128]{3,2,1,0:T(8,128)S(1)} %add.23.x_ref), custom_call_target="tpu_custom_call" | custom-call | tf_op jit(solution)/shard_map/orthonormal/pallas_call | solution.py:273
  (18 shorter events, 0.1 us)
Async XLA Ops:
  0.6 3.2 %copy-start.4 = (s32[1,1,12]{2,1,0:T(1,128)S(1)}, s32[1,1,12]{2,1,0:T(1,128)}, u32[]{:S(2)}) copy-start(s32[1,1,12]{2,1,0:T(1,128)} %param.9) | copy-start | bytes 148
  0.6 3.2 %copy-start.3 = (s32[1,1,32]{2,1,0:T(1,128)S(1)}, s32[1,1,32]{2,1,0:T(1,128)}, u32[]{:S(2)}) copy-start(s32[1,1,32]{2,1,0:T(1,128)} %param.7) | copy-start | bytes 388
  0.6 5.5 %collective-permute-start.2 = (bf16[1,16,128]{2,1,0:T(8,128)(2,1)}, bf16[1,16,128]{2,1,0:T(8,128)(2,1)S(1)}, u32[]{:S(2)}, u32[]{:S(2)}) collective-permute-start(bf16[1,16,128]{2,1,0:T(8,128)(2,1)} %refs_0_.3), channel_id=1, source_target_pairs={{0,24},{8,16},{16,8},{24,0},{1,25},{9,17},{17,9},{25,1},{2,26},{10... | collective-permute-start | bytes 12296 | tf_op jit(solution)/shard_map/ppermute | solution.py:304
  3.1 3.8 %collective-permute-start.1 = (bf16[1,16,128]{2,1,0:T(8,128)(2,1)}, bf16[1,16,128]{2,1,0:T(8,128)(2,1)S(1)}, u32[]{:S(2)}, u32[]{:S(2)}) collective-permute-start(bf16[1,16,128]{2,1,0:T(8,128)(2,1)} %refs_0_.3), channel_id=1, source_target_pairs={{0,16},{8,24},{16,0},{24,8},{1,17},{9,25},{17,1},{25,9},{2,18},{10... | collective-permute-start | bytes 12296 | tf_op jit(solution)/shard_map/ppermute | solution.py:304
  3.8 3.2 %collective-permute-start = (bf16[1,16,128]{2,1,0:T(8,128)(2,1)}, bf16[1,16,128]{2,1,0:T(8,128)(2,1)S(1)}, u32[]{:S(2)}, u32[]{:S(2)}) collective-permute-start(bf16[1,16,128]{2,1,0:T(8,128)(2,1)} %refs_0_.3), channel_id=1, source_target_pairs={{0,8},{8,0},{16,24},{24,16},{1,9},{9,1},{17,25},{25,17},{2,10},{10... | collective-permute-start | bytes 12296 | tf_op jit(solution)/shard_map/ppermute | solution.py:304
  3.8 1.2 %copy-start = (bf16[1,1,32,128,128]{4,3,2,1,0:T(8,128)(2,1)S(1)}, bf16[1,1,32,128,128]{4,3,2,1,0:T(8,128)(2,1)}, u32[]{:S(2)}) copy-start(bf16[1,1,32,128,128]{4,3,2,1,0:T(8,128)(2,1)} %param.6) | copy-start | bytes 3145732
  3.8 1.3 %copy-start.1 = (bf16[1,1,12,128,128]{4,3,2,1,0:T(8,128)(2,1)S(1)}, bf16[1,1,12,128,128]{4,3,2,1,0:T(8,128)(2,1)}, u32[]{:S(2)}) copy-start(bf16[1,1,12,128,128]{4,3,2,1,0:T(8,128)(2,1)} %param.8) | copy-start | bytes 1179652
  3.8 3.1 %copy-start.2 = (bf16[1,16,128]{2,1,0:T(8,128)(2,1)S(1)}, bf16[1,16,128]{2,1,0:T(8,128)(2,1)}, u32[]{:S(2)}) copy-start(bf16[1,16,128]{2,1,0:T(8,128)(2,1)} %refs_0_.3) | copy-start | bytes 12292
  7.3 4.6 %collective-permute-start.3 = (f32[1,12,16,128]{3,2,1,0:T(8,128)S(1)}, f32[1,12,16,128]{3,2,1,0:T(8,128)S(1)}, u32[]{:S(2)}, u32[]{:S(2)}) collective-permute-start(f32[1,12,16,128]{3,2,1,0:T(8,128)S(1)} %tile_products.3), channel_id=1, source_target_pairs={{0,1},{1,0},{2,3},{3,2},{4,5},{5,4},{6,7},{7,6},{8,9},{9,8},{10,11... | collective-permute-start | bytes 294920 | tf_op jit(solution)/shard_map/ppermute | solution.py:37
  11.9 4.7 %collective-permute-start.4 = (f32[1,12,16,128]{3,2,1,0:T(8,128)S(1)}, f32[1,12,16,128]{3,2,1,0:T(8,128)S(1)}, u32[]{:S(2)}, u32[]{:S(2)}) collective-permute-start(f32[1,12,16,128]{3,2,1,0:T(8,128)S(1)} %add.21), channel_id=1, source_target_pairs={{0,2},{1,3},{2,0},{3,1},{4,6},{5,7},{6,4},{7,5},{8,10},{9,11},{10,... | collective-permute-start | bytes 294920 | tf_op jit(solution)/shard_map/ppermute | solution.py:37
  16.6 5.6 %collective-permute-start.5 = (f32[1,12,16,128]{3,2,1,0:T(8,128)S(1)}, f32[1,12,16,128]{3,2,1,0:T(8,128)S(1)}, u32[]{:S(2)}, u32[]{:S(2)}) collective-permute-start(f32[1,12,16,128]{3,2,1,0:T(8,128)S(1)} %add.22), channel_id=1, source_target_pairs={{0,4},{1,5},{2,6},{3,7},{4,0},{5,1},{6,2},{7,3},{8,12},{9,13},{10,... | collective-permute-start | bytes 294920 | tf_op jit(solution)/shard_map/ppermute | solution.py:37
  22.4 3.1 %collective-permute-start.8 = (f32[1,16,128]{2,1,0:T(8,128)S(1)}, f32[1,16,128]{2,1,0:T(8,128)S(1)}, u32[]{:S(2)}, u32[]{:S(2)}) collective-permute-start(f32[1,16,128]{2,1,0:T(8,128)S(1)} %gram_parts.1), channel_id=1, source_target_pairs={{0,24},{1,25},{2,26},{3,27},{4,28},{5,29},{6,30},{7,31},{8,16},{9,... | collective-permute-start | bytes 24584 | tf_op jit(solution)/shard_map/ppermute | solution.py:44
  22.4 3.7 %collective-permute-start.7 = (f32[1,16,128]{2,1,0:T(8,128)S(1)}, f32[1,16,128]{2,1,0:T(8,128)S(1)}, u32[]{:S(2)}, u32[]{:S(2)}) collective-permute-start(f32[1,16,128]{2,1,0:T(8,128)S(1)} %gram_parts.1), channel_id=1, source_target_pairs={{0,16},{1,17},{2,18},{3,19},{4,20},{5,21},{6,22},{7,23},{8,24},{9,... | collective-permute-start | bytes 24584 | tf_op jit(solution)/shard_map/ppermute | solution.py:44
  23.6 2.5 %collective-permute-start.6 = (f32[1,16,128]{2,1,0:T(8,128)S(1)}, f32[1,16,128]{2,1,0:T(8,128)S(1)}, u32[]{:S(2)}, u32[]{:S(2)}) collective-permute-start(f32[1,16,128]{2,1,0:T(8,128)S(1)} %gram_parts.1), channel_id=1, source_target_pairs={{0,8},{1,9},{2,10},{3,11},{4,12},{5,13},{6,14},{7,15},{8,0},{9,1},... | collective-permute-start | bytes 24584 | tf_op jit(solution)/shard_map/ppermute | solution.py:44
  26.1 3.7 %collective-permute-start.9 = (f32[1,16,128]{2,1,0:T(8,128)S(1)}, f32[1,16,128]{2,1,0:T(8,128)S(1)}, u32[]{:S(2)}, u32[]{:S(2)}) collective-permute-start(f32[1,16,128]{2,1,0:T(8,128)S(1)} %add_add_fusion), channel_id=1, source_target_pairs={{0,1},{1,0},{2,3},{3,2},{4,5},{5,4},{6,7},{7,6},{8,9},{9,8},{10,11... | collective-permute-start | bytes 24584 | tf_op jit(solution)/shard_map/ppermute | solution.py:44

commit v8 on v7

--- a/solution.py
+++ b/solution.py
@@ -51,7 +51,7 @@
 
 def scatter_digit(size, piece, tile):
     for stride, factor in digits_of(size):
-        if factor == 2 and piece * stride % tile == 0:
+        if factor == 2 and stride > 1 and piece * stride % tile == 0:
             return (stride, factor)
     return None
 
@@ -322,8 +322,8 @@
 
     gram = gram_parts(x)
     if direct and n_row == 4 and digit is not None:
+        gram = gram + across(gram, 0, digit[0])
         gram = gram + across(gram, 1, 0) + across(gram, 2, 0) + across(gram, 3, 0)
-        gram = gram + across(gram, 0, digit[0])
     else:
         for other in digits_of(n_row):
             gram = summed(gram, "row", other)

time: 31.5 us -> 31.5 us (level)
  no operation moved by 1% of the time
where the time goes in v8:
time: 31.5 us; the launch traced here: 31.3 us
  waiting for transfers between devices  13.4 us (43%)
  starting transfers between devices  12.5 us (40%)
  Pallas kernels  3.49 us (11%)
  local copies, waits for them, and re-layouts  1.16 us (4%)
  between operations  0.71 us (2%)
    ppermute x3, waiting for transfers between devices, sent(): lax.ppermute(x, axis, [(i, moved(i, digit, shift)) for i in range(size)])  8.82 us
    ppermute x3, starting transfers between devices, sent(): lax.ppermute(x, axis, [(i, moved(i, digit, shift)) for i in range(size)])  5.82 us
    ppermute x4, waiting for transfers between devices, across(): return lax.ppermute(x, ('row', 'col'), moves)  3.79 us
    ppermute x4, starting transfers between devices, across(): return lax.ppermute(x, ('row', 'col'), moves)  3.53 us
    ppermute x3, starting transfers between devices, per_device(): lax.ppermute(vectors, 'row', [(i, i ^ mask) for i in range(n_row)])  3.15 us
    pallas_call x1, Pallas kernels, orthonormal(): pl.pallas_call(functools.partial(root_kernel, layout), out_shape=[jax.Sha...  1.55 us
    unnamed x10, local copies, waits for them, and re-layouts  1.16 us
    pallas_call x1, Pallas kernels, turned(): pl.pallas_call(functools.partial(turn_kernel, layout), out_shape=[jax.Sha...  0.98 us
  transfers between devices with their start and end apart: 10, of which 7 were waited for; matrix products, arithmetic and copies ran while one was open for 0% of the time, Pallas kernels for 5%

profile of v8, /device:TPU:0, one launch (start us, length us, event | category | flops | bytes accessed | tf_op | source)
XLA Modules:
  0.0 31.3 jit_solution(3894308318907886472)
XLA Ops:
  0.6 2.5 %collective-permute-start.2 = (bf16[1,16,128]{2,1,0:T(8,128)(2,1)}, bf16[1,16,128]{2,1,0:T(8,128)(2,1)S(1)}, u32[]{:S(2)}, u32[]{:S(2)}) collective-permute-start(bf16[1,16,128]{2,1,0:T(8,128)(2,1)} %refs_0_.3), channel_id=1, source_target_pairs={{0,24},{8,16},{16,8},{24,0},{1,25},{9,17},{17,9},{25,1},{2,26},{10... | collective-permute-start | bytes 12296 | tf_op jit(solution)/shard_map/ppermute | solution.py:304
  3.1 0.6 %collective-permute-start.1 = (bf16[1,16,128]{2,1,0:T(8,128)(2,1)}, bf16[1,16,128]{2,1,0:T(8,128)(2,1)S(1)}, u32[]{:S(2)}, u32[]{:S(2)}) collective-permute-start(bf16[1,16,128]{2,1,0:T(8,128)(2,1)} %refs_0_.3), channel_id=1, source_target_pairs={{0,16},{8,24},{16,0},{24,8},{1,17},{9,25},{17,1},{25,9},{2,18},{10... | collective-permute-start | bytes 12296 | tf_op jit(solution)/shard_map/ppermute | solution.py:304
  3.8 0.0 collective-permute-start
  3.8 0.1 spots.1.where_ref
  4.0 1.1 %copy-done = bf16[1,1,32,128,128]{4,3,2,1,0:T(8,128)(2,1)S(1)} copy-done((bf16[1,1,32,128,128]{4,3,2,1,0:T(8,128)(2,1)S(1)}, bf16[1,1,32,128,128]{4,3,2,1,0:T(8,128)(2,1)}, u32[]{:S(2)}) %copy-start) | copy-done | bytes 1048600
  5.0 0.1 copy-done.1
  5.1 1.0 %turned.1 = (bf16[1,4,9,128,128]{4,3,2,1,0:T(8,128)(2,1)S(1)}, bf16[1,4,17,128,128]{4,3,2,1,0:T(8,128)(2,1)S(1)}) custom-call(s32[1,44]{1,0:T(1,128)S(1)} %spots.1.where_ref, bf16[1,32,128,128]{3,2,1,0:T(8,128)(2,1)S(1)} %bitcast.4, bf16[1,12,128,128]{3,2,1,0:T(8,128)(2,1)S(1)} %bitcast.5), custom_call_target="tpu_custom_call" | custom-call | bytes 2883584 | tf_op jit(solution)/shard_map/turned/pallas_call | solution.py:139
  6.1 0.8 %collective-permute-done.1.refs_2_ = bf16[1,16,128]{2,1,0:T(8,128)(2,1)S(1)} collective-permute-done((bf16[1,16,128]{2,1,0:T(8,128)(2,1)}, bf16[1,16,128]{2,1,0:T(8,128)(2,1)S(1)}, u32[]{:S(2)}, u32[]{:S(2)}) %collective-permute-start.1) | collective-permute-done | bytes 4128 | tf_op jit(solution)/shard_map/ppermute | solution.py:304
  6.9 0.3 %tile_products.3 = f32[1,12,16,128]{3,2,1,0:T(8,128)S(1)} custom-call(bf16[1,16,128]{2,1,0:T(8,128)(2,1)S(1)} %copy-done.2, bf16[1,16,128]{2,1,0:T(8,128)(2,1)S(1)} %collective-permute-done.refs_1_, bf16[1,16,128]{2,1,0:T(8,128)(2,1)S(1)} %collective-permute-done.1.refs_2_, bf16[1,16,128]{2,1,0:T(8,128)(2,1)S(1)} %collective-permute-done.2.refs_3_, ...), custom_call_target="tpu_custom_call" | custom-call | flops 25165824 | bytes 1572864 | tf_op jit(solution)/shard_map/tile_products/pallas_call | solution.py:178
  7.3 1.6 %collective-permute-start.3 = (f32[1,12,16,128]{3,2,1,0:T(8,128)S(1)}, f32[1,12,16,128]{3,2,1,0:T(8,128)S(1)}, u32[]{:S(2)}, u32[]{:S(2)}) collective-permute-start(f32[1,12,16,128]{3,2,1,0:T(8,128)S(1)} %tile_products.3), channel_id=1, source_target_pairs={{0,2},{1,3},{2,0},{3,1},{4,6},{5,7},{6,4},{7,5},{8,10},{9,11},{10,... | collective-permute-start | bytes 294920 | tf_op jit(solution)/shard_map/ppermute | solution.py:37
  8.8 0.3 %tile_products.2 = f32[1,12,16,128]{3,2,1,0:T(8,128)S(1)} custom-call(bf16[1,16,128]{2,1,0:T(8,128)(2,1)S(1)} %copy-done.2, bf16[1,16,128]{2,1,0:T(8,128)(2,1)S(1)} %collective-permute-done.refs_1_, bf16[1,16,128]{2,1,0:T(8,128)(2,1)S(1)} %collective-permute-done.1.refs_2_, bf16[1,16,128]{2,1,0:T(8,128)(2,1)S(1)} %collective-permute-done.2.refs_3_, ...), custom_call_target="tpu_custom_call" | custom-call | flops 25165824 | bytes 1572864 | tf_op jit(solution)/shard_map/tile_products/pallas_call | solution.py:178
  9.2 2.7 %collective-permute-done.3 = f32[1,12,16,128]{3,2,1,0:T(8,128)S(1)} collective-permute-done((f32[1,12,16,128]{3,2,1,0:T(8,128)S(1)}, f32[1,12,16,128]{3,2,1,0:T(8,128)S(1)}, u32[]{:S(2)}, u32[]{:S(2)}) %collective-permute-start.3) | collective-permute-done | bytes 98336 | tf_op jit(solution)/shard_map/ppermute | solution.py:37
  11.9 1.6 %collective-permute-start.4 = (f32[1,12,16,128]{3,2,1,0:T(8,128)S(1)}, f32[1,12,16,128]{3,2,1,0:T(8,128)S(1)}, u32[]{:S(2)}, u32[]{:S(2)}) collective-permute-start(f32[1,12,16,128]{3,2,1,0:T(8,128)S(1)} %add.21), channel_id=1, source_target_pairs={{0,1},{1,0},{2,3},{3,2},{4,5},{5,4},{6,7},{7,6},{8,9},{9,8},{10,11... | collective-permute-start | bytes 294920 | tf_op jit(solution)/shard_map/ppermute | solution.py:37
  13.5 3.1 %collective-permute-done.4 = f32[1,12,16,128]{3,2,1,0:T(8,128)S(1)} collective-permute-done((f32[1,12,16,128]{3,2,1,0:T(8,128)S(1)}, f32[1,12,16,128]{3,2,1,0:T(8,128)S(1)}, u32[]{:S(2)}, u32[]{:S(2)}) %collective-permute-start.4) | collective-permute-done | bytes 98336 | tf_op jit(solution)/shard_map/ppermute | solution.py:37
  16.6 2.7 %collective-permute-start.5 = (f32[1,12,16,128]{3,2,1,0:T(8,128)S(1)}, f32[1,12,16,128]{3,2,1,0:T(8,128)S(1)}, u32[]{:S(2)}, u32[]{:S(2)}) collective-permute-start(f32[1,12,16,128]{3,2,1,0:T(8,128)S(1)} %add.22), channel_id=1, source_target_pairs={{0,4},{1,5},{2,6},{3,7},{4,0},{5,1},{6,2},{7,3},{8,12},{9,13},{10,... | collective-permute-start | bytes 294920 | tf_op jit(solution)/shard_map/ppermute | solution.py:37
  19.3 3.0 %collective-permute-done.5 = f32[1,12,16,128]{3,2,1,0:T(8,128)S(1)} collective-permute-done((f32[1,12,16,128]{3,2,1,0:T(8,128)S(1)}, f32[1,12,16,128]{3,2,1,0:T(8,128)S(1)}, u32[]{:S(2)}, u32[]{:S(2)}) %collective-permute-start.5) | collective-permute-done | bytes 98336 | tf_op jit(solution)/shard_map/ppermute | solution.py:37
  22.3 0.2 gram_parts.1
  22.5 1.7 %collective-permute-start.6 = (f32[1,16,128]{2,1,0:T(8,128)S(1)}, f32[1,16,128]{2,1,0:T(8,128)S(1)}, u32[]{:S(2)}, u32[]{:S(2)}) collective-permute-start(f32[1,16,128]{2,1,0:T(8,128)S(1)} %gram_parts.1), channel_id=1, source_target_pairs={{0,2},{1,3},{2,0},{3,1},{4,6},{5,7},{6,4},{7,5},{8,10},{9,11},{10,... | collective-permute-start | bytes 24584 | tf_op jit(solution)/shard_map/ppermute | solution.py:44
  24.1 2.0 %collective-permute-done.6 = f32[1,16,128]{2,1,0:T(8,128)S(1)} collective-permute-done((f32[1,16,128]{2,1,0:T(8,128)S(1)}, f32[1,16,128]{2,1,0:T(8,128)S(1)}, u32[]{:S(2)}, u32[]{:S(2)}) %collective-permute-start.6) | collective-permute-done | bytes 8224 | tf_op jit(solution)/shard_map/ppermute | solution.py:44
  26.1 1.1 %collective-permute-start.8 = (f32[1,16,128]{2,1,0:T(8,128)S(1)}, f32[1,16,128]{2,1,0:T(8,128)S(1)}, u32[]{:S(2)}, u32[]{:S(2)}) collective-permute-start(f32[1,16,128]{2,1,0:T(8,128)S(1)} %add.24), channel_id=1, source_target_pairs={{0,16},{1,17},{2,18},{3,19},{4,20},{5,21},{6,22},{7,23},{8,24},{9,... | collective-permute-start | bytes 24584 | tf_op jit(solution)/shard_map/ppermute | solution.py:44
  27.2 0.8 %collective-permute-start.7 = (f32[1,16,128]{2,1,0:T(8,128)S(1)}, f32[1,16,128]{2,1,0:T(8,128)S(1)}, u32[]{:S(2)}, u32[]{:S(2)}) collective-permute-start(f32[1,16,128]{2,1,0:T(8,128)S(1)} %add.24), channel_id=1, source_target_pairs={{0,8},{1,9},{2,10},{3,11},{4,12},{5,13},{6,14},{7,15},{8,0},{9,1},... | collective-permute-start | bytes 24584 | tf_op jit(solution)/shard_map/ppermute | solution.py:44
  28.0 1.2 %collective-permute-done.9 = f32[1,16,128]{2,1,0:T(8,128)S(1)} collective-permute-done((f32[1,16,128]{2,1,0:T(8,128)S(1)}, f32[1,16,128]{2,1,0:T(8,128)S(1)}, u32[]{:S(2)}, u32[]{:S(2)}) %collective-permute-start.9) | collective-permute-done | bytes 8224 | tf_op jit(solution)/shard_map/ppermute | solution.py:44
  29.2 0.6 %collective-permute-done.8 = f32[1,16,128]{2,1,0:T(8,128)S(1)} collective-permute-done((f32[1,16,128]{2,1,0:T(8,128)S(1)}, f32[1,16,128]{2,1,0:T(8,128)S(1)}, u32[]{:S(2)}, u32[]{:S(2)}) %collective-permute-start.8) | collective-permute-done | bytes 8224 | tf_op jit(solution)/shard_map/ppermute | solution.py:44
  29.8 1.6 %orthonormal.1 = (f32[1,16,128]{2,1,0:T(8,128)}, f32[1,2,16,16]{3,2,1,0:T(8,128)}) custom-call(f32[1,16,128]{2,1,0:T(8,128)S(1)} %add_add_fusion.gram_ref, f32[1,12,16,128]{3,2,1,0:T(8,128)S(1)} %add.23.x_ref), custom_call_target="tpu_custom_call" | custom-call | tf_op jit(solution)/shard_map/orthonormal/pallas_call | solution.py:273
  (18 shorter events, 0.1 us)
Async XLA Ops:
  0.6 3.2 %copy-start.4 = (s32[1,1,12]{2,1,0:T(1,128)S(1)}, s32[1,1,12]{2,1,0:T(1,128)}, u32[]{:S(2)}) copy-start(s32[1,1,12]{2,1,0:T(1,128)} %param.9) | copy-start | bytes 148
  0.6 3.2 %copy-start.3 = (s32[1,1,32]{2,1,0:T(1,128)S(1)}, s32[1,1,32]{2,1,0:T(1,128)}, u32[]{:S(2)}) copy-start(s32[1,1,32]{2,1,0:T(1,128)} %param.7) | copy-start | bytes 388
  0.6 5.5 %collective-permute-start.2 = (bf16[1,16,128]{2,1,0:T(8,128)(2,1)}, bf16[1,16,128]{2,1,0:T(8,128)(2,1)S(1)}, u32[]{:S(2)}, u32[]{:S(2)}) collective-permute-start(bf16[1,16,128]{2,1,0:T(8,128)(2,1)} %refs_0_.3), channel_id=1, source_target_pairs={{0,24},{8,16},{16,8},{24,0},{1,25},{9,17},{17,9},{25,1},{2,26},{10... | collective-permute-start | bytes 12296 | tf_op jit(solution)/shard_map/ppermute | solution.py:304
  3.1 3.8 %collective-permute-start.1 = (bf16[1,16,128]{2,1,0:T(8,128)(2,1)}, bf16[1,16,128]{2,1,0:T(8,128)(2,1)S(1)}, u32[]{:S(2)}, u32[]{:S(2)}) collective-permute-start(bf16[1,16,128]{2,1,0:T(8,128)(2,1)} %refs_0_.3), channel_id=1, source_target_pairs={{0,16},{8,24},{16,0},{24,8},{1,17},{9,25},{17,1},{25,9},{2,18},{10... | collective-permute-start | bytes 12296 | tf_op jit(solution)/shard_map/ppermute | solution.py:304
  3.8 3.2 %collective-permute-start = (bf16[1,16,128]{2,1,0:T(8,128)(2,1)}, bf16[1,16,128]{2,1,0:T(8,128)(2,1)S(1)}, u32[]{:S(2)}, u32[]{:S(2)}) collective-permute-start(bf16[1,16,128]{2,1,0:T(8,128)(2,1)} %refs_0_.3), channel_id=1, source_target_pairs={{0,8},{8,0},{16,24},{24,16},{1,9},{9,1},{17,25},{25,17},{2,10},{10... | collective-permute-start | bytes 12296 | tf_op jit(solution)/shard_map/ppermute | solution.py:304
  3.8 1.2 %copy-start = (bf16[1,1,32,128,128]{4,3,2,1,0:T(8,128)(2,1)S(1)}, bf16[1,1,32,128,128]{4,3,2,1,0:T(8,128)(2,1)}, u32[]{:S(2)}) copy-start(bf16[1,1,32,128,128]{4,3,2,1,0:T(8,128)(2,1)} %param.6) | copy-start | bytes 3145732
  3.8 1.3 %copy-start.1 = (bf16[1,1,12,128,128]{4,3,2,1,0:T(8,128)(2,1)S(1)}, bf16[1,1,12,128,128]{4,3,2,1,0:T(8,128)(2,1)}, u32[]{:S(2)}) copy-start(bf16[1,1,12,128,128]{4,3,2,1,0:T(8,128)(2,1)} %param.8) | copy-start | bytes 1179652
  3.8 3.1 %copy-start.2 = (bf16[1,16,128]{2,1,0:T(8,128)(2,1)S(1)}, bf16[1,16,128]{2,1,0:T(8,128)(2,1)}, u32[]{:S(2)}) copy-start(bf16[1,16,128]{2,1,0:T(8,128)(2,1)} %refs_0_.3) | copy-start | bytes 12292
  7.3 4.6 %collective-permute-start.3 = (f32[1,12,16,128]{3,2,1,0:T(8,128)S(1)}, f32[1,12,16,128]{3,2,1,0:T(8,128)S(1)}, u32[]{:S(2)}, u32[]{:S(2)}) collective-permute-start(f32[1,12,16,128]{3,2,1,0:T(8,128)S(1)} %tile_products.3), channel_id=1, source_target_pairs={{0,2},{1,3},{2,0},{3,1},{4,6},{5,7},{6,4},{7,5},{8,10},{9,11},{10,... | collective-permute-start | bytes 294920 | tf_op jit(solution)/shard_map/ppermute | solution.py:37
  11.9 4.7 %collective-permute-start.4 = (f32[1,12,16,128]{3,2,1,0:T(8,128)S(1)}, f32[1,12,16,128]{3,2,1,0:T(8,128)S(1)}, u32[]{:S(2)}, u32[]{:S(2)}) collective-permute-start(f32[1,12,16,128]{3,2,1,0:T(8,128)S(1)} %add.21), channel_id=1, source_target_pairs={{0,1},{1,0},{2,3},{3,2},{4,5},{5,4},{6,7},{7,6},{8,9},{9,8},{10,11... | collective-permute-start | bytes 294920 | tf_op jit(solution)/shard_map/ppermute | solution.py:37
  16.6 5.7 %collective-permute-start.5 = (f32[1,12,16,128]{3,2,1,0:T(8,128)S(1)}, f32[1,12,16,128]{3,2,1,0:T(8,128)S(1)}, u32[]{:S(2)}, u32[]{:S(2)}) collective-permute-start(f32[1,12,16,128]{3,2,1,0:T(8,128)S(1)} %add.22), channel_id=1, source_target_pairs={{0,4},{1,5},{2,6},{3,7},{4,0},{5,1},{6,2},{7,3},{8,12},{9,13},{10,... | collective-permute-start | bytes 294920 | tf_op jit(solution)/shard_map/ppermute | solution.py:37
  22.5 3.7 %collective-permute-start.6 = (f32[1,16,128]{2,1,0:T(8,128)S(1)}, f32[1,16,128]{2,1,0:T(8,128)S(1)}, u32[]{:S(2)}, u32[]{:S(2)}) collective-permute-start(f32[1,16,128]{2,1,0:T(8,128)S(1)} %gram_parts.1), channel_id=1, source_target_pairs={{0,2},{1,3},{2,0},{3,1},{4,6},{5,7},{6,4},{7,5},{8,10},{9,11},{10,... | collective-permute-start | bytes 24584 | tf_op jit(solution)/shard_map/ppermute | solution.py:44
  26.1 3.1 %collective-permute-start.9 = (f32[1,16,128]{2,1,0:T(8,128)S(1)}, f32[1,16,128]{2,1,0:T(8,128)S(1)}, u32[]{:S(2)}, u32[]{:S(2)}) collective-permute-start(f32[1,16,128]{2,1,0:T(8,128)S(1)} %add.24), channel_id=1, source_target_pairs={{0,24},{1,25},{2,26},{3,27},{4,28},{5,29},{6,30},{7,31},{8,16},{9,... | collective-permute-start | bytes 24584 | tf_op jit(solution)/shard_map/ppermute | solution.py:44
  26.1 3.7 %collective-permute-start.8 = (f32[1,16,128]{2,1,0:T(8,128)S(1)}, f32[1,16,128]{2,1,0:T(8,128)S(1)}, u32[]{:S(2)}, u32[]{:S(2)}) collective-permute-start(f32[1,16,128]{2,1,0:T(8,128)S(1)} %add.24), channel_id=1, source_target_pairs={{0,16},{1,17},{2,18},{3,19},{4,20},{5,21},{6,22},{7,23},{8,24},{9,... | collective-permute-start | bytes 24584 | tf_op jit(solution)/shard_map/ppermute | solution.py:44
  27.2 2.6 %collective-permute-start.7 = (f32[1,16,128]{2,1,0:T(8,128)S(1)}, f32[1,16,128]{2,1,0:T(8,128)S(1)}, u32[]{:S(2)}, u32[]{:S(2)}) collective-permute-start(f32[1,16,128]{2,1,0:T(8,128)S(1)} %add.24), channel_id=1, source_target_pairs={{0,8},{1,9},{2,10},{3,11},{4,12},{5,13},{6,14},{7,15},{8,0},{9,1},... | collective-permute-start | bytes 24584 | tf_op jit(solution)/shard_map/ppermute | solution.py:44

commit v9 on v7

--- a/solution.py
+++ b/solution.py
@@ -160,8 +160,8 @@
         )
         for block_ref, first, count in ((j_block_ref, 1, J_OPERATORS), (h_block_ref, 0, 1)):
             start, stop = half * kept_tiles * count, (half + 1) * kept_tiles * count
-            for strip in range(start, stop, 2):
-                strips = range(strip, min(strip + 2, stop))
+            for strip in range(start, stop, 4):
+                strips = range(strip, min(strip + 4, stop))
                 block = [jnp.concatenate([block_ref[s, c, n] for n in strips], 1) for c in range(column_tiles)]
                 product = jnp.dot(lined, jnp.concatenate(block, 0), preferred_element_type=jnp.float32)
                 for i, n in enumerate(strips):

time: 31.5 us -> 31.5 us (level)
  no operation moved by 1% of the time
where the time goes in v9:
time: 31.5 us; the launch traced here: 31.4 us
  waiting for transfers between devices  13.5 us (43%)
  starting transfers between devices  12.5 us (40%)
  Pallas kernels  3.49 us (11%)
  local copies, waits for them, and re-layouts  1.16 us (4%)
  between operations  0.71 us (2%)
    ppermute x3, waiting for transfers between devices, sent(): lax.ppermute(x, axis, [(i, moved(i, digit, shift)) for i in range(size)])  8.7 us
    ppermute x3, starting transfers between devices, sent(): lax.ppermute(x, axis, [(i, moved(i, digit, shift)) for i in range(size)])  5.88 us
    ppermute x4, waiting for transfers between devices, across(): return lax.ppermute(x, ('row', 'col'), moves)  3.95 us
    ppermute x4, starting transfers between devices, across(): return lax.ppermute(x, ('row', 'col'), moves)  3.46 us
    ppermute x3, starting transfers between devices, per_device(): lax.ppermute(vectors, 'row', [(i, i ^ mask) for i in range(n_row)])  3.15 us
    pallas_call x1, Pallas kernels, orthonormal(): pl.pallas_call(functools.partial(root_kernel, layout), out_shape=[jax.Sha...  1.55 us
    unnamed x10, local copies, waits for them, and re-layouts  1.16 us
    pallas_call x1, Pallas kernels, turned(): pl.pallas_call(functools.partial(turn_kernel, layout), out_shape=[jax.Sha...  0.98 us
  transfers between devices with their start and end apart: 10, of which 7 were waited for; matrix products, arithmetic and copies ran while one was open for 0% of the time, Pallas kernels for 5%

profile of v9, /device:TPU:0, one launch (start us, length us, event | category | flops | bytes accessed | tf_op | source)
XLA Modules:
  0.0 31.4 jit_solution(6406986925325843412)
XLA Ops:
  0.6 2.5 %collective-permute-start.2 = (bf16[1,16,128]{2,1,0:T(8,128)(2,1)}, bf16[1,16,128]{2,1,0:T(8,128)(2,1)S(1)}, u32[]{:S(2)}, u32[]{:S(2)}) collective-permute-start(bf16[1,16,128]{2,1,0:T(8,128)(2,1)} %refs_0_.3), channel_id=1, source_target_pairs={{0,24},{8,16},{16,8},{24,0},{1,25},{9,17},{17,9},{25,1},{2,26},{10... | collective-permute-start | bytes 12296 | tf_op jit(solution)/shard_map/ppermute | solution.py:304
  3.1 0.6 %collective-permute-start.1 = (bf16[1,16,128]{2,1,0:T(8,128)(2,1)}, bf16[1,16,128]{2,1,0:T(8,128)(2,1)S(1)}, u32[]{:S(2)}, u32[]{:S(2)}) collective-permute-start(bf16[1,16,128]{2,1,0:T(8,128)(2,1)} %refs_0_.3), channel_id=1, source_target_pairs={{0,16},{8,24},{16,0},{24,8},{1,17},{9,25},{17,1},{25,9},{2,18},{10... | collective-permute-start | bytes 12296 | tf_op jit(solution)/shard_map/ppermute | solution.py:304
  3.8 0.0 collective-permute-start
  3.8 0.1 spots.1.where_ref
  4.0 1.1 %copy-done = bf16[1,1,32,128,128]{4,3,2,1,0:T(8,128)(2,1)S(1)} copy-done((bf16[1,1,32,128,128]{4,3,2,1,0:T(8,128)(2,1)S(1)}, bf16[1,1,32,128,128]{4,3,2,1,0:T(8,128)(2,1)}, u32[]{:S(2)}) %copy-start) | copy-done | bytes 1048600
  5.0 0.1 copy-done.1
  5.1 1.0 %turned.1 = (bf16[1,4,9,128,128]{4,3,2,1,0:T(8,128)(2,1)S(1)}, bf16[1,4,17,128,128]{4,3,2,1,0:T(8,128)(2,1)S(1)}) custom-call(s32[1,44]{1,0:T(1,128)S(1)} %spots.1.where_ref, bf16[1,32,128,128]{3,2,1,0:T(8,128)(2,1)S(1)} %bitcast.4, bf16[1,12,128,128]{3,2,1,0:T(8,128)(2,1)S(1)} %bitcast.5), custom_call_target="tpu_custom_call" | custom-call | bytes 2883584 | tf_op jit(solution)/shard_map/turned/pallas_call | solution.py:139
  6.1 0.8 %collective-permute-done.1.refs_2_ = bf16[1,16,128]{2,1,0:T(8,128)(2,1)S(1)} collective-permute-done((bf16[1,16,128]{2,1,0:T(8,128)(2,1)}, bf16[1,16,128]{2,1,0:T(8,128)(2,1)S(1)}, u32[]{:S(2)}, u32[]{:S(2)}) %collective-permute-start.1) | collective-permute-done | bytes 4128 | tf_op jit(solution)/shard_map/ppermute | solution.py:304
  6.9 0.3 %tile_products.3 = f32[1,12,16,128]{3,2,1,0:T(8,128)S(1)} custom-call(bf16[1,16,128]{2,1,0:T(8,128)(2,1)S(1)} %copy-done.2, bf16[1,16,128]{2,1,0:T(8,128)(2,1)S(1)} %collective-permute-done.refs_1_, bf16[1,16,128]{2,1,0:T(8,128)(2,1)S(1)} %collective-permute-done.1.refs_2_, bf16[1,16,128]{2,1,0:T(8,128)(2,1)S(1)} %collective-permute-done.2.refs_3_, ...), custom_call_target="tpu_custom_call" | custom-call | flops 25165824 | bytes 1572864 | tf_op jit(solution)/shard_map/tile_products/pallas_call | solution.py:178
  7.3 1.5 %collective-permute-start.3 = (f32[1,12,16,128]{3,2,1,0:T(8,128)S(1)}, f32[1,12,16,128]{3,2,1,0:T(8,128)S(1)}, u32[]{:S(2)}, u32[]{:S(2)}) collective-permute-start(f32[1,12,16,128]{3,2,1,0:T(8,128)S(1)} %tile_products.3), channel_id=1, source_target_pairs={{0,1},{1,0},{2,3},{3,2},{4,5},{5,4},{6,7},{7,6},{8,9},{9,8},{10,11... | collective-permute-start | bytes 294920 | tf_op jit(solution)/shard_map/ppermute | solution.py:37
  8.8 0.3 %tile_products.2 = f32[1,12,16,128]{3,2,1,0:T(8,128)S(1)} custom-call(bf16[1,16,128]{2,1,0:T(8,128)(2,1)S(1)} %copy-done.2, bf16[1,16,128]{2,1,0:T(8,128)(2,1)S(1)} %collective-permute-done.refs_1_, bf16[1,16,128]{2,1,0:T(8,128)(2,1)S(1)} %collective-permute-done.1.refs_2_, bf16[1,16,128]{2,1,0:T(8,128)(2,1)S(1)} %collective-permute-done.2.refs_3_, ...), custom_call_target="tpu_custom_call" | custom-call | flops 25165824 | bytes 1572864 | tf_op jit(solution)/shard_map/tile_products/pallas_call | solution.py:178
  9.1 2.8 %collective-permute-done.3 = f32[1,12,16,128]{3,2,1,0:T(8,128)S(1)} collective-permute-done((f32[1,12,16,128]{3,2,1,0:T(8,128)S(1)}, f32[1,12,16,128]{3,2,1,0:T(8,128)S(1)}, u32[]{:S(2)}, u32[]{:S(2)}) %collective-permute-start.3) | collective-permute-done | bytes 98336 | tf_op jit(solution)/shard_map/ppermute | solution.py:37
  11.9 1.6 %collective-permute-start.4 = (f32[1,12,16,128]{3,2,1,0:T(8,128)S(1)}, f32[1,12,16,128]{3,2,1,0:T(8,128)S(1)}, u32[]{:S(2)}, u32[]{:S(2)}) collective-permute-start(f32[1,12,16,128]{3,2,1,0:T(8,128)S(1)} %add.21), channel_id=1, source_target_pairs={{0,2},{1,3},{2,0},{3,1},{4,6},{5,7},{6,4},{7,5},{8,10},{9,11},{10,... | collective-permute-start | bytes 294920 | tf_op jit(solution)/shard_map/ppermute | solution.py:37
  13.5 3.0 %collective-permute-done.4 = f32[1,12,16,128]{3,2,1,0:T(8,128)S(1)} collective-permute-done((f32[1,12,16,128]{3,2,1,0:T(8,128)S(1)}, f32[1,12,16,128]{3,2,1,0:T(8,128)S(1)}, u32[]{:S(2)}, u32[]{:S(2)}) %collective-permute-start.4) | collective-permute-done | bytes 98336 | tf_op jit(solution)/shard_map/ppermute | solution.py:37
  16.6 2.7 %collective-permute-start.5 = (f32[1,12,16,128]{3,2,1,0:T(8,128)S(1)}, f32[1,12,16,128]{3,2,1,0:T(8,128)S(1)}, u32[]{:S(2)}, u32[]{:S(2)}) collective-permute-start(f32[1,12,16,128]{3,2,1,0:T(8,128)S(1)} %add.22), channel_id=1, source_target_pairs={{0,4},{1,5},{2,6},{3,7},{4,0},{5,1},{6,2},{7,3},{8,12},{9,13},{10,... | collective-permute-start | bytes 294920 | tf_op jit(solution)/shard_map/ppermute | solution.py:37
  19.3 2.9 %collective-permute-done.5 = f32[1,12,16,128]{3,2,1,0:T(8,128)S(1)} collective-permute-done((f32[1,12,16,128]{3,2,1,0:T(8,128)S(1)}, f32[1,12,16,128]{3,2,1,0:T(8,128)S(1)}, u32[]{:S(2)}, u32[]{:S(2)}) %collective-permute-start.5) | collective-permute-done | bytes 98336 | tf_op jit(solution)/shard_map/ppermute | solution.py:37
  22.2 0.2 gram_parts.1
  22.4 1.2 %collective-permute-start.7 = (f32[1,16,128]{2,1,0:T(8,128)S(1)}, f32[1,16,128]{2,1,0:T(8,128)S(1)}, u32[]{:S(2)}, u32[]{:S(2)}) collective-permute-start(f32[1,16,128]{2,1,0:T(8,128)S(1)} %gram_parts.1), channel_id=1, source_target_pairs={{0,16},{1,17},{2,18},{3,19},{4,20},{5,21},{6,22},{7,23},{8,24},{9,... | collective-permute-start | bytes 24584 | tf_op jit(solution)/shard_map/ppermute | solution.py:44
  23.6 0.7 %collective-permute-start.6 = (f32[1,16,128]{2,1,0:T(8,128)S(1)}, f32[1,16,128]{2,1,0:T(8,128)S(1)}, u32[]{:S(2)}, u32[]{:S(2)}) collective-permute-start(f32[1,16,128]{2,1,0:T(8,128)S(1)} %gram_parts.1), channel_id=1, source_target_pairs={{0,8},{1,9},{2,10},{3,11},{4,12},{5,13},{6,14},{7,15},{8,0},{9,1},... | collective-permute-start | bytes 24584 | tf_op jit(solution)/shard_map/ppermute | solution.py:44
  24.3 1.2 %collective-permute-done.8 = f32[1,16,128]{2,1,0:T(8,128)S(1)} collective-permute-done((f32[1,16,128]{2,1,0:T(8,128)S(1)}, f32[1,16,128]{2,1,0:T(8,128)S(1)}, u32[]{:S(2)}, u32[]{:S(2)}) %collective-permute-start.8) | collective-permute-done | bytes 8224 | tf_op jit(solution)/shard_map/ppermute | solution.py:44
  25.5 0.6 %collective-permute-done.7 = f32[1,16,128]{2,1,0:T(8,128)S(1)} collective-permute-done((f32[1,16,128]{2,1,0:T(8,128)S(1)}, f32[1,16,128]{2,1,0:T(8,128)S(1)}, u32[]{:S(2)}, u32[]{:S(2)}) %collective-permute-start.7) | collective-permute-done | bytes 8224 | tf_op jit(solution)/shard_map/ppermute | solution.py:44
  26.1 1.6 %collective-permute-start.9 = (f32[1,16,128]{2,1,0:T(8,128)S(1)}, f32[1,16,128]{2,1,0:T(8,128)S(1)}, u32[]{:S(2)}, u32[]{:S(2)}) collective-permute-start(f32[1,16,128]{2,1,0:T(8,128)S(1)} %add_add_fusion), channel_id=1, source_target_pairs={{0,1},{1,0},{2,3},{3,2},{4,5},{5,4},{6,7},{7,6},{8,9},{9,8},{10,11... | collective-permute-start | bytes 24584 | tf_op jit(solution)/shard_map/ppermute | solution.py:44
  27.7 2.1 %collective-permute-done.9 = f32[1,16,128]{2,1,0:T(8,128)S(1)} collective-permute-done((f32[1,16,128]{2,1,0:T(8,128)S(1)}, f32[1,16,128]{2,1,0:T(8,128)S(1)}, u32[]{:S(2)}, u32[]{:S(2)}) %collective-permute-start.9) | collective-permute-done | bytes 8224 | tf_op jit(solution)/shard_map/ppermute | solution.py:44
  29.8 1.6 %orthonormal.1 = (f32[1,16,128]{2,1,0:T(8,128)}, f32[1,2,16,16]{3,2,1,0:T(8,128)}) custom-call(f32[1,16,128]{2,1,0:T(8,128)S(1)} %add.27.gram_ref, f32[1,12,16,128]{3,2,1,0:T(8,128)S(1)} %add.23.x_ref), custom_call_target="tpu_custom_call" | custom-call | tf_op jit(solution)/shard_map/orthonormal/pallas_call | solution.py:273
  (18 shorter events, 0.1 us)
Async XLA Ops:
  0.6 3.2 %copy-start.4 = (s32[1,1,12]{2,1,0:T(1,128)S(1)}, s32[1,1,12]{2,1,0:T(1,128)}, u32[]{:S(2)}) copy-start(s32[1,1,12]{2,1,0:T(1,128)} %param.9) | copy-start | bytes 148
  0.6 3.2 %copy-start.3 = (s32[1,1,32]{2,1,0:T(1,128)S(1)}, s32[1,1,32]{2,1,0:T(1,128)}, u32[]{:S(2)}) copy-start(s32[1,1,32]{2,1,0:T(1,128)} %param.7) | copy-start | bytes 388
  0.6 5.5 %collective-permute-start.2 = (bf16[1,16,128]{2,1,0:T(8,128)(2,1)}, bf16[1,16,128]{2,1,0:T(8,128)(2,1)S(1)}, u32[]{:S(2)}, u32[]{:S(2)}) collective-permute-start(bf16[1,16,128]{2,1,0:T(8,128)(2,1)} %refs_0_.3), channel_id=1, source_target_pairs={{0,24},{8,16},{16,8},{24,0},{1,25},{9,17},{17,9},{25,1},{2,26},{10... | collective-permute-start | bytes 12296 | tf_op jit(solution)/shard_map/ppermute | solution.py:304
  3.1 3.8 %collective-permute-start.1 = (bf16[1,16,128]{2,1,0:T(8,128)(2,1)}, bf16[1,16,128]{2,1,0:T(8,128)(2,1)S(1)}, u32[]{:S(2)}, u32[]{:S(2)}) collective-permute-start(bf16[1,16,128]{2,1,0:T(8,128)(2,1)} %refs_0_.3), channel_id=1, source_target_pairs={{0,16},{8,24},{16,0},{24,8},{1,17},{9,25},{17,1},{25,9},{2,18},{10... | collective-permute-start | bytes 12296 | tf_op jit(solution)/shard_map/ppermute | solution.py:304
  3.8 3.2 %collective-permute-start = (bf16[1,16,128]{2,1,0:T(8,128)(2,1)}, bf16[1,16,128]{2,1,0:T(8,128)(2,1)S(1)}, u32[]{:S(2)}, u32[]{:S(2)}) collective-permute-start(bf16[1,16,128]{2,1,0:T(8,128)(2,1)} %refs_0_.3), channel_id=1, source_target_pairs={{0,8},{8,0},{16,24},{24,16},{1,9},{9,1},{17,25},{25,17},{2,10},{10... | collective-permute-start | bytes 12296 | tf_op jit(solution)/shard_map/ppermute | solution.py:304
  3.8 1.2 %copy-start = (bf16[1,1,32,128,128]{4,3,2,1,0:T(8,128)(2,1)S(1)}, bf16[1,1,32,128,128]{4,3,2,1,0:T(8,128)(2,1)}, u32[]{:S(2)}) copy-start(bf16[1,1,32,128,128]{4,3,2,1,0:T(8,128)(2,1)} %param.6) | copy-start | bytes 3145732
  3.8 1.3 %copy-start.1 = (bf16[1,1,12,128,128]{4,3,2,1,0:T(8,128)(2,1)S(1)}, bf16[1,1,12,128,128]{4,3,2,1,0:T(8,128)(2,1)}, u32[]{:S(2)}) copy-start(bf16[1,1,12,128,128]{4,3,2,1,0:T(8,128)(2,1)} %param.8) | copy-start | bytes 1179652
  3.8 3.1 %copy-start.2 = (bf16[1,16,128]{2,1,0:T(8,128)(2,1)S(1)}, bf16[1,16,128]{2,1,0:T(8,128)(2,1)}, u32[]{:S(2)}) copy-start(bf16[1,16,128]{2,1,0:T(8,128)(2,1)} %refs_0_.3) | copy-start | bytes 12292
  7.3 4.6 %collective-permute-start.3 = (f32[1,12,16,128]{3,2,1,0:T(8,128)S(1)}, f32[1,12,16,128]{3,2,1,0:T(8,128)S(1)}, u32[]{:S(2)}, u32[]{:S(2)}) collective-permute-start(f32[1,12,16,128]{3,2,1,0:T(8,128)S(1)} %tile_products.3), channel_id=1, source_target_pairs={{0,1},{1,0},{2,3},{3,2},{4,5},{5,4},{6,7},{7,6},{8,9},{9,8},{10,11... | collective-permute-start | bytes 294920 | tf_op jit(solution)/shard_map/ppermute | solution.py:37
  11.9 4.7 %collective-permute-start.4 = (f32[1,12,16,128]{3,2,1,0:T(8,128)S(1)}, f32[1,12,16,128]{3,2,1,0:T(8,128)S(1)}, u32[]{:S(2)}, u32[]{:S(2)}) collective-permute-start(f32[1,12,16,128]{3,2,1,0:T(8,128)S(1)} %add.21), channel_id=1, source_target_pairs={{0,2},{1,3},{2,0},{3,1},{4,6},{5,7},{6,4},{7,5},{8,10},{9,11},{10,... | collective-permute-start | bytes 294920 | tf_op jit(solution)/shard_map/ppermute | solution.py:37
  16.6 5.6 %collective-permute-start.5 = (f32[1,12,16,128]{3,2,1,0:T(8,128)S(1)}, f32[1,12,16,128]{3,2,1,0:T(8,128)S(1)}, u32[]{:S(2)}, u32[]{:S(2)}) collective-permute-start(f32[1,12,16,128]{3,2,1,0:T(8,128)S(1)} %add.22), channel_id=1, source_target_pairs={{0,4},{1,5},{2,6},{3,7},{4,0},{5,1},{6,2},{7,3},{8,12},{9,13},{10,... | collective-permute-start | bytes 294920 | tf_op jit(solution)/shard_map/ppermute | solution.py:37
  22.4 3.1 %collective-permute-start.8 = (f32[1,16,128]{2,1,0:T(8,128)S(1)}, f32[1,16,128]{2,1,0:T(8,128)S(1)}, u32[]{:S(2)}, u32[]{:S(2)}) collective-permute-start(f32[1,16,128]{2,1,0:T(8,128)S(1)} %gram_parts.1), channel_id=1, source_target_pairs={{0,24},{1,25},{2,26},{3,27},{4,28},{5,29},{6,30},{7,31},{8,16},{9,... | collective-permute-start | bytes 24584 | tf_op jit(solution)/shard_map/ppermute | solution.py:44
  22.4 3.7 %collective-permute-start.7 = (f32[1,16,128]{2,1,0:T(8,128)S(1)}, f32[1,16,128]{2,1,0:T(8,128)S(1)}, u32[]{:S(2)}, u32[]{:S(2)}) collective-permute-start(f32[1,16,128]{2,1,0:T(8,128)S(1)} %gram_parts.1), channel_id=1, source_target_pairs={{0,16},{1,17},{2,18},{3,19},{4,20},{5,21},{6,22},{7,23},{8,24},{9,... | collective-permute-start | bytes 24584 | tf_op jit(solution)/shard_map/ppermute | solution.py:44
  23.6 2.5 %collective-permute-start.6 = (f32[1,16,128]{2,1,0:T(8,128)S(1)}, f32[1,16,128]{2,1,0:T(8,128)S(1)}, u32[]{:S(2)}, u32[]{:S(2)}) collective-permute-start(f32[1,16,128]{2,1,0:T(8,128)S(1)} %gram_parts.1), channel_id=1, source_target_pairs={{0,8},{1,9},{2,10},{3,11},{4,12},{5,13},{6,14},{7,15},{8,0},{9,1},... | collective-permute-start | bytes 24584 | tf_op jit(solution)/shard_map/ppermute | solution.py:44
  26.1 3.7 %collective-permute-start.9 = (f32[1,16,128]{2,1,0:T(8,128)S(1)}, f32[1,16,128]{2,1,0:T(8,128)S(1)}, u32[]{:S(2)}, u32[]{:S(2)}) collective-permute-start(f32[1,16,128]{2,1,0:T(8,128)S(1)} %add_add_fusion), channel_id=1, source_target_pairs={{0,1},{1,0},{2,3},{3,2},{4,5},{5,4},{6,7},{7,6},{8,9},{9,8},{10,11... | collective-permute-start | bytes 24584 | tf_op jit(solution)/shard_map/ppermute | solution.py:44
